TPU v7x, 32 devices: a whole 2x2x4 slice. The times are simulated.
32 devices in a mesh: stream: 2 (over core), frames: 16 (over z, y, x).
Axes of the slice: x: 2, y: 2, z: 4, core: 2. Of those that a mesh axis runs over, the one named last changes fastest.
Arguments:
- tokens: bfloat16 [2048, 2, 1024], P('frames', 'stream'), may hold values from -6 to 6
- context: bfloat16 [2048, 4096], P('frames'), may hold values from -6 to 6
- w_in: bfloat16 [1024, 4096], P('stream', 'frames'), may hold values from -0.09375 to 0.09375
- attn_gain: bfloat16 [2, 1024], P('stream', 'frames'), may hold values from 0.5 to 1.5
- w_qkv: bfloat16 [2, 1024, 3072], P('stream', 'frames'), may hold values from -0.1875 to 0.1875
- w_out: bfloat16 [2, 1024, 1024], P('stream', 'frames'), may hold values from -0.1875 to 0.1875
- ffn_gain: bfloat16 [2, 1024], P('stream', 'frames'), may hold values from 0.5 to 1.5
- w_gate_up: bfloat16 [2, 1024, 5632], P('stream', 'frames'), may hold values from -0.1875 to 0.1875
- w_down: bfloat16 [2, 2816, 1024], P('stream', 'frames'), may hold values from -0.21875 to 0.21875
- cotangent: bfloat16 [2048, 2, 1024], P('frames', 'stream'), may hold values from -6 to 6
Outputs:
- out: float32 [2048, 2, 1024], P('frames', 'stream')
- grad_tokens: float32 [2048, 2, 1024], P('frames', 'stream')
- grad_context: float32 [2048, 4096], P('frames')
- grad_w_in: float32 [1024, 4096], P('stream', 'frames')
- grad_attn_gain: float32 [2, 1024], P('stream', 'frames')
- grad_w_qkv: float32 [2, 1024, 3072], P('stream', 'frames')
- grad_w_out: float32 [2, 1024, 1024], P('stream', 'frames')
- grad_ffn_gain: float32 [2, 1024], P('stream', 'frames')
- grad_w_gate_up: float32 [2, 1024, 5632], P('stream', 'frames')
- grad_w_down: float32 [2, 2816, 1024], P('stream', 'frames')
All inputs are finite; a program needn't handle non-finite values.
Results may differ from a plain program's by a relative error of at most 0.014.
Values may be sent and summed in bfloat16 or wider, within the bound.
No kernel may reach another device: no remote copies, remote signals or barrier semaphores. Data moves between devices by JAX's collectives and lax.ppermute only.
A program may use at most 192 MiB of HBM per device.

v0:
```python
import jax
import jax.numpy as jnp
from jax import lax
from jax.sharding import PartitionSpec as P

D = 1024
H = 16
HD = 64


def from_behind(value, axis, steps):
    count = lax.axis_size(axis)
    initial, last = (max(0, -steps), min(count, count - steps))
    return lax.ppermute(value, axis, [(source, source + steps) for source in range(initial, last)])


def norm_parts(values):
    scale = lax.rsqrt(jnp.mean(values * values, axis=-1, keepdims=True) + 1e-05)
    return (values * scale, scale)


def norm_back(unit, scale, grad_unit):
    return scale * (grad_unit - unit * jnp.mean(grad_unit * unit, axis=-1, keepdims=True))


def attend(query, keys, stream_pos, per_stream):
    frame_count = query.shape[0]
    query_heads = query.reshape(frame_count, per_stream, H, HD)
    key_heads = keys[..., :D].reshape(frame_count, 2 * per_stream, H, HD)
    value_heads = keys[..., D:].reshape(frame_count, 2 * per_stream, H, HD)
    scores = jnp.sum(query_heads[:, :, None] * key_heads[:, None], axis=-1) * HD ** (-0.5)
    query_place = stream_pos * per_stream + jnp.arange(per_stream)
    key_place = jnp.concatenate(
        [
            (stream_pos - 1) * per_stream + jnp.arange(per_stream),
            stream_pos * per_stream + jnp.arange(per_stream),
        ]
    )
    allowed = (key_place[None, :] >= 0) & (key_place[None, :] <= query_place[:, None])
    scores = jnp.where(allowed[None, :, :, None], scores, -1e30)
    weights = jax.nn.softmax(scores, axis=2)
    mixed = jnp.sum(weights[..., None] * value_heads[:, None], axis=2)
    return mixed.reshape(frame_count, per_stream, D)


def on_device(
    tokens, context, w_in, attn_gain, w_qkv, w_out, ffn_gain, w_gate_up, w_down, cotangent
):
    stream_pos = lax.axis_index("stream")
    per_stream = tokens.shape[1]
    shards = (attn_gain, w_qkv, w_out, ffn_gain, w_gate_up, w_down, w_in)
    gain_one, qkv_weight, out_weight, gain_two, gate_up_weight, down_weight, in_weight = (
        lax.all_gather(shards[0], "frames", axis=1, tiled=True),
        lax.all_gather(shards[1], "frames", axis=1, tiled=True),
        lax.all_gather(shards[2], "frames", axis=1, tiled=True),
        lax.all_gather(shards[3], "frames", axis=1, tiled=True),
        lax.all_gather(shards[4], "frames", axis=1, tiled=True),
        lax.all_gather(shards[5], "frames", axis=1, tiled=True),
        lax.all_gather(shards[6], "frames", axis=1, tiled=True),
    )
    proj_half = jnp.einsum(
        "fc,dc->fd", context, in_weight, preferred_element_type=jnp.float32
    ).astype(jnp.bfloat16)
    projected = lax.all_gather(proj_half, "stream", axis=1, tiled=True)
    start = tokens.astype(jnp.float32) + projected.astype(jnp.float32)[:, None, :]
    unit_one, scale_one = norm_parts(start)
    normed_one = (unit_one * gain_one.astype(jnp.float32)).astype(jnp.bfloat16)
    qkv = jnp.einsum(
        "fpd,pde->fpe", normed_one, qkv_weight, preferred_element_type=jnp.float32
    ).astype(jnp.bfloat16)
    query = qkv[..., :D]
    own_kv = qkv[..., D:]
    far_kv = from_behind(own_kv, "stream", 1)
    keys = jnp.concatenate([far_kv, own_kv], axis=1)

    def attend_local(query_part, key_part):
        return attend(query_part, key_part, stream_pos, per_stream)

    mixed, attend_pull = jax.vjp(attend_local, query.astype(jnp.float32), keys.astype(jnp.float32))
    mixed_low = mixed.astype(jnp.bfloat16)
    middle = start + jnp.einsum(
        "fpd,pde->fpe", mixed_low, out_weight, preferred_element_type=jnp.float32
    )
    unit_two, scale_two = norm_parts(middle)
    normed_two = (unit_two * gain_two.astype(jnp.float32)).astype(jnp.bfloat16)
    gate_up = jnp.einsum(
        "fpd,pde->fpe", normed_two, gate_up_weight, preferred_element_type=jnp.float32
    )
    half_width = gate_up.shape[-1] // 2
    gate = gate_up[..., :half_width]
    upper = gate_up[..., half_width:]
    sigmoid = jax.nn.sigmoid(gate)
    hidden = (gate * sigmoid * upper).astype(jnp.bfloat16)
    result = middle + jnp.einsum(
        "fpk,pkd->fpd", hidden, down_weight, preferred_element_type=jnp.float32
    )
    gain_one, qkv_weight, out_weight, gain_two, gate_up_weight, down_weight, in_weight = (
        lax.all_gather(shards[0], "frames", axis=1, tiled=True),
        lax.all_gather(shards[1], "frames", axis=1, tiled=True),
        lax.all_gather(shards[2], "frames", axis=1, tiled=True),
        lax.all_gather(shards[3], "frames", axis=1, tiled=True),
        lax.all_gather(shards[4], "frames", axis=1, tiled=True),
        lax.all_gather(shards[5], "frames", axis=1, tiled=True),
        lax.all_gather(shards[6], "frames", axis=1, tiled=True),
    )
    grad_down = jnp.einsum("fpk,fpd->pkd", hidden, cotangent, preferred_element_type=jnp.float32)
    grad_hidden = jnp.einsum(
        "fpd,pkd->fpk", cotangent, down_weight, preferred_element_type=jnp.float32
    )
    grad_gate = grad_hidden * upper * sigmoid * (1.0 + gate * (1.0 - sigmoid))
    grad_upper = grad_hidden * gate * sigmoid
    grad_gu = jnp.concatenate([grad_gate, grad_upper], axis=-1).astype(jnp.bfloat16)
    grad_gate_up = jnp.einsum(
        "fpd,fpe->pde", normed_two, grad_gu, preferred_element_type=jnp.float32
    )
    grad_normed_two = jnp.einsum(
        "fpe,pde->fpd", grad_gu, gate_up_weight, preferred_element_type=jnp.float32
    )
    grad_gain_two = jnp.sum(grad_normed_two * unit_two, axis=0)
    grad_middle = cotangent.astype(jnp.float32) + norm_back(
        unit_two, scale_two, grad_normed_two * gain_two.astype(jnp.float32)
    )
    grad_branch = grad_middle.astype(jnp.bfloat16)
    grad_out = jnp.einsum(
        "fpd,fpe->pde", mixed_low, grad_branch, preferred_element_type=jnp.float32
    )
    grad_mixed = jnp.einsum(
        "fpe,pde->fpd", grad_branch, out_weight, preferred_element_type=jnp.float32
    )
    grad_query, grad_keys = attend_pull(grad_mixed)
    returned = from_behind(grad_keys[:, :per_stream].astype(jnp.bfloat16), "stream", -1).astype(
        jnp.float32
    )
    grad_kv = grad_keys[:, per_stream:] + returned
    grad_qkv_low = jnp.concatenate([grad_query, grad_kv], axis=-1).astype(jnp.bfloat16)
    grad_qkv = jnp.einsum(
        "fpd,fpe->pde", normed_one, grad_qkv_low, preferred_element_type=jnp.float32
    )
    grad_normed_one = jnp.einsum(
        "fpe,pde->fpd", grad_qkv_low, qkv_weight, preferred_element_type=jnp.float32
    )
    grad_gain_one = jnp.sum(grad_normed_one * unit_one, axis=0)
    grad_start = grad_middle + norm_back(
        unit_one, scale_one, grad_normed_one * gain_one.astype(jnp.float32)
    )
    grad_proj = lax.psum_scatter(
        jnp.sum(grad_start, axis=1).astype(jnp.bfloat16), "stream", scatter_dimension=1, tiled=True
    )
    grad_in = jnp.einsum("fd,fc->dc", grad_proj, context, preferred_element_type=jnp.float32)
    context_term = jnp.einsum("fd,dc->fc", grad_proj, in_weight, preferred_element_type=jnp.float32)
    grad_context = lax.psum(context_term.astype(jnp.bfloat16), "stream").astype(jnp.float32)
    summed = (
        lax.psum_scatter(grad_gain_one, "frames", scatter_dimension=1, tiled=True),
        lax.psum_scatter(grad_qkv, "frames", scatter_dimension=1, tiled=True),
        lax.psum_scatter(grad_out, "frames", scatter_dimension=1, tiled=True),
        lax.psum_scatter(grad_gain_two, "frames", scatter_dimension=1, tiled=True),
        lax.psum_scatter(grad_gate_up, "frames", scatter_dimension=1, tiled=True),
        lax.psum_scatter(grad_down, "frames", scatter_dimension=1, tiled=True),
        lax.psum_scatter(grad_in, "frames", scatter_dimension=1, tiled=True),
    )
    return (
        result,
        grad_start,
        grad_context,
        summed[6],
        summed[0],
        summed[1],
        summed[2],
        summed[3],
        summed[4],
        summed[5],
    )


def solution(mesh):
    return jax.shard_map(
        on_device,
        mesh=mesh,
        in_specs=(
            P("frames", "stream", None),
            P("frames", None),
            P("stream", "frames"),
            P("stream", "frames"),
            P("stream", "frames", None),
            P("stream", "frames", None),
            P("stream", "frames"),
            P("stream", "frames", None),
            P("stream", "frames", None),
            P("frames", "stream", None),
        ),
        out_specs=(
            P("frames", "stream", None),
            P("frames", "stream", None),
            P("frames", None),
            P("stream", "frames"),
            P("stream", "frames"),
            P("stream", "frames", None),
            P("stream", "frames", None),
            P("stream", "frames"),
            P("stream", "frames", None),
            P("stream", "frames", None),
        ),
        check_vma=False,
    )
```

profile of v0, /device:TPU:0, one launch (start us, length us, event | category | flops | bytes accessed | tf_op | source)
XLA Modules:
  0.0 1931.6 jit_solution(13674588787667469239)
XLA Ops:
  10.6 1.2 dynamic-slice
  14.2 44.4 %all-reduce.4 = (bf16[1024]{0:T(1024)(128)(2,1)S(1)}, bf16[1024]{0:T(1024)(128)(2,1)S(1)}) all-reduce(bf16[1024]{0:T(1024)(128)(2,1)S(1)} %dynamic-update-slice, bf16[1024]{0:T(1024)(128)(2,1)S(1)} %dynamic-update-slice.1), channel_id=1, replica_groups=mesh['stream'=2,'frames'=16] {'frames'}, use_global_device_ids=true, to_apply=%add.2 | all-reduce | flops 2048 | bytes 8192
  58.6 42.2 %all-gather.6.cloned.1.call-done = bf16[512,4096]{1,0:T(8,128)(2,1)} async-done(((bf16[512,256]{1,0:T(8,128)(2,1)}), bf16[512,4096]{1,0:T(8,128)(2,1)}) %all-gather.6.cloned.1.call-update) | async-done | bytes 4194320 | tf_op jit(solution)/shard_map/all_gather | solution.py:59
  100.9 3.7 convolution_convert_fusion.1
  104.6 2.0 all_gather.32
  106.8 89.3 %all-gather.8.cloned.1.call-done = bf16[1,1024,3072]{2,1,0:T(8,128)(2,1)} async-done(((bf16[1,64,3072]{2,1,0:T(8,128)(2,1)}), bf16[1,1024,3072]{2,1,0:T(8,128)(2,1)}) %all-gather.8.cloned.1.call-update) | async-done | bytes 6291472 | tf_op jit(solution)/shard_map/all_gather | solution.py:54
  196.1 3.9 fusion.21
  200.8 2.1 collective-permute-start
  203.1 1.0 copy.34
  204.1 1.0 copy.42
  205.1 1.4 maximum_convert_fusion
  206.4 1.2 slice.35
  207.6 2.5 copy.35
  210.1 1.5 multiply_reduce_fusion.3
  211.9 1.0 mul.265
  213.0 2.5 copy.36
  215.5 3.1 fusion.77
  218.7 2.6 copy.39
  221.3 36.6 %all-gather.10.cloned.1.call-done = bf16[1,1024,1024]{2,1,0:T(8,128)(2,1)} async-done(((bf16[1,64,1024]{2,1,0:T(8,128)(2,1)}), bf16[1,1024,1024]{2,1,0:T(8,128)(2,1)}) %all-gather.10.cloned.1.call-update) | async-done | bytes 2097168 | tf_op jit(solution)/shard_map/all_gather | solution.py:55
  257.9 2.1 multiply_reduce_fusion.8
  260.6 140.7 %all-gather.12.cloned.1.call-done = bf16[1,1024,5632]{2,1,0:T(8,128)(2,1)} async-done(((bf16[1,64,5632]{2,1,0:T(8,128)(2,1)}), bf16[1,1024,5632]{2,1,0:T(8,128)(2,1)}) %all-gather.12.cloned.1.call-update) | async-done | bytes 11534352 | tf_op jit(solution)/shard_map/all_gather | solution.py:57
  401.3 7.6 fusion.4
  408.9 82.6 %all-gather.14.cloned.1.call-done = bf16[1,2816,1024]{2,1,0:T(8,128)(2,1)} async-done(((bf16[1,176,1024]{2,1,0:T(8,128)(2,1)}), bf16[1,2816,1024]{2,1,0:T(8,128)(2,1)}) %all-gather.14.cloned.1.call-update) | async-done | bytes 5767184 | tf_op jit(solution)/shard_map/all_gather | solution.py:58
  491.6 6.7 fusion.53
  498.3 3.9 multiply_reduce_fusion.4
  502.2 1.2 multiply_add_fusion.1
  504.3 1.0 copy.41
  505.5 1.4 multiply_reduce_fusion.1
  507.2 1.2 bitcast_multiply_fusion
  508.4 1.0 copy-done.4
  510.2 1.3 collective-permute-start.1
  511.5 1.1 broadcast_in_dim.63
  512.5 2.5 copy.40
  515.1 2.5 multiply_reduce_fusion
  517.5 1.8 copy.43
  519.3 1.4 fusion.54
  520.8 5.3 multiply_reduce_fusion.5
  526.1 1.1 convert_bitcast_fusion
  527.5 1.0 copy.49
  528.6 1.0 copy.47
  529.7 5.3 reduce-scatter.13.cloned.1.call-done
  535.0 4.0 convolution_convert_fusion
  539.1 2.8 convolution_bitcast_fusion.3
  542.8 4.6 fusion.82
  547.4 1.0 copy-done.10
  548.5 6.0 convolution_bitcast_fusion.1
  554.6 0.9 copy-done.9
  555.7 6.5 convolution_bitcast_fusion.2
  562.2 1.0 copy-done.12
  563.5 9.5 convolution_bitcast_fusion
  573.0 3.6 fusion.40
  576.7 1.3 copy.44
  578.0 37.2 %reduce-scatter.27.cloned.1.call-done = f32[64,1]{1,0:T(8,128)} async-done(((f32[1024,1]{1,0:T(8,128)}), f32[64,1]{1,0:T(8,128)}) %reduce-scatter.27.cloned.1.call-update) | async-done | bytes 272
  615.2 1.3 copy.50
  616.5 1.3 copy.45
  617.8 72.5 %reduce-scatter.25.cloned.1.call-done = f32[64,1]{1,0:T(8,128)} async-done(((f32[1024,1]{1,0:T(8,128)}), f32[64,1]{1,0:T(8,128)}) %reduce-scatter.25.cloned.1.call-update) | async-done | bytes 272
  690.3 1.3 copy.48
  691.7 17.7 all-reduce.7.cloned.1.call-done
  709.4 2.8 convert_element_type.100
  712.1 96.3 %reduce-scatter.19.cloned.1.call-done = f32[1,64,1024]{2,1,0:T(8,128)} async-done(((f32[1,1024,1024]{2,1,0:T(8,128)}), f32[1,64,1024]{2,1,0:T(8,128)}) %reduce-scatter.19.cloned.1.call-update) | async-done | bytes 262160 | tf_op jit(solution)/shard_map/reduce_scatter | solution.py:155
  808.4 180.4 %reduce-scatter.15.cloned.1.call-done = f32[512,256]{1,0:T(8,128)} async-done(((f32[512,4096]{1,0:T(8,128)}), f32[512,256]{1,0:T(8,128)}) %reduce-scatter.15.cloned.1.call-update) | async-done | bytes 524304 | tf_op jit(solution)/shard_map/reduce_scatter | solution.py:159
  988.8 246.0 %reduce-scatter.23.cloned.1.call-done = f32[1,176,1024]{2,1,0:T(8,128)} async-done(((f32[1,2816,1024]{2,1,0:T(8,128)}), f32[1,176,1024]{2,1,0:T(8,128)}) %reduce-scatter.23.cloned.1.call-update) | async-done | bytes 720912 | tf_op jit(solution)/shard_map/reduce_scatter | solution.py:158
  1234.8 214.8 %reduce-scatter.17.cloned.1.call-done = f32[1,64,3072]{2,1,0:T(8,128)} async-done(((f32[1,1024,3072]{2,1,0:T(8,128)}), f32[1,64,3072]{2,1,0:T(8,128)}) %reduce-scatter.17.cloned.1.call-update) | async-done | bytes 786448 | tf_op jit(solution)/shard_map/reduce_scatter | solution.py:154
  1449.6 475.5 %reduce-scatter.21.cloned.1.call-done = f32[1,64,5632]{2,1,0:T(8,128)} async-done(((f32[1,1024,5632]{2,1,0:T(8,128)}), f32[1,64,5632]{2,1,0:T(8,128)}) %reduce-scatter.21.cloned.1.call-update) | async-done | bytes 1441808 | tf_op jit(solution)/shard_map/reduce_scatter | solution.py:157
  (130 shorter events, 11.3 us)
Async XLA Ops:
  7.2 93.7 %copy-start = (bf16[128,4096]{1,0:T(8,128)(2,1)S(1)}, bf16[128,4096]{1,0:T(8,128)(2,1)}, u32[]{:S(2)}) copy-start(bf16[128,4096]{1,0:T(8,128)(2,1)} %param.11) | copy-start | bytes 3145732
  7.2 93.7 %all-gather.6.cloned.1.call-start = ((), (), s32[]{:S(2)}) async-start(), calls=%async_computation.8 | async-start | bytes 4456448 | tf_op jit(solution)/shard_map/all_gather | solution.py:59
  7.9 188.1 %all-gather.8.cloned.1.call-start = ((), (), s32[]{:S(2)}) async-start(), calls=%async_computation.9 | async-start | bytes 6684672 | tf_op jit(solution)/shard_map/all_gather | solution.py:54
  8.7 249.2 %all-gather.10.cloned.1.call-start = ((), (), s32[]{:S(2)}) async-start(), calls=%async_computation.10 | async-start | bytes 2228224 | tf_op jit(solution)/shard_map/all_gather | solution.py:55
  9.4 391.9 %all-gather.12.cloned.1.call-start = ((), (), s32[]{:S(2)}) async-start(), calls=%async_computation.11 | async-start | bytes 12255232 | tf_op jit(solution)/shard_map/all_gather | solution.py:57
  10.0 481.6 %all-gather.14.cloned.1.call-start = ((), (), s32[]{:S(2)}) async-start(), calls=%async_computation.12 | async-start | bytes 6127616 | tf_op jit(solution)/shard_map/all_gather | solution.py:58
  10.6 524.4 %reduce-scatter.13.cloned.1.call-start = ((), (), s32[]{:S(2)}) async-start(), calls=%async_computation.13 | async-start | bytes 393216 | tf_op jit(solution)/shard_map/reduce_scatter | solution.py:146
  58.6 48.0 %copy-start.6 = (bf16[128,1,1024]{2,0,1:T(8,128)(2,1)S(1)}, bf16[128,1,1024]{2,0,1:T(8,128)(2,1)}, u32[]{:S(2)}) copy-start(bf16[128,1,1024]{2,0,1:T(8,128)(2,1)} %param.10) | copy-start | bytes 786436
  106.8 93.1 %copy-start.38 = (f32[128]{0:T(128)}, f32[128]{0:T(128)S(1)}, u32[]{:S(2)}) copy-start(f32[128]{0:T(128)S(1)} %add_rsqrt_fusion.1) | copy-start | bytes 1540
  200.8 4.3 collective-permute-start
  202.9 8.9 copy-start.36
  206.4 9.1 copy-start.3
  211.7 7.0 copy-start.25
  211.8 48.2 %copy-start.30 = (f32[128,16]{0,1:T(8,128)}, f32[128,16]{0,1:T(8,128)S(1)}, u32[]{:S(2)}) copy-start(f32[128,16]{0,1:T(8,128)S(1)} %fusion.72) | copy-start | bytes 24580
  211.9 6.7 copy-start.28
  218.7 39.2 %copy-start.7 = (bf16[128,1,1024]{2,0,1:T(8,128)(2,1)S(1)}, bf16[128,1,1024]{2,0,1:T(8,128)(2,1)}, u32[]{:S(2)}) copy-start(bf16[128,1,1024]{2,0,1:T(8,128)(2,1)} %param.10) | copy-start | bytes 786436
  218.7 39.2 %copy-start.15 = (bf16[128,1024]{1,0:T(8,128)(2,1)S(1)}, bf16[128,1024]{1,0:T(8,128)(2,1)}, u32[]{:S(2)}) copy-start(bf16[128,1024]{1,0:T(8,128)(2,1)} %get-tuple-element.52) | copy-start | bytes 786436
  260.0 148.9 %copy-start.33 = (f32[128]{0:T(128)}, f32[128]{0:T(128)S(1)}, u32[]{:S(2)}) copy-start(f32[128]{0:T(128)S(1)} %add_rsqrt_fusion) | copy-start | bytes 1540
  401.3 90.3 %copy-start.21 = (bf16[128,1,1024]{2,0,1:T(8,128)(2,1)S(1)}, bf16[128,1,1024]{2,0,1:T(8,128)(2,1)}, u32[]{:S(2)}) copy-start(bf16[128,1,1024]{2,0,1:T(8,128)(2,1)} %param.19) | copy-start | bytes 786436
  491.6 6.8 copy-start.2
  491.6 6.8 copy-start.34
  498.3 3.9 copy-start.11
  498.3 3.9 copy-start.13
  498.3 5.0 copy-start.5
  504.2 2.7 copy-start.26
  504.2 2.7 copy-start.32
  504.2 2.7 copy-start.37
  504.2 2.8 copy-start.31
  504.3 2.9 copy-start.29
  505.5 1.7 copy-start.17
  508.4 1.0 copy-start.4
  510.2 9.2 collective-permute-start.1
  517.5 3.2 copy-start.39
  519.3 1.4 copy-start.8
  519.3 1.4 copy-start.23
  520.7 5.3 copy-start.18
  527.2 87.9 %reduce-scatter.27.cloned.1.call-start = ((), (), s32[]{:S(2)}) async-start(), calls=%async_computation.21 | async-start | bytes 557056
  528.6 161.8 %reduce-scatter.25.cloned.1.call-start = ((), (), s32[]{:S(2)}) async-start(), calls=%async_computation.20 | async-start | bytes 557056
  529.7 9.4 copy-start.16
  529.7 179.7 %all-reduce.7.cloned.1.call-start = ((), (), s32[]{:S(2)}) async-start(), calls=%async_computation.14 | async-start | bytes 2097152 | tf_op jit(solution)/shard_map/psum | solution.py:151
  539.0 269.4 %reduce-scatter.19.cloned.1.call-start = ((), (), s32[]{:S(2)}) async-start(), calls=%async_computation.17 | async-start | bytes 4456448 | tf_op jit(solution)/shard_map/reduce_scatter | solution.py:155
  541.9 0.9 copy-start.27
  541.9 446.9 %reduce-scatter.15.cloned.1.call-start = ((), (), s32[]{:S(2)}) async-start(), calls=%async_computation.15 | async-start | bytes 8912896 | tf_op jit(solution)/shard_map/reduce_scatter | solution.py:159
  547.3 1.1 copy-start.10
  547.3 1.2 copy-start.22
  547.4 687.4 %reduce-scatter.23.cloned.1.call-start = ((), (), s32[]{:S(2)}) async-start(), calls=%async_computation.19 | async-start | bytes 12255232 | tf_op jit(solution)/shard_map/reduce_scatter | solution.py:158
  554.5 1.0 copy-start.9
  554.5 1.1 copy-start.19
  554.5 1.2 copy-start.24
  554.5 895.1 %reduce-scatter.17.cloned.1.call-start = ((), (), s32[]{:S(2)}) async-start(), calls=%async_computation.16 | async-start | bytes 13369344 | tf_op jit(solution)/shard_map/reduce_scatter | solution.py:154
  562.1 1.1 copy-start.12
  562.1 1.3 copy-start.14
  562.1 1.3 copy-start.35
  562.2 1362.9 %reduce-scatter.21.cloned.1.call-start = ((), (), s32[]{:S(2)}) async-start(), calls=%async_computation.18 | async-start | bytes 24510464 | tf_op jit(solution)/shard_map/reduce_scatter | solution.py:157
  573.0 43.5 %copy-start.20 = (f32[128,1,1024]{2,0,1:T(8,128)S(1)}, f32[128,1,1024]{2,0,1:T(8,128)}, u32[]{:S(2)}) copy-start(f32[128,1,1024]{2,0,1:T(8,128)} %get-tuple-element.47) | copy-start | bytes 1572868
  616.5 1308.5 %copy-start.1 = (bf16[128,4096]{1,0:T(8,128)(2,1)S(1)}, bf16[128,4096]{1,0:T(8,128)(2,1)}, u32[]{:S(2)}) copy-start(bf16[128,4096]{1,0:T(8,128)(2,1)} %param.11) | copy-start | bytes 3145732
Sparse Core Ops, SparseCore 0:
  10.7 90.0 all-gather.5
  103.7 92.3 all-gather.7
  198.8 58.9 all-gather.9
  260.5 140.7 all-gather.11
  403.8 87.6 all-gather.13
  527.3 7.6 reduce-scatter.12
  537.4 77.7 reduce-scatter.26
  617.4 72.8 reduce-scatter.24
  693.4 15.9 all-reduce.6
  712.1 96.2 reduce-scatter.18
  811.2 177.4 reduce-scatter.14
  991.5 243.2 reduce-scatter.22
  1241.0 208.4 reduce-scatter.16
  1452.4 472.5 reduce-scatter.20
where the time goes:
time: 1940 us; the launch traced here: 1930 us
  waiting for transfers between devices  1740 us (90%)
  matrix products  71 us (4%)
  blocking collectives  46.4 us (2%)
  local copies, waits for them, and re-layouts  35.1 us (2%)
  other arithmetic  19.7 us (1%)
    reduce_scatter x1, waiting for transfers between devices, on_device(): lax.psum_scatter(grad_gate_up, 'frames', scatter_dimension=1, tiled=True)  475 us
    reduce_scatter x1, waiting for transfers between devices, on_device(): lax.psum_scatter(grad_down, 'frames', scatter_dimension=1, tiled=True)  246 us
    reduce_scatter x1, waiting for transfers between devices, on_device(): lax.psum_scatter(grad_qkv, 'frames', scatter_dimension=1, tiled=True)  215 us
    reduce_scatter x1, waiting for transfers between devices, on_device(): lax.psum_scatter(grad_in, 'frames', scatter_dimension=1, tiled=True)  180 us
    all_gather x1, waiting for transfers between devices, on_device(): lax.all_gather(shards[4], 'frames', axis=1, tiled=True)  141 us
    unnamed x16, waiting for transfers between devices  113 us
    reduce_scatter x1, waiting for transfers between devices, on_device(): lax.psum_scatter(grad_out, 'frames', scatter_dimension=1, tiled=True)  96.3 us
    all_gather x1, waiting for transfers between devices, on_device(): lax.all_gather(shards[1], 'frames', axis=1, tiled=True)  89.3 us
  transfers between devices with their start and end apart: 16, of which 14 were waited for; matrix products, arithmetic and copies ran while one was open for 5% of the time, Pallas kernels for 0%

commit v1 on v0

v1 whole, which is shorter than its diff:
```python
import jax
import jax.numpy as jnp
from jax import lax
from jax.sharding import Mesh
from jax.sharding import PartitionSpec as P

HD = 64
F32 = jnp.float32
BF = jnp.bfloat16


def dot(form, a, b):
    return jnp.einsum(form, a, b, preferred_element_type=F32)


def peers(r):
    return [(i, i ^ r) for i in range(4)]


def hop(x, r):
    return lax.ppermute(x, "t", peers(r))


def spread(x):
    return [x] + [hop(x, r) for r in (1, 2, 3)]


def collect(x):
    b = x.shape[0] // 4
    low = [x[r * b : (r + 1) * b].astype(BF) for r in range(4)]
    return low[0].astype(F32) + sum(hop(low[r], r).astype(F32) for r in (1, 2, 3))


def swap(x):
    return lax.ppermute(x, "stream", [(0, 1), (1, 0)])


def norm_parts(v):
    scale = lax.rsqrt(jnp.mean(v * v, axis=-1, keepdims=True) + 1e-05)
    return v * scale, scale


def norm_back(unit, scale, g):
    return scale * (g - unit * jnp.mean(g * unit, axis=-1, keepdims=True))


def columns_to_t(w, k):
    rows = w.shape[0]
    c = w.shape[1] // (k * 16)
    w = w.reshape(rows, k, 4, 4, c).transpose(3, 0, 1, 2, 4).reshape(4, rows, k * 4 * c)
    return lax.all_to_all(w, "t", 0, 0, tiled=True).reshape(4 * rows, k * 4 * c)


def columns_back(g, k):
    rows = g.shape[0] // 4
    c = g.shape[1] // (k * 4)
    g = lax.all_to_all(g.reshape(4, rows, k * 4 * c), "t", 0, 0, tiled=True)
    return g.reshape(4, rows, k, 4, c).transpose(1, 2, 3, 0, 4).reshape(rows, k * 16 * c)


def on_device(
    tokens, context, w_in, attn_gain, w_qkv, w_out, ffn_gain, w_gate_up, w_down, cotangent
):
    s = lax.axis_index("stream")
    t = lax.axis_index("t")
    many = lax.axis_size("d2") > 1
    frames = tokens.shape[0]
    d = tokens.shape[2]
    half = frames // 2

    def near(w, axis=0):
        return lax.all_gather(w, "d2", axis=axis, tiled=True) if many else w

    def near_sum(g, axis=0):
        return lax.psum_scatter(g, "d2", scatter_dimension=axis, tiled=True) if many else g

    def over_d(w, axis=0):
        return lax.all_gather(w, "d1", axis=axis, tiled=True)

    def sum_d(g, axis=0):
        return lax.psum_scatter(g.astype(BF), "d1", scatter_dimension=axis, tiled=True)

    tokens = tokens[:, 0]
    cotangent = cotangent[:, 0]
    gain_one = lax.all_gather(attn_gain[0], ("d1", "t", "d2"), axis=0, tiled=True).astype(F32)
    gain_two = lax.all_gather(ffn_gain[0], ("d1", "t", "d2"), axis=0, tiled=True).astype(F32)
    in_w = over_d(near(w_in, 1), 1)
    qkv_w = over_d(columns_to_t(near(w_qkv[0]), 3))
    out_w = over_d(near(w_out[0]))
    gu_w = over_d(columns_to_t(near(w_gate_up[0]), 2))
    down_w = over_d(near(w_down[0]))

    mine = lax.dynamic_slice_in_dim(context, s * half, half, 0).reshape(half, 4, 4, -1)
    feats = mine.shape[-1] * 4
    parts = []
    for r in range(4):
        block = lax.dynamic_index_in_dim(mine, t ^ r, 2, keepdims=False).reshape(half, feats)
        parts.append(hop(block, r) if r else block)
    own = jnp.stack(parts)
    other = swap(own)
    group = jnp.where(
        s == 0, jnp.concatenate([own, other], axis=1), jnp.concatenate([other, own], axis=1)
    ).reshape(4 * frames, feats)

    proj_half = collect(dot("fc,dc->fd", group, in_w)).astype(BF)
    proj_other = swap(proj_half)
    projected = jnp.where(
        s == 0,
        jnp.concatenate([proj_half, proj_other], axis=1),
        jnp.concatenate([proj_other, proj_half], axis=1),
    )
    start = tokens.astype(F32) + projected.astype(F32)
    unit_one, scale_one = norm_parts(start)
    normed_one = jnp.concatenate(spread((unit_one * gain_one).astype(BF)))
    qkv = dot("fd,de->fe", normed_one, qkv_w).astype(BF)
    width = qkv.shape[1] // 3
    far = lax.ppermute(qkv[:, width:], "stream", [(0, 1)]).astype(F32)
    q, k, v = (qkv[:, i * width : (i + 1) * width].astype(F32) for i in range(3))
    lane = jnp.arange(width) // HD
    heads = (lane[:, None] == lane[None, :]).astype(F32)

    def head_sum(x):
        return jnp.dot(x, heads, precision=lax.Precision.HIGHEST)

    dk = k - far[:, :width]
    dv = v - far[:, width:]
    w_own = jnp.where(s == 0, 1.0, jax.nn.sigmoid(head_sum(q * dk) * HD ** (-0.5)))
    w_far = 1.0 - w_own
    mixed = (w_own * v + w_far * far[:, width:]).astype(BF)
    middle = start + collect(dot("fd,de->fe", mixed, out_w))
    unit_two, scale_two = norm_parts(middle)
    normed_two = jnp.concatenate(spread((unit_two * gain_two).astype(BF)))
    cot = jnp.concatenate(spread(cotangent))
    gate_up = dot("fd,de->fe", normed_two, gu_w)
    ff = gate_up.shape[1] // 2
    gate, up = gate_up[:, :ff], gate_up[:, ff:]
    sig = jax.nn.sigmoid(gate)
    hidden = (gate * sig * up).astype(BF)
    result = middle + collect(dot("fk,kd->fd", hidden, down_w))

    grad_down = near_sum(sum_d(dot("fk,fd->kd", hidden, cot)).astype(F32))
    grad_hidden = dot("fd,kd->fk", cot, down_w)
    grad_gu = jnp.concatenate(
        [grad_hidden * up * sig * (1.0 + gate * (1.0 - sig)), grad_hidden * gate * sig], axis=-1
    ).astype(BF)
    grad_normed_two = collect(dot("fe,de->fd", grad_gu, gu_w))
    grad_gate_up = near_sum(
        columns_back(sum_d(dot("fd,fe->de", normed_two, grad_gu)), 2).astype(F32)
    )
    grad_gain_two = jnp.sum(grad_normed_two * unit_two, axis=0)
    grad_middle = cotangent.astype(F32) + norm_back(
        unit_two, scale_two, grad_normed_two * gain_two
    )
    branch = jnp.concatenate(spread(grad_middle.astype(BF)))
    grad_out = near_sum(sum_d(dot("fd,fe->de", mixed, branch)).astype(F32))
    gm = dot("fe,de->fd", branch, out_w)
    gs = w_own * w_far * head_sum(gm * dv) * HD ** (-0.5)
    gq = gs * dk
    gk = gs * q
    back = lax.ppermute(
        jnp.concatenate([-gk, w_far * gm], axis=1).astype(BF), "stream", [(1, 0)]
    ).astype(F32)
    grad_kv = jnp.concatenate([gk, w_own * gm], axis=1) + back
    grad_qkv_low = jnp.concatenate([gq, grad_kv], axis=1).astype(BF)
    grad_normed_one = collect(dot("fe,de->fd", grad_qkv_low, qkv_w))
    grad_qkv = near_sum(
        columns_back(sum_d(dot("fd,fe->de", normed_one, grad_qkv_low)), 3).astype(F32)
    )
    grad_gain_one = jnp.sum(grad_normed_one * unit_one, axis=0)
    grad_start = grad_middle + norm_back(unit_one, scale_one, grad_normed_one * gain_one)
    halves = grad_start.astype(BF).reshape(frames, 2, d // 2)
    keep = lax.dynamic_index_in_dim(halves, s, 1, keepdims=False)
    give = lax.dynamic_index_in_dim(halves, 1 - s, 1, keepdims=False)
    grad_proj = (keep.astype(F32) + swap(give).astype(F32)).astype(BF)
    gproj = jnp.concatenate(spread(grad_proj))
    grad_in = near_sum(sum_d(dot("fd,fc->dc", gproj, group), 1).astype(F32), 1)
    term = dot("fd,dc->fc", gproj, in_w).astype(BF).reshape(4, 2, half, feats)
    keep = lax.dynamic_index_in_dim(term, s, 1, keepdims=False)
    give = lax.dynamic_index_in_dim(term, 1 - s, 1, keepdims=False)
    both = (keep.astype(F32) + swap(give).astype(F32)).astype(BF).reshape(4, half, 4, feats // 4)
    got = jnp.stack([hop(both[r], r) if r else both[0] for r in range(4)])
    ordered = jnp.stack(
        [lax.dynamic_index_in_dim(got, t ^ j, 0, keepdims=False) for j in range(4)], axis=2
    ).reshape(half, -1)
    far_half = swap(ordered)
    grad_context = jnp.where(
        s == 0, jnp.concatenate([ordered, far_half]), jnp.concatenate([far_half, ordered])
    ).astype(F32)
    gains = lax.psum_scatter(
        jnp.stack([grad_gain_one, grad_gain_two]),
        ("d1", "t", "d2"),
        scatter_dimension=1,
        tiled=True,
    )
    return (
        result[:, None],
        grad_start[:, None],
        grad_context,
        grad_in,
        gains[:1],
        grad_qkv[None],
        grad_out[None],
        gains[1:],
        grad_gate_up[None],
        grad_down[None],
    )


def solution(mesh):
    n = mesh.shape["frames"]
    grid = Mesh(mesh.devices.reshape(2, 4, 4, n // 16), ("stream", "d1", "t", "d2"))
    f = ("d1", "t", "d2")
    return jax.shard_map(
        on_device,
        mesh=grid,
        in_specs=(
            P(f, "stream", None),
            P(f, None),
            P("stream", f),
            P("stream", f),
            P("stream", f, None),
            P("stream", f, None),
            P("stream", f),
            P("stream", f, None),
            P("stream", f, None),
            P(f, "stream", None),
        ),
        out_specs=(
            P(f, "stream", None),
            P(f, "stream", None),
            P(f, None),
            P("stream", f),
            P("stream", f),
            P("stream", f, None),
            P("stream", f, None),
            P("stream", f),
            P("stream", f, None),
            P("stream", f, None),
        ),
        check_vma=False,
    )
```

time: 1940 us -> 526 us (0.27)
  waiting for transfers between devices: 1740 us -> 267 us
  starting transfers between devices: 4.15 us -> 54.1 us
  blocking collectives: 46.4 us -> 86.7 us
  matrix products: 71 us -> 40.9 us
    reduce_scatter x6 -> x5, waiting for transfers between devices: 1220 us -> 131 us  [sum_d(): lax.psum_scatter(g.astype(BF), 'd1', scatter_dimension=axis, tiled=True)]
    all_gather x5 -> x4, waiting for transfers between devices: 391 us -> 2.39 us  [over_d(): return lax.all_gather(w, 'd1', axis=axis, tiled=True)]
    ppermute x2 -> x43, waiting for transfers between devices: 0.01 us -> 88.7 us  [the longest x36 81.1 us: hop(): return lax.ppermute(x, 't', peers(r))]
    unnamed x16 -> x11, waiting for transfers between devices: 113 us -> 45 us
    ppermute x2 -> x43, starting transfers between devices: 3.37 us -> 46 us  [the longest x36 42.7 us: hop(): return lax.ppermute(x, 't', peers(r))]
    dot_general x15 -> x17, matrix products: 71 us -> 40.9 us  [the longest x15 37.7 us: dot(): return jnp.einsum(form, a, b, preferred_element_type=F32)]
    all_to_all x0 -> x2, blocking collectives: none -> 24.8 us  [columns_to_t(): return lax.all_to_all(w, 't', 0, 0, tiled=True).reshape(4 * rows, k * 4 * c)]
  transfers between devices with their start and end apart: 16 -> 55, of which waited for: 14 -> 36; matrix products, arithmetic and copies ran while one was open for 5% -> 13% of each run, Pallas kernels for 0% -> 0%
where the time goes in v1:
time: 526 us; the launch traced here: 520 us
  waiting for transfers between devices  267 us (51%)
  blocking collectives  86.7 us (16%)
  starting transfers between devices  54.1 us (10%)
  local copies, waits for them, and re-layouts  41.4 us (8%)
  matrix products  40.9 us (8%)
  between operations  16 us (3%)
  other arithmetic  13.9 us (3%)
    reduce_scatter x5, waiting for transfers between devices, sum_d(): lax.psum_scatter(g.astype(BF), 'd1', scatter_dimension=axis, tiled=True)  131 us
    ppermute x36, waiting for transfers between devices, hop(): return lax.ppermute(x, 't', peers(r))  81.1 us
    unnamed x11, waiting for transfers between devices  45 us
    ppermute x36, starting transfers between devices, hop(): return lax.ppermute(x, 't', peers(r))  42.7 us
    unnamed x1, blocking collectives  42.1 us
    dot_general x15, matrix products, dot(): return jnp.einsum(form, a, b, preferred_element_type=F32)  37.7 us
    all_to_all x2, blocking collectives, columns_to_t(): return lax.all_to_all(w, 't', 0, 0, tiled=True).reshape(4 * rows, k * 4 * c)  24.8 us
    all_gather x1, blocking collectives, over_d(): return lax.all_gather(w, 'd1', axis=axis, tiled=True)  19.8 us
  transfers between devices with their start and end apart: 55, of which 36 were waited for; matrix products, arithmetic and copies ran while one was open for 13% of the time, Pallas kernels for 0%

profile of v1, /device:TPU:0, one launch (start us, length us, event | category | flops | bytes accessed | tf_op | source)
XLA Modules:
  0.0 520.2 jit_solution(8159532757236586821)
XLA Ops:
  10.3 12.2 %all_to_all.20 = bf16[4,64,768]{2,1,0:T(8,128)(2,1)} all-to-all(bf16[4,64,768]{2,1,0:T(8,128)(2,1)S(1)} %reshape.174), channel_id=1, replica_groups=mesh['stream'=2,'d1'=4,'t'=4,'d2'=1] {'t'}, dimensions={0} | all-to-all | bytes 786432 | tf_op jit(solution)/shard_map/all_to_all | solution.py:51
  22.5 4.4 reshape_squeeze.7
  28.5 12.7 %all_to_all.21 = bf16[4,64,1408]{2,1,0:T(8,128)(2,1)} all-to-all(bf16[4,64,1408]{2,1,0:T(8,128)(2,1)S(1)} %reshape.176), channel_id=1, replica_groups=mesh['stream'=2,'d1'=4,'t'=4,'d2'=1] {'t'}, dimensions={0} | all-to-all | bytes 1441792 | tf_op jit(solution)/shard_map/all_to_all | solution.py:51
  41.9 3.3 dynamic-slice_reduce_fusion.3
  49.0 2.2 collective-permute-done.2
  52.8 1.9 collective-permute-done.3
  55.3 2.4 convolution_convert_fusion.11
  61.3 3.8 collective-permute-done.6
  65.1 2.0 collective-permute-done.5
  69.3 42.1 %all-reduce.2 = (bf16[1024]{0:T(1024)(128)(2,1)S(1)}, bf16[1024]{0:T(1024)(128)(2,1)S(1)}) all-reduce(bf16[1024]{0:T(1024)(128)(2,1)S(1)} %dynamic-update-slice, bf16[1024]{0:T(1024)(128)(2,1)S(1)} %dynamic-update-slice.1), channel_id=2, replica_groups=mesh['stream'=2,'d1'=4,'t'=4,'d2'=1] {'d1','t','d2'}, use_global_device_ids=true, to_apply=%add | all-reduce | flops 2048 | bytes 8192
  111.9 3.4 collective-permute-start.8
  115.3 3.9 collective-permute-done.10
  119.2 1.9 collective-permute-done.9
  121.9 2.4 convolution_convert_fusion.9
  125.8 19.8 %all-gather.1 = bf16[1,256,1024]{2,1,0:T(8,128)(2,1)S(1)} all-gather(bf16[1,64,1024]{2,1,0:T(8,128)(2,1)S(1)} %copy-done.19), channel_id=3, replica_groups=mesh['stream'=2,'d1'=4,'t'=4,'d2'=1] {'d1'}, dimensions={1}, use_global_device_ids=true | all-gather | bytes 655360 | tf_op jit(solution)/shard_map/all_gather | solution.py:78
  151.4 6.5 %collective-permute-done.14 = bf16[128,1024]{0,1:T(8,128)(2,1)S(1)} collective-permute-done((bf16[128,1024]{0,1:T(8,128)(2,1)S(1)}, bf16[128,1024]{0,1:T(8,128)(2,1)S(1)}, u32[]{:S(2)}, u32[]{:S(2)}) %collective-permute-start.14) | collective-permute-done | bytes 262176 | tf_op jit(solution)/shard_map/ppermute | solution.py:21
  157.8 5.7 %collective-permute-done.13 = bf16[128,1024]{0,1:T(8,128)(2,1)S(1)} collective-permute-done((bf16[128,1024]{0,1:T(8,128)(2,1)S(1)}, bf16[128,1024]{0,1:T(8,128)(2,1)S(1)}, u32[]{:S(2)}, u32[]{:S(2)}) %collective-permute-start.13) | collective-permute-done | bytes 262176 | tf_op jit(solution)/shard_map/ppermute | solution.py:21
  169.9 2.4 collective-permute-done.17
  172.7 2.2 collective-permute-done.16
  174.9 5.5 %fusion.28 = f32[512,1408]{1,0:T(8,128)} fusion(bf16[1024,1408]{1,0:T(8,128)(2,1)} %all-gather.13.cloned.1.call-done, bf16[128,1024]{0,1:T(8,128)(2,1)} %collective-permute-done.17, bf16[128,1024]{0,1:T(8,128)(2,1)} %collective-permute-done.16, bf16[128,1024]{0,1:T(8,128)(2,1)} %collective-permute-done.15, bf16[128,1024]{0,1:T(8,128)(2,1)S(1)} %multiply_convert_fusion.4), kind=kOutput, calls=%fused_computation.98 | convolution fusion | flops 1480589312 | bytes 6815744 | tf_op jit(solution)/shard_map/fd,de->fe/dot_general | solution.py:13
  180.5 2.4 all-gather.15.cloned.1.call-done
  182.9 4.2 multiply_convert_fusion.1
  187.2 1.8 convolution_convert_fusion.4
  189.2 2.4 collective-permute-start.26
  193.9 2.4 collective-permute-start.20
  196.9 2.5 collective-permute-done.26
  200.9 4.2 collective-permute-done.25
  205.5 5.2 collective-permute-done.20
  210.7 3.6 collective-permute-done.19
  215.5 1.7 collective-permute-start.29
  219.0 6.6 %collective-permute-done.29 = bf16[128,1024]{0,1:T(8,128)(2,1)S(1)} collective-permute-done((bf16[128,1024]{0,1:T(8,128)(2,1)S(1)}, bf16[128,1024]{0,1:T(8,128)(2,1)S(1)}, u32[]{:S(2)}, u32[]{:S(2)}) %collective-permute-start.29) | collective-permute-done | bytes 262176 | tf_op jit(solution)/shard_map/ppermute | solution.py:21
  225.6 4.5 collective-permute-done.28
  231.0 1.7 negate_convert_fusion
  234.2 2.5 collective-permute-done.30
  236.9 2.1 convolution_convert_fusion.1
  239.3 2.5 convolution_convert_fusion.3
  245.5 6.6 %collective-permute-done.33 = bf16[128,1024]{0,1:T(8,128)(2,1)S(1)} collective-permute-done((bf16[128,1024]{0,1:T(8,128)(2,1)S(1)}, bf16[128,1024]{0,1:T(8,128)(2,1)S(1)}, u32[]{:S(2)}, u32[]{:S(2)}) %collective-permute-start.33) | collective-permute-done | bytes 262176 | tf_op jit(solution)/shard_map/ppermute | solution.py:21
  252.1 4.8 collective-permute-done.32
  259.3 2.6 convolution_convert_fusion.10
  261.9 5.1 convolution_convert_fusion
  267.9 3.5 convolution_convert_fusion.2
  279.7 3.8 collective-permute-done.37
  283.5 2.0 collective-permute-done.36
  286.2 1.9 convolution_convert_fusion.8
  288.3 1.9 collective-permute-done.38
  294.4 1.7 convolution_convert_fusion.7
  296.2 2.4 collective-permute-done.41
  298.6 1.9 collective-permute-done.40
  304.3 3.5 all-to-all-start.2
  307.8 44.1 %reduce-scatter.19.cloned.1.call-done = f32[64,2]{1,0:T(8,128)} async-done(((f32[1024,2]{1,0:T(8,128)}), f32[64,2]{1,0:T(8,128)}) %reduce-scatter.19.cloned.1.call-update) | async-done | bytes 528
  354.0 18.9 %reduce-scatter.13.cloned.1.call-done = bf16[64,1024]{1,0:T(8,128)(2,1)} async-done(((bf16[256,1024]{1,0:T(8,128)(2,1)}), bf16[64,1024]{1,0:T(8,128)(2,1)}) %reduce-scatter.13.cloned.1.call-update) | async-done | bytes 131088 | tf_op jit(solution)/shard_map/reduce_scatter | solution.py:81
  372.8 1.6 bitcast_convert_fusion.1
  374.5 55.2 %reduce-scatter.15.cloned.1.call-done = bf16[256,1408]{1,0:T(8,128)(2,1)} async-done(((bf16[1024,1408]{1,0:T(8,128)(2,1)}), bf16[256,1408]{1,0:T(8,128)(2,1)}) %reduce-scatter.15.cloned.1.call-update) | async-done | bytes 720912 | tf_op jit(solution)/shard_map/reduce_scatter | solution.py:81
  429.7 3.9 all-to-all-start.3
  435.1 30.7 %reduce-scatter.17.cloned.1.call-done = bf16[176,1024]{1,0:T(8,128)(2,1)} async-done(((bf16[704,1024]{1,0:T(8,128)(2,1)}), bf16[176,1024]{1,0:T(8,128)(2,1)}) %reduce-scatter.17.cloned.1.call-update) | async-done | bytes 360464 | tf_op jit(solution)/shard_map/reduce_scatter | solution.py:81
  465.8 1.9 bitcast_convert_fusion
  467.7 26.4 %reduce-scatter.9.cloned.1.call-done = bf16[512,256]{1,0:T(8,128)(2,1)} async-done(((bf16[512,1024]{1,0:T(8,128)(2,1)}), bf16[512,256]{1,0:T(8,128)(2,1)}) %reduce-scatter.9.cloned.1.call-update) | async-done | bytes 262160 | tf_op jit(solution)/shard_map/reduce_scatter | solution.py:81
  494.1 1.8 convert_element_type.279
  495.9 1.8 reshape.190
  497.7 2.4 copy.131
  500.1 2.0 reshape.186
  502.1 4.4 reshape.191
  506.5 3.0 copy.130
  509.6 3.5 reshape.188
  (235 shorter events, 70.0 us)
Async XLA Ops:
  7.2 34.2 %copy-start = (bf16[128,4096]{1,0:T(8,128)(2,1)S(1)}, bf16[128,4096]{1,0:T(8,128)(2,1)}, u32[]{:S(2)}) copy-start(bf16[128,4096]{1,0:T(8,128)(2,1)} %param.11) | copy-start | bytes 3145732
  7.2 48.1 %all-gather.9.cloned.1.call-start = ((), (), s32[]{:S(2)}) async-start(), calls=%async_computation.10 | async-start | bytes 1310720 | tf_op jit(solution)/shard_map/all_gather | solution.py:78
  7.9 113.2 %all-gather.11.cloned.1.call-start = ((), (), s32[]{:S(2)}) async-start(), calls=%async_computation.11 | async-start | bytes 1966080 | tf_op jit(solution)/shard_map/all_gather | solution.py:78
  22.5 152.4 %all-gather.13.cloned.1.call-start = ((), (), s32[]{:S(2)}) async-start(), calls=%async_computation.12 | async-start | bytes 3604480 | tf_op jit(solution)/shard_map/all_gather | solution.py:78
  41.1 141.7 %all-gather.15.cloned.1.call-start = ((), (), s32[]{:S(2)}) async-start(), calls=%async_computation.18 | async-start | bytes 1802240 | tf_op jit(solution)/shard_map/all_gather | solution.py:78
  45.2 6.0 %collective-permute-start.2 = (bf16[64,1024]{1,0:T(8,128)(2,1)S(1)}, bf16[64,1024]{1,0:T(8,128)(2,1)S(1)}, u32[]{:S(2)}, u32[]{:S(2)}) collective-permute-start(bf16[64,1024]{1,0:T(8,128)(2,1)S(1)} %bitcast.140), channel_id=1, source_target_pairs={{0,3},{1,2},{2,1},{3,0},{4,7},{5,6},{6,5},{7,4},{8,11},{9,10},{10,... | collective-permute-start | bytes 393224 | tf_op jit(solution)/shard_map/ppermute | solution.py:21
  46.1 6.4 %collective-permute-start.1 = (bf16[64,1024]{1,0:T(8,128)(2,1)S(1)}, bf16[64,1024]{1,0:T(8,128)(2,1)S(1)}, u32[]{:S(2)}, u32[]{:S(2)}) collective-permute-start(bf16[64,1024]{1,0:T(8,128)(2,1)S(1)} %bitcast.141), channel_id=1, source_target_pairs={{0,2},{1,3},{2,0},{3,1},{4,6},{5,7},{6,4},{7,5},{8,10},{9,11},{10,... | collective-permute-start | bytes 393224 | tf_op jit(solution)/shard_map/ppermute | solution.py:21
  47.6 5.1 collective-permute-start
  52.8 2.0 collective-permute-start.3
  57.8 7.3 %collective-permute-start.6 = (bf16[128,512]{0,1:T(8,128)(2,1)S(1)}, bf16[128,512]{0,1:T(8,128)(2,1)S(1)}, u32[]{:S(2)}, u32[]{:S(2)}) collective-permute-start(bf16[128,512]{0,1:T(8,128)(2,1)S(1)} %get-tuple-element.96), channel_id=1, source_target_pairs={{0,3},{1,2},{2,1},{3,0},{4,7},{5,6},{6,5},{7,4},{8,11},{9,10},{10,... | collective-permute-start | bytes 393224 | tf_op jit(solution)/shard_map/ppermute | solution.py:21
  59.3 7.8 %collective-permute-start.5 = (bf16[128,512]{0,1:T(8,128)(2,1)S(1)}, bf16[128,512]{0,1:T(8,128)(2,1)S(1)}, u32[]{:S(2)}, u32[]{:S(2)}) collective-permute-start(bf16[128,512]{0,1:T(8,128)(2,1)S(1)} %get-tuple-element.97), channel_id=1, source_target_pairs={{0,2},{1,3},{2,0},{3,1},{4,6},{5,7},{6,4},{7,5},{8,10},{9,11},{10,... | collective-permute-start | bytes 393224 | tf_op jit(solution)/shard_map/ppermute | solution.py:21
  60.6 6.5 %collective-permute-start.4 = (bf16[128,512]{0,1:T(8,128)(2,1)S(1)}, bf16[128,512]{0,1:T(8,128)(2,1)S(1)}, u32[]{:S(2)}, u32[]{:S(2)}) collective-permute-start(bf16[128,512]{0,1:T(8,128)(2,1)S(1)} %get-tuple-element.95), channel_id=1, source_target_pairs={{0,1},{1,0},{2,3},{3,2},{4,5},{5,4},{6,7},{7,6},{8,9},{9,8},{10,11... | collective-permute-start | bytes 393224 | tf_op jit(solution)/shard_map/ppermute | solution.py:21
  67.2 44.2 %collective-permute-start.7 = (bf16[128,512]{0,1:T(8,128)(2,1)S(1)}, bf16[128,512]{0,1:T(8,128)(2,1)S(1)}, u32[]{:S(2)}, u32[]{:S(2)}) collective-permute-start(bf16[128,512]{0,1:T(8,128)(2,1)S(1)} %add_convert_fusion), channel_id=1, source_target_pairs={{0,16},{16,0},{1,17},{17,1},{2,18},{18,2},{3,19},{19,3},{4,20},{20... | collective-permute-start | bytes 393224 | tf_op jit(solution)/shard_map/ppermute | solution.py:35
  111.7 14.1 %copy-start.19 = (bf16[1,64,1024]{2,1,0:T(8,128)(2,1)S(1)}, bf16[1,64,1024]{2,1,0:T(8,128)(2,1)}, u32[]{:S(2)}) copy-start(bf16[1,64,1024]{2,1,0:T(8,128)(2,1)} %param.15) | copy-start | bytes 393220
  111.8 7.4 %collective-permute-start.10 = (bf16[128,1024]{0,1:T(8,128)(2,1)S(1)}, bf16[128,1024]{0,1:T(8,128)(2,1)S(1)}, u32[]{:S(2)}, u32[]{:S(2)}) collective-permute-start(bf16[128,1024]{0,1:T(8,128)(2,1)S(1)} %multiply_convert_fusion.5), channel_id=1, source_target_pairs={{0,3},{1,2},{2,1},{3,0},{4,7},{5,6},{6,5},{7,4},{8,11},{9,10},{10,... | collective-permute-start | bytes 786440 | tf_op jit(solution)/shard_map/ppermute | solution.py:21
  111.8 9.2 %collective-permute-start.9 = (bf16[128,1024]{0,1:T(8,128)(2,1)S(1)}, bf16[128,1024]{0,1:T(8,128)(2,1)S(1)}, u32[]{:S(2)}, u32[]{:S(2)}) collective-permute-start(bf16[128,1024]{0,1:T(8,128)(2,1)S(1)} %multiply_convert_fusion.5), channel_id=1, source_target_pairs={{0,2},{1,3},{2,0},{3,1},{4,6},{5,7},{6,4},{7,5},{8,10},{9,11},{10,... | collective-permute-start | bytes 786440 | tf_op jit(solution)/shard_map/ppermute | solution.py:21
  111.9 9.2 %collective-permute-start.8 = (bf16[128,1024]{0,1:T(8,128)(2,1)S(1)}, bf16[128,1024]{0,1:T(8,128)(2,1)S(1)}, u32[]{:S(2)}, u32[]{:S(2)}) collective-permute-start(bf16[128,1024]{0,1:T(8,128)(2,1)S(1)} %multiply_convert_fusion.5), channel_id=1, source_target_pairs={{0,1},{1,0},{2,3},{3,2},{4,5},{5,4},{6,7},{7,6},{8,9},{9,8},{10,11... | collective-permute-start | bytes 786440 | tf_op jit(solution)/shard_map/ppermute | solution.py:21
  124.3 22.8 %copy-start.9 = (bf16[512,768]{1,0:T(8,128)(2,1)}, bf16[512,768]{1,0:T(8,128)(2,1)S(1)}, u32[]{:S(2)}) copy-start(bf16[512,768]{1,0:T(8,128)(2,1)S(1)} %convolution_convert_fusion.9) | copy-start | bytes 2359300
  124.4 21.2 %collective-permute-start.11 = (bf16[512,512]{1,0:T(8,128)(2,1)S(1)}, bf16[512,512]{1,0:T(8,128)(2,1)S(1)}, u32[]{:S(2)}, u32[]{:S(2)}) collective-permute-start(bf16[512,512]{1,0:T(8,128)(2,1)S(1)} %slice.170), channel_id=1, source_target_pairs={{0,16},{1,17},{2,18},{3,19},{4,20},{5,21},{6,22},{7,23},{8,24},{9,... | collective-permute-start | bytes 1572872 | tf_op jit(solution)/shard_map/ppermute | solution.py:117
  125.7 178.6 %reduce-scatter.11.cloned.1.call-start = ((), (), s32[]{:S(2)}) async-start(), calls=%async_computation.14 | async-start | bytes 1966080 | tf_op jit(solution)/shard_map/reduce_scatter | solution.py:81
  147.2 16.4 %copy-start.11 = (bf16[512,256]{1,0:T(8,128)(2,1)}, bf16[512,256]{1,0:T(8,128)(2,1)S(1)}, u32[]{:S(2)}) copy-start(bf16[512,256]{1,0:T(8,128)(2,1)S(1)} %get-tuple-element.100) | copy-start | bytes 786436
  147.7 20.0 %copy-start.15 = (bf16[128,1,1024]{2,0,1:T(8,128)(2,1)S(1)}, bf16[128,1,1024]{2,0,1:T(8,128)(2,1)}, u32[]{:S(2)}) copy-start(bf16[128,1,1024]{2,0,1:T(8,128)(2,1)} %param.19) | copy-start | bytes 786436
  147.8 10.0 %collective-permute-start.14 = (bf16[128,1024]{0,1:T(8,128)(2,1)S(1)}, bf16[128,1024]{0,1:T(8,128)(2,1)S(1)}, u32[]{:S(2)}, u32[]{:S(2)}) collective-permute-start(bf16[128,1024]{0,1:T(8,128)(2,1)S(1)} %get-tuple-element.83), channel_id=1, source_target_pairs={{0,3},{1,2},{2,1},{3,0},{4,7},{5,6},{6,5},{7,4},{8,11},{9,10},{10,... | collective-permute-start | bytes 786440 | tf_op jit(solution)/shard_map/ppermute | solution.py:21
  148.9 14.7 %collective-permute-start.13 = (bf16[128,1024]{0,1:T(8,128)(2,1)S(1)}, bf16[128,1024]{0,1:T(8,128)(2,1)S(1)}, u32[]{:S(2)}, u32[]{:S(2)}) collective-permute-start(bf16[128,1024]{0,1:T(8,128)(2,1)S(1)} %get-tuple-element.84), channel_id=1, source_target_pairs={{0,2},{1,3},{2,0},{3,1},{4,6},{5,7},{6,4},{7,5},{8,10},{9,11},{10,... | collective-permute-start | bytes 786440 | tf_op jit(solution)/shard_map/ppermute | solution.py:21
  149.8 13.8 %collective-permute-start.12 = (bf16[128,1024]{0,1:T(8,128)(2,1)S(1)}, bf16[128,1024]{0,1:T(8,128)(2,1)S(1)}, u32[]{:S(2)}, u32[]{:S(2)}) collective-permute-start(bf16[128,1024]{0,1:T(8,128)(2,1)S(1)} %get-tuple-element.82), channel_id=1, source_target_pairs={{0,1},{1,0},{2,3},{3,2},{4,5},{5,4},{6,7},{7,6},{8,9},{9,8},{10,11... | collective-permute-start | bytes 786440 | tf_op jit(solution)/shard_map/ppermute | solution.py:21
  164.1 16.4 %copy-start.18 = (bf16[128,1024]{0,1:T(8,128)(2,1)}, bf16[128,1024]{0,1:T(8,128)(2,1)S(1)}, u32[]{:S(2)}) copy-start(bf16[128,1024]{0,1:T(8,128)(2,1)S(1)} %multiply_convert_fusion.4) | copy-start | bytes 786436
  164.1 8.2 %collective-permute-start.17 = (bf16[128,1024]{0,1:T(8,128)(2,1)S(1)}, bf16[128,1024]{0,1:T(8,128)(2,1)}, u32[]{:S(2)}, u32[]{:S(2)}) collective-permute-start(bf16[128,1024]{0,1:T(8,128)(2,1)S(1)} %multiply_convert_fusion.4), channel_id=1, source_target_pairs={{0,3},{1,2},{2,1},{3,0},{4,7},{5,6},{6,5},{7,4},{8,11},{9,10},{10,... | collective-permute-start | bytes 786440 | tf_op jit(solution)/shard_map/ppermute | solution.py:21
  165.2 9.7 %collective-permute-start.16 = (bf16[128,1024]{0,1:T(8,128)(2,1)S(1)}, bf16[128,1024]{0,1:T(8,128)(2,1)}, u32[]{:S(2)}, u32[]{:S(2)}) collective-permute-start(bf16[128,1024]{0,1:T(8,128)(2,1)S(1)} %multiply_convert_fusion.4), channel_id=1, source_target_pairs={{0,2},{1,3},{2,0},{3,1},{4,6},{5,7},{6,4},{7,5},{8,10},{9,11},{10,... | collective-permute-start | bytes 786440 | tf_op jit(solution)/shard_map/ppermute | solution.py:21
  166.1 8.8 %collective-permute-start.15 = (bf16[128,1024]{0,1:T(8,128)(2,1)S(1)}, bf16[128,1024]{0,1:T(8,128)(2,1)}, u32[]{:S(2)}, u32[]{:S(2)}) collective-permute-start(bf16[128,1024]{0,1:T(8,128)(2,1)S(1)} %multiply_convert_fusion.4), channel_id=1, source_target_pairs={{0,1},{1,0},{2,3},{3,2},{4,5},{5,4},{6,7},{7,6},{8,9},{9,8},{10,11... | collective-permute-start | bytes 786440 | tf_op jit(solution)/shard_map/ppermute | solution.py:21
  167.8 12.6 %collective-permute-start.23 = (bf16[128,1024]{0,1:T(8,128)(2,1)S(1)}, bf16[128,1024]{0,1:T(8,128)(2,1)S(1)}, u32[]{:S(2)}, u32[]{:S(2)}) collective-permute-start(bf16[128,1024]{0,1:T(8,128)(2,1)S(1)} %bitcast.115), channel_id=1, source_target_pairs={{0,3},{1,2},{2,1},{3,0},{4,7},{5,6},{6,5},{7,4},{8,11},{9,10},{10,... | collective-permute-start | bytes 786440 | tf_op jit(solution)/shard_map/ppermute | solution.py:21
  168.9 11.6 %collective-permute-start.22 = (bf16[128,1024]{0,1:T(8,128)(2,1)S(1)}, bf16[128,1024]{0,1:T(8,128)(2,1)}, u32[]{:S(2)}, u32[]{:S(2)}) collective-permute-start(bf16[128,1024]{0,1:T(8,128)(2,1)S(1)} %bitcast.116), channel_id=1, source_target_pairs={{0,2},{1,3},{2,0},{3,1},{4,6},{5,7},{6,4},{7,5},{8,10},{9,11},{10,... | collective-permute-start | bytes 786440 | tf_op jit(solution)/shard_map/ppermute | solution.py:21
  172.3 8.2 %collective-permute-start.21 = (bf16[128,1024]{0,1:T(8,128)(2,1)S(1)}, bf16[128,1024]{0,1:T(8,128)(2,1)}, u32[]{:S(2)}, u32[]{:S(2)}) collective-permute-start(bf16[128,1024]{0,1:T(8,128)(2,1)S(1)} %bitcast.117), channel_id=1, source_target_pairs={{0,1},{1,0},{2,3},{3,2},{4,5},{5,4},{6,7},{7,6},{8,9},{9,8},{10,11... | collective-permute-start | bytes 786440 | tf_op jit(solution)/shard_map/ppermute | solution.py:21
  189.2 10.3 %collective-permute-start.26 = (bf16[128,1024]{0,1:T(8,128)(2,1)S(1)}, bf16[128,1024]{0,1:T(8,128)(2,1)S(1)}, u32[]{:S(2)}, u32[]{:S(2)}) collective-permute-start(bf16[128,1024]{0,1:T(8,128)(2,1)S(1)} %get-tuple-element.77), channel_id=1, source_target_pairs={{0,3},{1,2},{2,1},{3,0},{4,7},{5,6},{6,5},{7,4},{8,11},{9,10},{10,... | collective-permute-start | bytes 786440 | tf_op jit(solution)/shard_map/ppermute | solution.py:21
  191.6 13.5 %collective-permute-start.25 = (bf16[128,1024]{0,1:T(8,128)(2,1)S(1)}, bf16[128,1024]{0,1:T(8,128)(2,1)S(1)}, u32[]{:S(2)}, u32[]{:S(2)}) collective-permute-start(bf16[128,1024]{0,1:T(8,128)(2,1)S(1)} %get-tuple-element.78), channel_id=1, source_target_pairs={{0,2},{1,3},{2,0},{3,1},{4,6},{5,7},{6,4},{7,5},{8,10},{9,11},{10,... | collective-permute-start | bytes 786440 | tf_op jit(solution)/shard_map/ppermute | solution.py:21
  192.2 12.9 %collective-permute-start.24 = (bf16[128,1024]{0,1:T(8,128)(2,1)S(1)}, bf16[128,1024]{0,1:T(8,128)(2,1)S(1)}, u32[]{:S(2)}, u32[]{:S(2)}) collective-permute-start(bf16[128,1024]{0,1:T(8,128)(2,1)S(1)} %get-tuple-element.76), channel_id=1, source_target_pairs={{0,1},{1,0},{2,3},{3,2},{4,5},{5,4},{6,7},{7,6},{8,9},{9,8},{10,11... | collective-permute-start | bytes 786440 | tf_op jit(solution)/shard_map/ppermute | solution.py:21
  193.9 16.8 %collective-permute-start.20 = (bf16[128,1024]{0,1:T(8,128)(2,1)S(1)}, bf16[128,1024]{0,1:T(8,128)(2,1)S(1)}, u32[]{:S(2)}, u32[]{:S(2)}) collective-permute-start(bf16[128,1024]{0,1:T(8,128)(2,1)S(1)} %get-tuple-element.80), channel_id=1, source_target_pairs={{0,3},{1,2},{2,1},{3,0},{4,7},{5,6},{6,5},{7,4},{8,11},{9,10},{10,... | collective-permute-start | bytes 786440 | tf_op jit(solution)/shard_map/ppermute | solution.py:21
  196.4 17.9 %collective-permute-start.19 = (bf16[128,1024]{0,1:T(8,128)(2,1)S(1)}, bf16[128,1024]{0,1:T(8,128)(2,1)S(1)}, u32[]{:S(2)}, u32[]{:S(2)}) collective-permute-start(bf16[128,1024]{0,1:T(8,128)(2,1)S(1)} %get-tuple-element.81), channel_id=1, source_target_pairs={{0,2},{1,3},{2,0},{3,1},{4,6},{5,7},{6,4},{7,5},{8,10},{9,11},{10,... | collective-permute-start | bytes 786440 | tf_op jit(solution)/shard_map/ppermute | solution.py:21
  199.4 15.0 %collective-permute-start.18 = (bf16[128,1024]{0,1:T(8,128)(2,1)S(1)}, bf16[128,1024]{0,1:T(8,128)(2,1)S(1)}, u32[]{:S(2)}, u32[]{:S(2)}) collective-permute-start(bf16[128,1024]{0,1:T(8,128)(2,1)S(1)} %get-tuple-element.79), channel_id=1, source_target_pairs={{0,1},{1,0},{2,3},{3,2},{4,5},{5,4},{6,7},{7,6},{8,9},{9,8},{10,11... | collective-permute-start | bytes 786440 | tf_op jit(solution)/shard_map/ppermute | solution.py:21
  205.5 24.7 %copy-start.10 = (f32[512,256]{1,0:T(8,128)S(1)}, f32[512,256]{1,0:T(8,128)}, u32[]{:S(2)}) copy-start(f32[512,256]{1,0:T(8,128)} %get-tuple-element.101) | copy-start | bytes 1572868
  215.5 15.2 %copy-start.12 = (bf16[128,1024]{0,1:T(8,128)(2,1)}, bf16[128,1024]{0,1:T(8,128)(2,1)S(1)}, u32[]{:S(2)}) copy-start(bf16[128,1024]{0,1:T(8,128)(2,1)S(1)} %get-tuple-element.93) | copy-start | bytes 786436
  215.5 10.1 %collective-permute-start.29 = (bf16[128,1024]{0,1:T(8,128)(2,1)S(1)}, bf16[128,1024]{0,1:T(8,128)(2,1)S(1)}, u32[]{:S(2)}, u32[]{:S(2)}) collective-permute-start(bf16[128,1024]{0,1:T(8,128)(2,1)S(1)} %get-tuple-element.93), channel_id=1, source_target_pairs={{0,3},{1,2},{2,1},{3,0},{4,7},{5,6},{6,5},{7,4},{8,11},{9,10},{10,... | collective-permute-start | bytes 786440 | tf_op jit(solution)/shard_map/ppermute | solution.py:21
  217.2 13.0 %collective-permute-start.28 = (bf16[128,1024]{0,1:T(8,128)(2,1)S(1)}, bf16[128,1024]{0,1:T(8,128)(2,1)S(1)}, u32[]{:S(2)}, u32[]{:S(2)}) collective-permute-start(bf16[128,1024]{0,1:T(8,128)(2,1)S(1)} %get-tuple-element.93), channel_id=1, source_target_pairs={{0,2},{1,3},{2,0},{3,1},{4,6},{5,7},{6,4},{7,5},{8,10},{9,11},{10,... | collective-permute-start | bytes 786440 | tf_op jit(solution)/shard_map/ppermute | solution.py:21
  218.4 11.8 %collective-permute-start.27 = (bf16[128,1024]{0,1:T(8,128)(2,1)S(1)}, bf16[128,1024]{0,1:T(8,128)(2,1)S(1)}, u32[]{:S(2)}, u32[]{:S(2)}) collective-permute-start(bf16[128,1024]{0,1:T(8,128)(2,1)S(1)} %get-tuple-element.93), channel_id=1, source_target_pairs={{0,1},{1,0},{2,3},{3,2},{4,5},{5,4},{6,7},{7,6},{8,9},{9,8},{10,11... | collective-permute-start | bytes 786440 | tf_op jit(solution)/shard_map/ppermute | solution.py:21
  232.8 3.9 collective-permute-start.30
  239.1 112.8 %reduce-scatter.19.cloned.1.call-start = ((), (), s32[]{:S(2)}) async-start(), calls=%async_computation.19 | async-start | bytes 557056
  242.0 10.2 %collective-permute-start.33 = (bf16[128,1024]{0,1:T(8,128)(2,1)S(1)}, bf16[128,1024]{0,1:T(8,128)(2,1)S(1)}, u32[]{:S(2)}, u32[]{:S(2)}) collective-permute-start(bf16[128,1024]{0,1:T(8,128)(2,1)S(1)} %get-tuple-element.72), channel_id=1, source_target_pairs={{0,3},{1,2},{2,1},{3,0},{4,7},{5,6},{6,5},{7,4},{8,11},{9,10},{10,... | collective-permute-start | bytes 786440 | tf_op jit(solution)/shard_map/ppermute | solution.py:21
  243.4 13.5 %collective-permute-start.32 = (bf16[128,1024]{0,1:T(8,128)(2,1)S(1)}, bf16[128,1024]{0,1:T(8,128)(2,1)S(1)}, u32[]{:S(2)}, u32[]{:S(2)}) collective-permute-start(bf16[128,1024]{0,1:T(8,128)(2,1)S(1)} %get-tuple-element.73), channel_id=1, source_target_pairs={{0,2},{1,3},{2,0},{3,1},{4,6},{5,7},{6,4},{7,5},{8,10},{9,11},{10,... | collective-permute-start | bytes 786440 | tf_op jit(solution)/shard_map/ppermute | solution.py:21
  245.0 12.0 %collective-permute-start.31 = (bf16[128,1024]{0,1:T(8,128)(2,1)S(1)}, bf16[128,1024]{0,1:T(8,128)(2,1)S(1)}, u32[]{:S(2)}, u32[]{:S(2)}) collective-permute-start(bf16[128,1024]{0,1:T(8,128)(2,1)S(1)} %get-tuple-element.71), channel_id=1, source_target_pairs={{0,1},{1,0},{2,3},{3,2},{4,5},{5,4},{6,7},{7,6},{8,9},{9,8},{10,11... | collective-permute-start | bytes 786440 | tf_op jit(solution)/shard_map/ppermute | solution.py:21
  252.1 14.8 %copy-start.3 = (bf16[128,1024]{0,1:T(8,128)(2,1)}, bf16[128,1024]{0,1:T(8,128)(2,1)S(1)}, u32[]{:S(2)}) copy-start(bf16[128,1024]{0,1:T(8,128)(2,1)S(1)} %collective-permute-done.33) | copy-start | bytes 786436
  259.2 113.6 %reduce-scatter.13.cloned.1.call-start = ((), (), s32[]{:S(2)}) async-start(), calls=%async_computation.15 | async-start | bytes 655360 | tf_op jit(solution)/shard_map/reduce_scatter | solution.py:81
  261.8 167.8 %reduce-scatter.15.cloned.1.call-start = ((), (), s32[]{:S(2)}) async-start(), calls=%async_computation.16 | async-start | bytes 3604480 | tf_op jit(solution)/shard_map/reduce_scatter | solution.py:81
  267.0 198.8 %reduce-scatter.17.cloned.1.call-start = ((), (), s32[]{:S(2)}) async-start(), calls=%async_computation.17 | async-start | bytes 1802240 | tf_op jit(solution)/shard_map/reduce_scatter | solution.py:81
  271.4 222.7 %reduce-scatter.9.cloned.1.call-start = ((), (), s32[]{:S(2)}) async-start(), calls=%async_computation.13 | async-start | bytes 1310720 | tf_op jit(solution)/shard_map/reduce_scatter | solution.py:81
  273.8 1.4 collective-permute-start.34
  276.2 7.3 %collective-permute-start.37 = (bf16[128,512]{0,1:T(8,128)(2,1)S(1)}, bf16[128,512]{0,1:T(8,128)(2,1)S(1)}, u32[]{:S(2)}, u32[]{:S(2)}) collective-permute-start(bf16[128,512]{0,1:T(8,128)(2,1)S(1)} %fusion.24), channel_id=1, source_target_pairs={{0,3},{1,2},{2,1},{3,0},{4,7},{5,6},{6,5},{7,4},{8,11},{9,10},{10,... | collective-permute-start | bytes 393224 | tf_op jit(solution)/shard_map/ppermute | solution.py:21
  277.6 7.8 %collective-permute-start.36 = (bf16[128,512]{0,1:T(8,128)(2,1)S(1)}, bf16[128,512]{0,1:T(8,128)(2,1)S(1)}, u32[]{:S(2)}, u32[]{:S(2)}) collective-permute-start(bf16[128,512]{0,1:T(8,128)(2,1)S(1)} %fusion.24), channel_id=1, source_target_pairs={{0,2},{1,3},{2,0},{3,1},{4,6},{5,7},{6,4},{7,5},{8,10},{9,11},{10,... | collective-permute-start | bytes 393224 | tf_op jit(solution)/shard_map/ppermute | solution.py:21
  279.1 7.2 %collective-permute-start.35 = (bf16[128,512]{0,1:T(8,128)(2,1)S(1)}, bf16[128,512]{0,1:T(8,128)(2,1)S(1)}, u32[]{:S(2)}, u32[]{:S(2)}) collective-permute-start(bf16[128,512]{0,1:T(8,128)(2,1)S(1)} %fusion.24), channel_id=1, source_target_pairs={{0,1},{1,0},{2,3},{3,2},{4,5},{5,4},{6,7},{7,6},{8,9},{9,8},{10,11... | collective-permute-start | bytes 393224 | tf_op jit(solution)/shard_map/ppermute | solution.py:21
  288.3 2.0 collective-permute-start.38
  290.6 8.1 %collective-permute-start.41 = (bf16[64,4,256]{2,1,0:T(4,128)(2,1)S(1)}, bf16[64,4,256]{2,1,0:T(4,128)(2,1)S(1)}, u32[]{:S(2)}, u32[]{:S(2)}) collective-permute-start(bf16[64,4,256]{2,1,0:T(4,128)(2,1)S(1)} %squeeze.54), channel_id=1, source_target_pairs={{0,3},{1,2},{2,1},{3,0},{4,7},{5,6},{6,5},{7,4},{8,11},{9,10},{10,... | collective-permute-start | bytes 393224 | tf_op jit(solution)/shard_map/ppermute | solution.py:21
  292.2 8.3 %collective-permute-start.40 = (bf16[64,4,256]{2,1,0:T(4,128)(2,1)S(1)}, bf16[64,4,256]{2,1,0:T(4,128)(2,1)S(1)}, u32[]{:S(2)}, u32[]{:S(2)}) collective-permute-start(bf16[64,4,256]{2,1,0:T(4,128)(2,1)S(1)} %squeeze.53), channel_id=1, source_target_pairs={{0,2},{1,3},{2,0},{3,1},{4,6},{5,7},{6,4},{7,5},{8,10},{9,11},{10,... | collective-permute-start | bytes 393224 | tf_op jit(solution)/shard_map/ppermute | solution.py:21
  293.3 7.2 %collective-permute-start.39 = (bf16[64,4,256]{2,1,0:T(4,128)(2,1)S(1)}, bf16[64,4,256]{2,1,0:T(4,128)(2,1)S(1)}, u32[]{:S(2)}, u32[]{:S(2)}) collective-permute-start(bf16[64,4,256]{2,1,0:T(4,128)(2,1)S(1)} %squeeze.52), channel_id=1, source_target_pairs={{0,1},{1,0},{2,3},{3,2},{4,5},{5,4},{6,7},{7,6},{8,9},{9,8},{10,11... | collective-permute-start | bytes 393224 | tf_op jit(solution)/shard_map/ppermute | solution.py:21
  302.1 131.4 %collective-permute-start.42 = (bf16[64,4096]{1,0:T(8,128)(2,1)S(1)}, bf16[64,4096]{1,0:T(8,128)(2,1)S(1)}, u32[]{:S(2)}, u32[]{:S(2)}) collective-permute-start(bf16[64,4096]{1,0:T(8,128)(2,1)S(1)} %reshape.180), channel_id=1, source_target_pairs={{0,16},{16,0},{1,17},{17,1},{2,18},{18,2},{3,19},{19,3},{4,20},{20... | collective-permute-start | bytes 1572872 | tf_op jit(solution)/shard_map/ppermute | solution.py:35
  304.3 70.2 %all-to-all-start.2 = ((bf16[4,64,768]{2,1,0:T(8,128)(2,1)}), bf16[4,64,768]{2,1,0:T(8,128)(2,1)S(1)}, u32[]{:S(2)}, u32[]{:S(2)}) async-start(bf16[4,64,768]{2,1,0:T(8,128)(2,1)} %bitcast.139), calls=%async_computation.4 | async-start | bytes 786432 | tf_op jit(solution)/shard_map/all_to_all | solution.py:57
  429.7 72.5 %all-to-all-start.3 = ((bf16[4,64,1408]{2,1,0:T(8,128)(2,1)}), bf16[4,64,1408]{2,1,0:T(8,128)(2,1)S(1)}, u32[]{:S(2)}, u32[]{:S(2)}) async-start(bf16[4,64,1408]{2,1,0:T(8,128)(2,1)} %bitcast.129), calls=%async_computation.7 | async-start | bytes 1441792 | tf_op jit(solution)/shard_map/all_to_all | solution.py:57
  (30 other events, 152.9 us)
Sparse Core Ops, SparseCore 0:
  9.6 32.8 all-gather.8
  44.1 35.5 all-gather.10
  81.2 66.2 all-gather.12
  149.0 33.8 all-gather.14
  239.2 34.1 reduce-scatter.10
  276.1 75.7 reduce-scatter.18
  354.8 17.9 reduce-scatter.12
  375.2 54.3 reduce-scatter.14
  432.7 33.0 reduce-scatter.16
  468.1 26.0 reduce-scatter.8

commit v2 on v1

v2 whole, which is shorter than its diff:
```python
import jax
import jax.numpy as jnp
from jax import lax
from jax.experimental import pallas as pl
from jax.experimental.pallas import tpu as pltpu
from jax.sharding import Mesh
from jax.sharding import PartitionSpec as P

HD = 64
F32 = jnp.float32
BF = jnp.bfloat16


def dot(form, a, b):
    return jnp.einsum(form, a, b, preferred_element_type=F32)


def peers(r):
    return [(i, i ^ r) for i in range(4)]


def hop(x, r):
    return lax.ppermute(x, "t", peers(r))


def spread(x):
    a, b = hop(x, 1), hop(x, 2)
    return [x, a, b, hop(b, 1)]


def zhop(x, r):
    return lax.ppermute(x, "d1", peers(r))


def gather_z(w):
    a, b = zhop(w, 1), zhop(w, 3)
    return [w, a, zhop(b, 1), b]


def scatter_z(g):
    g = [x.astype(BF) for x in g]
    far = (g[3].astype(F32) + zhop(g[2], 1).astype(F32)).astype(BF)
    return g[0].astype(F32) + zhop(g[1], 1).astype(F32) + zhop(far, 3).astype(F32)


def total(parts):
    return sum(p.astype(F32) for p in parts)


def turn(x, d, axis):
    n = x.shape[axis] // 4
    return [lax.dynamic_slice_in_dim(x, (d ^ r) * n, n, axis) for r in range(4)]


def collect(x):
    b = x.shape[0] // 4
    low = [x[r * b : (r + 1) * b].astype(BF) for r in range(4)]
    return low[0].astype(F32) + sum(hop(low[r], r).astype(F32) for r in (3, 2, 1))


def swap(x):
    return lax.ppermute(x, "stream", [(0, 1), (1, 0)])


def norm_parts(v):
    scale = lax.rsqrt(jnp.mean(v * v, axis=-1, keepdims=True) + 1e-05)
    return v * scale, scale


def norm_back(unit, scale, g):
    return scale * (g - unit * jnp.mean(g * unit, axis=-1, keepdims=True))


def quarters(x, axis=0):
    n = x.shape[axis] // 4
    return [lax.slice_in_dim(x, r * n, (r + 1) * n, axis=axis) for r in range(4)]


def tie(x, *after):
    return lax.optimization_barrier((x,) + after)[0]


def call(body, outs, *args, scalars=None):
    inside = [pl.BlockSpec(memory_space=pltpu.VMEM)] * len(args)
    if scalars is not None:
        inside = [pl.BlockSpec(memory_space=pltpu.SMEM)] + inside
        args = (scalars,) + args
    single = not isinstance(outs, list)
    shapes = [jax.ShapeDtypeStruct(*o) for o in ([outs] if single else outs)]
    got = pl.pallas_call(
        body,
        out_shape=shapes,
        in_specs=inside,
        out_specs=[pl.BlockSpec(memory_space=pltpu.VMEM)] * len(shapes),
        compiler_params=pltpu.CompilerParams(vmem_limit_bytes=48 << 20),
    )(*args)
    return got[0] if single else got


def join(blocks, d=None):
    n, c = blocks[0].shape

    def body(*refs):
        shift = 0 if d is None else refs[0][0]
        ins = refs if d is None else refs[1:]
        for r in range(4):
            row = r * n if d is None else pl.multiple_of((shift ^ r) * n, 16)
            ins[4][pl.ds(row, n)] = ins[r][...]

    scalars = None if d is None else d.astype(jnp.int32)[None]
    return call(body, ((4 * n, c), blocks[0].dtype), *blocks, scalars=scalars)


def beside(blocks, rows):
    c = blocks[0].shape[1]

    def body(*refs):
        for r in range(4):
            refs[4][:, r * c : (r + 1) * c] = refs[r][:rows]

    return call(body, ((rows, 4 * c), blocks[0].dtype), *blocks)


def pack_columns(w, k):
    rows = w.shape[0]
    c = w.shape[1] // (k * 16)

    def body(w_ref, o_ref):
        x = w_ref[...]
        for t in range(4):
            o_ref[t] = jnp.concatenate(
                [x[:, (i * 4 + t) * c : (i * 4 + t + 1) * c] for i in range(k * 4)], axis=1
            )

    return call(body, ((4, rows, k * 4 * c), w.dtype), w)


def unpack_columns(g, k):
    rows = g.shape[1]
    c = g.shape[2] // (k * 4)

    def body(g_ref, o_ref):
        x = [g_ref[t].astype(F32) for t in range(4)]
        o_ref[...] = jnp.concatenate(
            [x[t][:, i * c : (i + 1) * c] for i in range(k * 4) for t in range(4)], axis=1
        )

    return call(body, ((rows, k * 16 * c), F32), g)


def pack_context(context, scalars):
    half = context.shape[0] // 2
    c = context.shape[1] // 16

    def body(n_ref, x_ref, *o_refs):
        s, t, d = n_ref[0], n_ref[1], n_ref[2]
        for r in range(4):
            for q in range(4):
                col = pl.multiple_of(((d ^ q) * 4 + (t ^ r)) * c, c)
                row = pl.multiple_of(s * half, half)
                o_refs[r][:, q * c : (q + 1) * c] = x_ref[pl.ds(row, half), pl.ds(col, c)]

    return call(body, [((half, 4 * c), context.dtype)] * 4, context, scalars=scalars)


def unpack_context(own, other, scalars):
    half = own.shape[1]
    c = own.shape[2] // 4

    def body(n_ref, a_ref, b_ref, o_ref):
        s, t, d = n_ref[0], n_ref[1], n_ref[2]
        for ref, place in ((a_ref, s), (b_ref, 1 - s)):
            row = pl.multiple_of(place * half, half)
            for r in range(4):
                for q in range(4):
                    col = pl.multiple_of(((d ^ q) * 4 + (t ^ r)) * c, c)
                    o_ref[pl.ds(row, half), pl.ds(col, c)] = ref[
                        r, :, q * c : (q + 1) * c
                    ].astype(F32)

    return call(body, ((2 * half, 16 * c), F32), own, other, scalars=scalars)


def on_device(
    tokens, context, w_in, attn_gain, w_qkv, w_out, ffn_gain, w_gate_up, w_down, cotangent
):
    s = lax.axis_index("stream")
    t = lax.axis_index("t")
    d = lax.axis_index("d1")
    many = lax.axis_size("d2") > 1
    frames = tokens.shape[0]
    wide = tokens.shape[2]
    half = frames // 2

    def near(w, axis=0):
        return lax.all_gather(w, "d2", axis=axis, tiled=True) if many else w

    def near_sum(g, axis=0):
        return lax.psum_scatter(g, "d2", scatter_dimension=axis, tiled=True) if many else g

    scalars = jnp.stack([s, t, d]).astype(jnp.int32)

    def over_d(w):
        return lax.all_gather(w, "d1", axis=0, tiled=True)

    def sum_d(g):
        return lax.psum_scatter(g.astype(BF), "d1", scatter_dimension=0, tiled=True).astype(F32)

    tokens = tokens[:, 0]
    cotangent = cotangent[:, 0]
    every = ("d1", "t", "d2")

    each = attn_gain.shape[1]
    gains = jnp.concatenate(
        [
            lax.all_gather(g[0], "d2", axis=0, tiled=True) if many else g[0]
            for g in (attn_gain, ffn_gain)
        ]
    )
    some = gains.shape[0]
    in_mine = near(w_in, 1)
    in_mine = jnp.concatenate(
        [in_mine, jnp.pad(gains[None], ((0, 15), (0, in_mine.shape[1] - some)))]
    )
    in_one, in_three = zhop(in_mine, 1), zhop(in_mine, 3)
    parts = pack_context(context, scalars)
    feats = parts[0].shape[1]
    got = {r: hop(parts[r], r) for r in (3, 2, 1)}
    packed = pack_columns(tie(near(w_qkv[0]), parts[0]), 3)
    qkv_mine = lax.all_to_all(packed, "t", 0, 0, tiled=True).reshape(-1, packed.shape[2])
    packed = pack_columns(tie(near(w_gate_up[0]), qkv_mine), 2)
    gu_mine = lax.all_to_all(packed, "t", 0, 0, tiled=True).reshape(-1, packed.shape[2])
    own = tie(jnp.stack([parts[0], got[1], got[2], got[3]]), qkv_mine)
    other = swap(own)
    in_two = zhop(tie(in_three, own), 1)
    qkv_one, qkv_three = zhop(qkv_mine, 1), zhop(qkv_mine, 3)
    group = jnp.where(
        s == 0, jnp.concatenate([own, other], axis=1), jnp.concatenate([other, own], axis=1)
    ).reshape(4 * frames, feats)
    in_w = beside([in_mine, in_one, in_two, in_three], near(w_in, 1).shape[0])
    partial = dot("fc,dc->fd", group, in_w).astype(BF)

    gains = jnp.concatenate([w[-16:, :some] for w in (in_mine, in_one, in_two, in_three)], axis=1)
    size = partial.shape[0] // 4
    parts = [jnp.concatenate([partial[r * size : (r + 1) * size], gains]) for r in range(4)]
    parts = [parts[0]] + [hop(parts[r], r) for r in (3, 2, 1)]
    proj_half = total([w[:size] for w in parts]).astype(BF)
    proj_half = tie(proj_half, gu_mine, qkv_one, qkv_three)
    qkv_two = zhop(tie(qkv_three, proj_half), 1)
    out_mine = tie(near(w_out[0]), proj_half)
    out_one, out_three = zhop(out_mine, 1), zhop(out_mine, 3)
    gains = jnp.stack([parts[i][size].astype(F32) for i in (0, 3, 2, 1)])
    gains = jnp.stack([lax.dynamic_index_in_dim(gains, t ^ r, 0, keepdims=False) for r in range(4)])
    gains = gains.reshape(4, 4, 2, some // 2).transpose(2, 1, 0, 3).reshape(2, wide)
    gain_one, gain_two = (jnp.concatenate(turn(gains[i], d, 0)) for i in (0, 1))
    proj_other = swap(proj_half)
    projected = jnp.where(
        s == 0,
        jnp.concatenate([proj_half, proj_other], axis=1),
        jnp.concatenate([proj_other, proj_half], axis=1),
    )
    start = tokens.astype(F32) + projected.astype(F32)
    unit_one, scale_one = norm_parts(start)
    mine = jnp.concatenate(turn((unit_one * gain_one).astype(BF), d, 1), axis=1)
    by_x, by_y = hop(mine, 1), hop(mine, 2)
    by_xy = hop(tie(by_y, qkv_two), 1)
    gu_mine = tie(gu_mine, mine)
    gu_one, gu_three = zhop(gu_mine, 1), zhop(gu_mine, 3)
    normed_one = tie(join([mine, by_x, by_y, by_xy]), out_one, out_three)
    out_two = zhop(out_three, 1)
    qkv_w = join([qkv_mine, qkv_one, qkv_two, qkv_three])
    out_w = join([out_mine, out_one, out_two, out_three], d)
    qkv = dot("fd,de->fe", normed_one, qkv_w).astype(BF)
    width = qkv.shape[1] // 3
    far = lax.ppermute(qkv[:, width:], "stream", [(0, 1)])
    far = far.astype(F32)
    q, k, v = (qkv[:, i * width : (i + 1) * width].astype(F32) for i in range(3))
    lane = jnp.arange(width) // HD
    heads = (lane[:, None] == lane[None, :]).astype(F32)

    def head_sum(x):
        return jnp.dot(x, heads, precision=lax.Precision.HIGHEST)

    dk = k - far[:, :width]
    dv = v - far[:, width:]
    w_own = jnp.where(s == 0, 1.0, jax.nn.sigmoid(head_sum(q * dk) * HD ** (-0.5)))
    w_far = 1.0 - w_own
    mixed = (w_own * v + w_far * far[:, width:]).astype(BF)
    mixed = tie(mixed, gu_one)
    partial = dot("fd,de->fe", mixed, out_w).astype(BF)
    cot = lax.all_to_all(
        jnp.broadcast_to(tie(cotangent, partial)[None], (4, frames, wide)), "t", 0, 0, tiled=True
    )
    down_mine = near(w_down[0])
    down_one = zhop(tie(down_mine, normed_one), 1)
    middle = start + tie(collect(partial), gu_three, down_one)

    unit_two, scale_two = norm_parts(middle)
    mine = jnp.concatenate(turn((unit_two * gain_two).astype(BF), d, 1), axis=1)
    by_x, by_y = hop(mine, 1), hop(mine, 2)
    gu_two = zhop(gu_three, 1)
    by_xy = hop(by_y, 1)
    down_three = zhop(tie(down_mine, middle), 3)
    normed_two = tie(join([mine, by_x, by_y, by_xy]), down_three)
    gu_w = join([gu_mine, gu_one, gu_two, gu_three])
    cot = jnp.concatenate(turn(cot.reshape(4 * frames, wide), t, 0))
    gate_up = dot("fd,de->fe", normed_two, gu_w)
    down_two = zhop(down_three, 1)
    down_w = join([down_mine, down_one, down_two, down_three], d)
    ff = gate_up.shape[1] // 2
    gate, up = gate_up[:, :ff], gate_up[:, ff:]
    sig = jax.nn.sigmoid(gate)
    hidden = (gate * sig * up).astype(BF)
    g = turn(dot("fk,fd->kd", hidden, cot).astype(BF), d, 0)
    down_back_two, down_back_one = zhop(g[2], 1), zhop(g[1], 1)
    grad_hidden = dot("fd,kd->fk", tie(cot, g[0]), down_w)
    grad_gu = jnp.concatenate(
        [grad_hidden * up * sig * (1.0 + gate * (1.0 - sig)), grad_hidden * gate * sig], axis=-1
    ).astype(BF)
    partial = dot("fe,de->fd", grad_gu, gu_w).astype(BF)
    grad_normed_two = jnp.concatenate(turn(tie(collect(partial), down_back_two), d, 1), axis=1)
    u = quarters(dot("fd,fe->de", normed_two, tie(grad_gu, partial)).astype(BF))
    gu_two = zhop(u[2], 1)
    far_sum = (g[3].astype(F32) + tie(down_back_two, grad_normed_two).astype(F32)).astype(BF)
    down_three = zhop(far_sum, 3)
    grad_gain_two = jnp.sum(grad_normed_two * unit_two, axis=0)
    grad_middle = cotangent.astype(F32) + norm_back(
        unit_two, scale_two, grad_normed_two * gain_two
    )
    mine = tie(grad_middle.astype(BF), far_sum)
    by_x, by_y = hop(mine, 1), hop(mine, 2)
    gu_one = zhop(tie(u[1], mine), 1)
    by_xy = hop(by_y, 1)
    branch = tie(join([mine, by_x, by_y, by_xy]), gu_two)
    grad_down = near_sum(
        g[0].astype(F32) + down_back_one.astype(F32) + tie(down_three, branch).astype(F32)
    )

    gm = dot("fe,de->fd", branch, out_w)
    gs = w_own * w_far * head_sum(gm * dv) * HD ** (-0.5)
    gq = gs * dk
    gk = gs * q
    back = lax.ppermute(
        jnp.concatenate([-gk, w_far * gm], axis=1).astype(BF), "stream", [(1, 0)]
    ).astype(F32)
    grad_kv = jnp.concatenate([gk, w_own * gm], axis=1) + back
    far_sum = (u[3].astype(F32) + tie(gu_two, branch).astype(F32)).astype(BF)
    gu_three = zhop(far_sum, 3)
    grad_qkv_low = jnp.concatenate([gq, grad_kv], axis=1).astype(BF)
    grad_qkv_low = tie(grad_qkv_low, far_sum, gu_one)
    partial = dot("fe,de->fd", grad_qkv_low, qkv_w).astype(BF)
    grad_normed_one = jnp.concatenate(turn(collect(partial), d, 1), axis=1)
    g = quarters(dot("fd,fe->de", normed_one, tie(grad_qkv_low, partial)).astype(BF))
    h = turn(dot("fd,fe->de", tie(mixed, g[0]), branch).astype(BF), d, 0)
    grad_gain_one = jnp.sum(grad_normed_one * unit_one, axis=0)
    grad_start = grad_middle + norm_back(unit_one, scale_one, grad_normed_one * gain_one)
    halves = grad_start.astype(BF).reshape(frames, 2, wide // 2)
    keep = lax.dynamic_index_in_dim(halves, s, 1, keepdims=False)
    give = lax.dynamic_index_in_dim(halves, 1 - s, 1, keepdims=False)
    grad_proj = (keep.astype(F32) + swap(give).astype(F32)).astype(BF)
    by_x, by_y = hop(grad_proj, 1), hop(grad_proj, 2)
    qkv_back_two = zhop(g[2], 1)
    qkv_back_one = zhop(tie(g[1], grad_proj), 1)
    by_xy = hop(by_y, 1)
    gproj = join([grad_proj, by_x, by_y, by_xy])
    gu_sum = u[0].astype(F32) + gu_one.astype(F32) + tie(gu_three, gproj).astype(F32)
    far_sum = (g[3].astype(F32) + tie(qkv_back_two, gproj).astype(F32)).astype(BF)
    qkv_back_three = zhop(far_sum, 3)
    result = middle + collect(dot("fk,kd->fd", tie(hidden, gproj), down_w).astype(BF))
    out_back_two, out_back_one = zhop(tie(h[2], result), 1), zhop(tie(h[1], result), 1)

    term = dot("fd,dc->fc", gproj, in_w).astype(BF).reshape(4, 2, half, feats)
    keep = lax.dynamic_index_in_dim(term, s, 1, keepdims=False)
    give = lax.dynamic_index_in_dim(term, 1 - s, 1, keepdims=False)
    both = (keep.astype(F32) + swap(give).astype(F32)).astype(BF)
    g_in = quarters(dot("fd,fc->dc", gproj, tie(group, give)).astype(BF), 1)
    got = {r: hop(both[r], r) for r in (3, 2, 1)}
    in_back_two = zhop(tie(g_in[2], both), 1)
    grad_qkv = g[0].astype(F32) + qkv_back_one.astype(F32) + qkv_back_three.astype(F32)
    gu_back = lax.all_to_all(
        tie(gu_sum.astype(BF), both).reshape(4, -1, gu_sum.shape[1]), "t", 0, 0, tiled=True
    )
    qkv_back = lax.all_to_all(
        tie(grad_qkv.astype(BF), gu_back).reshape(4, -1, grad_qkv.shape[1]), "t", 0, 0, tiled=True
    )
    far_sum = (h[3].astype(F32) + out_back_two.astype(F32)).astype(BF)
    out_back_three = zhop(far_sum, 3)
    grad_out = near_sum(
        h[0].astype(F32) + out_back_one.astype(F32) + out_back_three.astype(F32)
    )
    got = jnp.stack([both[0], got[1], got[2], got[3]])
    far_sum = (g_in[3].astype(F32) + tie(in_back_two, got).astype(F32)).astype(BF)
    in_back_three, in_back_one = zhop(far_sum, 3), zhop(tie(g_in[1], got), 1)
    grad_context = unpack_context(got, swap(got), scalars)
    grad_gate_up = near_sum(unpack_columns(gu_back, 2))
    grad_qkv = near_sum(unpack_columns(qkv_back, 3))
    grad_in = near_sum(
        g_in[0].astype(F32) + in_back_one.astype(F32) + in_back_three.astype(F32), 1
    )
    gains = jnp.stack([grad_gain_one, grad_gain_two]).reshape(2, -1, each).transpose(1, 0, 2)
    gains = jnp.sum(lax.all_to_all(tie(gains, both), every, 0, 0, tiled=True), axis=0)
    return (
        result[:, None],
        grad_start[:, None],
        grad_context,
        grad_in,
        gains[:1],
        grad_qkv[None],
        grad_out[None],
        gains[1:],
        grad_gate_up[None],
        grad_down[None],
    )


def solution(mesh):
    n = mesh.shape["frames"]
    grid = Mesh(mesh.devices.reshape(2, 4, 4, n // 16), ("stream", "d1", "t", "d2"))
    f = ("d1", "t", "d2")
    return jax.shard_map(
        on_device,
        mesh=grid,
        in_specs=(
            P(f, "stream", None),
            P(f, None),
            P("stream", f),
            P("stream", f),
            P("stream", f, None),
            P("stream", f, None),
            P("stream", f),
            P("stream", f, None),
            P("stream", f, None),
            P(f, "stream", None),
        ),
        out_specs=(
            P(f, "stream", None),
            P(f, "stream", None),
            P(f, None),
            P("stream", f),
            P("stream", f),
            P("stream", f, None),
            P("stream", f, None),
            P("stream", f),
            P("stream", f, None),
            P("stream", f, None),
        ),
        check_vma=False,
    )
```

time: 526 us -> 327 us (0.62)
  waiting for transfers between devices: 267 us -> 114 us
  blocking collectives: 86.7 us -> 0 us
  starting transfers between devices: 54.1 us -> 117 us
  matrix products: 40.9 us -> 22 us
  other arithmetic: 13.9 us -> 28.1 us
  between operations: 16 us -> 1.94 us
  Pallas kernels: 0 us -> 10.4 us
  local copies, waits for them, and re-layouts: 41.4 us -> 31.4 us
    reduce_scatter x5 -> x0, waiting for transfers between devices: 131 us -> none  [sum_d(): lax.psum_scatter(g.astype(BF), 'd1', scatter_dimension=axis, tiled=True)]
    ppermute x1 -> x31, waiting for transfers between devices: 0.01 us -> 77.2 us  [the longest x30 77.2 us: zhop(): return lax.ppermute(x, 'd1', peers(r))]
    ppermute x36 -> x33, waiting for transfers between devices: 81.1 us -> 32 us  [hop(): return lax.ppermute(x, 't', peers(r))]
    unnamed x11 -> x0, waiting for transfers between devices: 45 us -> none
    ppermute x1 -> x31, starting transfers between devices: 1.32 us -> 45.9 us  [the longest x30 44.6 us: zhop(): return lax.ppermute(x, 'd1', peers(r))]
    unnamed x1 -> x0, blocking collectives: 42.1 us -> none
    all_to_all x2 -> x0, blocking collectives: 24.8 us -> none  [columns_to_t(): return lax.all_to_all(w, 't', 0, 0, tiled=True).reshape(4 * rows, k * 4 * c)]
    all_to_all x2 -> x6, starting transfers between devices: 7.34 us -> 28.5 us  [the longest x1 8.64 us: on_device(): lax.all_to_all(tie(gains, both), every, 0, 0, tiled=True)]
  transfers between devices with their start and end apart: 55 -> 76, of which waited for: 36 -> 29; matrix products, arithmetic and copies ran while one was open for 13% -> 20% of each run, Pallas kernels for 0% -> 3%
where the time goes in v2:
time: 327 us; the launch traced here: 325 us
  starting transfers between devices  117 us (36%)
  waiting for transfers between devices  114 us (35%)
  local copies, waits for them, and re-layouts  31.4 us (10%)
  other arithmetic  28.1 us (9%)
  matrix products  22 us (7%)
  Pallas kernels  10.4 us (3%)
    ppermute x30, waiting for transfers between devices, zhop(): return lax.ppermute(x, 'd1', peers(r))  77.2 us
    ppermute x30, starting transfers between devices, zhop(): return lax.ppermute(x, 'd1', peers(r))  44.6 us
    ppermute x33, starting transfers between devices, hop(): return lax.ppermute(x, 't', peers(r))  40.4 us
    ppermute x33, waiting for transfers between devices, hop(): return lax.ppermute(x, 't', peers(r))  32 us
    dot_general x15, matrix products, dot(): return jnp.einsum(form, a, b, preferred_element_type=F32)  18.9 us
    unnamed x145, local copies, waits for them, and re-layouts  16.9 us
    pallas_call x15, Pallas kernels, call(): pl.pallas_call(body, out_shape=shapes, in_specs=inside, out_specs=[pl.Blo...  10.4 us
    all_to_all x1, starting transfers between devices, on_device(): lax.all_to_all(tie(gains, both), every, 0, 0, tiled=True)  8.64 us
  transfers between devices with their start and end apart: 76, of which 29 were waited for; matrix products, arithmetic and copies ran while one was open for 20% of the time, Pallas kernels for 3%

profile of v2, /device:TPU:0, one launch (start us, length us, event | category | flops | bytes accessed | tf_op | source)
XLA Modules:
  0.0 324.5 jit_solution(3543005648657880234)
XLA Ops:
  2.6 4.0 %collective-permute-start.2 = (bf16[64,1024]{1,0:T(8,128)(2,1)S(1)}, bf16[64,1024]{1,0:T(8,128)(2,1)S(1)}, u32[]{:S(2)}, u32[]{:S(2)}) collective-permute-start(bf16[64,1024]{1,0:T(8,128)(2,1)S(1)} %get-tuple-element.58), channel_id=1, source_target_pairs={{0,3},{1,2},{2,1},{3,0},{4,7},{5,6},{6,5},{7,4},{8,11},{9,10},{10,... | collective-permute-start | bytes 393224 | tf_op jit(solution)/shard_map/ppermute | solution.py:23
  9.1 4.1 %all-to-all-start = ((bf16[4,64,768]{2,1,0:T(8,128)(2,1)}), bf16[4,64,768]{2,1,0:T(8,128)(2,1)S(1)}, u32[]{:S(2)}, u32[]{:S(2)}) async-start(bf16[4,64,768]{2,1,0:T(8,128)(2,1)} %shard_map.178), calls=%async_computation | async-start | bytes 786432 | tf_op jit(solution)/shard_map/all_to_all | solution.py:230
  13.3 3.7 %collective-permute-start.5 = (bf16[528,256]{1,0:T(8,128)(2,1)S(1)}, bf16[528,256]{1,0:T(8,128)(2,1)S(1)}, u32[]{:S(2)}, u32[]{:S(2)}) collective-permute-start(bf16[528,256]{1,0:T(8,128)(2,1)S(1)} %pad_maximum_fusion.8.refs_0_), channel_id=1, source_target_pairs={{0,12},{4,8},{8,4},{12,0},{1,13},{5,9},{9,5},{13,1},{2,14},{6,10},... | collective-permute-start | bytes 811016 | tf_op jit(solution)/shard_map/ppermute | solution.py:32
  17.1 2.0 all-to-all-done
  19.1 1.6 collective-permute-start.4
  20.7 1.9 collective-permute-done.5.refs_3_
  22.6 5.4 %collective-permute-start.6 = (bf16[528,256]{1,0:T(8,128)(2,1)S(1)}, bf16[528,256]{1,0:T(8,128)(2,1)S(1)}, u32[]{:S(2)}, u32[]{:S(2)}) collective-permute-start(bf16[528,256]{1,0:T(8,128)(2,1)S(1)} %collective-permute-done.5.refs_3_), channel_id=1, source_target_pairs={{0,4},{4,0},{8,12},{12,8},{1,5},{5,1},{9,13},{13,9},{2,6},{6,2},{1... | collective-permute-start | bytes 811016 | tf_op jit(solution)/shard_map/ppermute | solution.py:32
  28.5 5.6 %collective-permute-done.6.refs_2_ = bf16[528,256]{1,0:T(8,128)(2,1)S(1)} collective-permute-done((bf16[528,256]{1,0:T(8,128)(2,1)S(1)}, bf16[528,256]{1,0:T(8,128)(2,1)S(1)}, u32[]{:S(2)}, u32[]{:S(2)}) %collective-permute-start.6) | collective-permute-done | bytes 270368 | tf_op jit(solution)/shard_map/ppermute | solution.py:32
  35.8 2.7 collective-permute-start.7
  39.4 1.7 collective-permute-start.10
  41.1 2.1 collective-permute-start.11
  44.3 3.7 %all-to-all-start.1 = ((bf16[4,64,1408]{2,1,0:T(8,128)(2,1)}), bf16[4,64,1408]{2,1,0:T(8,128)(2,1)S(1)}, u32[]{:S(2)}, u32[]{:S(2)}) async-start(bf16[4,64,1408]{2,1,0:T(8,128)(2,1)} %shard_map.180), calls=%async_computation.1 | async-start | bytes 1441792 | tf_op jit(solution)/shard_map/all_to_all | solution.py:232
  51.6 8.3 %collective-permute-done.11.refs_3_ = bf16[256,768]{1,0:T(8,128)(2,1)S(1)} collective-permute-done((bf16[256,768]{1,0:T(8,128)(2,1)S(1)}, bf16[256,768]{1,0:T(8,128)(2,1)S(1)}, u32[]{:S(2)}, u32[]{:S(2)}) %collective-permute-start.11) | collective-permute-done | bytes 393248 | tf_op jit(solution)/shard_map/ppermute | solution.py:32
  62.2 1.7 collective-permute-start.14
  65.4 5.2 %collective-permute-done.14.refs_2_ = bf16[128,1024]{1,0:T(8,128)(2,1)S(1)} collective-permute-done((bf16[128,1024]{1,0:T(8,128)(2,1)S(1)}, bf16[128,1024]{1,0:T(8,128)(2,1)S(1)}, u32[]{:S(2)}, u32[]{:S(2)}) %collective-permute-start.14) | collective-permute-done | bytes 262176 | tf_op jit(solution)/shard_map/ppermute | solution.py:23
  71.4 1.7 collective-permute-start.16
  73.8 2.6 collective-permute-start.18
  76.6 2.7 collective-permute-done.16.refs_3_
  79.3 2.7 collective-permute-done.18.refs_4_
  84.5 2.0 collective-permute-start.21
  87.9 18.4 %collective-permute-done.21.refs_3_ = bf16[64,1024]{1,0:T(8,128)(2,1)S(1)} collective-permute-done((bf16[64,1024]{1,0:T(8,128)(2,1)S(1)}, bf16[64,1024]{1,0:T(8,128)(2,1)S(1)}, u32[]{:S(2)}, u32[]{:S(2)}) %collective-permute-start.21) | collective-permute-done | bytes 131104 | tf_op jit(solution)/shard_map/ppermute | solution.py:32
  108.9 1.8 collective-permute-start.23
  110.7 1.7 collective-permute-start.22
  112.4 9.9 %collective-permute-done.25.refs_3_ = bf16[256,1408]{1,0:T(8,128)(2,1)S(1)} collective-permute-done((bf16[256,1408]{1,0:T(8,128)(2,1)S(1)}, bf16[256,1408]{1,0:T(8,128)(2,1)S(1)}, u32[]{:S(2)}, u32[]{:S(2)}) %collective-permute-start.25) | collective-permute-done | bytes 720928 | tf_op jit(solution)/shard_map/ppermute | solution.py:32
  122.6 4.6 %collective-permute-done.26.refs_2_ = bf16[176,1024]{1,0:T(8,128)(2,1)S(1)} collective-permute-done((bf16[176,1024]{1,0:T(8,128)(2,1)}, bf16[176,1024]{1,0:T(8,128)(2,1)S(1)}, u32[]{:S(2)}, u32[]{:S(2)}) %collective-permute-start.26) | collective-permute-done | bytes 360480 | tf_op jit(solution)/shard_map/ppermute | solution.py:32
  130.5 2.5 collective-permute-start.30
  133.6 3.7 %collective-permute-done.28.refs_2_ = bf16[128,1024]{1,0:T(8,128)(2,1)} collective-permute-done((bf16[128,1024]{1,0:T(8,128)(2,1)}, bf16[128,1024]{1,0:T(8,128)(2,1)}, u32[]{:S(2)}, u32[]{:S(2)}) %collective-permute-start.28) | collective-permute-done | bytes 262176 | tf_op jit(solution)/shard_map/ppermute | solution.py:23
  139.1 4.4 %all-to-all-start.2 = ((bf16[4,128,1024]{2,1,0:T(8,128)(2,1)}), bf16[4,128,1024]{2,1,0:T(8,128)(2,1)}, u32[]{:S(2)}, u32[]{:S(2)}) async-start(bf16[4,128,1024]{2,1,0:T(8,128)(2,1)} %broadcast_in_dim.22), calls=%async_computation.2 | async-start | bytes 2097152 | tf_op jit(solution)/shard_map/all_to_all | solution.py:291
  143.6 1.9 collective-permute-done.31.refs_2_
  152.4 1.8 fusion.51
  154.2 1.6 copy-done.30
  160.8 2.0 collective-permute-start.36
  166.1 1.8 convolution_convert_fusion.5
  168.4 1.7 collective-permute-start.34
  171.6 1.8 convolution_convert_fusion
  177.3 4.9 %collective-permute-done.33 = bf16[128,1024]{1,0:T(8,128)(2,1)S(1)} collective-permute-done((bf16[128,1024]{1,0:T(8,128)(2,1)S(1)}, bf16[128,1024]{1,0:T(8,128)(2,1)S(1)}, u32[]{:S(2)}, u32[]{:S(2)}) %collective-permute-start.33) | collective-permute-done | bytes 262176 | tf_op jit(solution)/shard_map/ppermute | solution.py:23
  185.9 4.4 %collective-permute-done.38.refs_2_ = bf16[128,1024]{1,0:T(8,128)(2,1)S(1)} collective-permute-done((bf16[128,1024]{1,0:T(8,128)(2,1)S(1)}, bf16[128,1024]{1,0:T(8,128)(2,1)S(1)}, u32[]{:S(2)}, u32[]{:S(2)}) %collective-permute-start.38) | collective-permute-done | bytes 262176 | tf_op jit(solution)/shard_map/ppermute | solution.py:23
  194.3 2.4 collective-permute-done.39.refs_3_
  197.9 1.7 negate_convert_fusion
  199.7 1.6 collective-permute-start.41
  201.4 2.4 add_convert_fusion.1
  205.1 5.8 %collective-permute-done.69 = bf16[176,1024]{1,0:T(8,128)(2,1)} collective-permute-done((bf16[176,1024]{1,0:T(8,128)(2,1)}, bf16[176,1024]{1,0:T(8,128)(2,1)}, u32[]{:S(2)}, u32[]{:S(2)}) %collective-permute-start.69) | collective-permute-done | bytes 360480 | tf_op jit(solution)/shard_map/ppermute | solution.py:32
  212.4 13.1 %collective-permute-done.42 = bf16[256,1408]{1,0:T(8,128)(2,1)S(1)} collective-permute-done((bf16[256,1408]{1,0:T(8,128)(2,1)}, bf16[256,1408]{1,0:T(8,128)(2,1)S(1)}, u32[]{:S(2)}, u32[]{:S(2)}) %collective-permute-start.42) | collective-permute-done | bytes 720928 | tf_op jit(solution)/shard_map/ppermute | solution.py:32
  230.1 2.1 add_bitcast_fusion
  233.0 2.5 collective-permute-done.44
  239.6 3.3 %convolution_convert_fusion.1 = bf16[1024,768]{1,0:T(8,128)(2,1)} fusion(bf16[512,1024]{1,0:T(8,128)(2,1)S(1)} %copy-done.10, bf16[512,768]{1,0:T(8,128)(2,1)} %copy-done.50), kind=kOutput, calls=%fused_computation.1 | convolution fusion | flops 806092800 | bytes 3407872 | tf_op jit(solution)/shard_map/fd,fe->de/dot_general | solution.py:15
  243.1 1.6 collective-permute-start.48
  244.7 2.0 fusion.39
  253.8 1.6 collective-permute-start.61
  256.5 2.1 convolution_convert_fusion.4
  261.6 1.6 collective-permute-start.50
  265.7 2.5 add_convert_fusion
  269.8 2.7 collective-permute-done.50
  282.0 8.6 %all-to-all-start.3 = ((f32[16,1,128]{2,1,0:T(1,128)}), f32[16,1,128]{2,1,0:T(1,128)S(1)}, u32[]{:S(2)}, u32[]{:S(2)}) async-start(f32[16,1,128]{2,1,0:T(1,128)} %reshape.129), calls=%async_computation.3 | async-start | bytes 16384 | tf_op jit(solution)/shard_map/all_to_all | solution.py:401
  290.6 2.0 collective-permute-start.59
  293.3 2.4 collective-permute-start.67
  295.7 2.3 all-to-all-done.3
  297.9 3.5 %all-to-all-start.4 = ((bf16[4,64,1408]{2,1,0:T(8,128)(2,1)}), bf16[4,64,1408]{2,1,0:T(8,128)(2,1)S(1)}, u32[]{:S(2)}, u32[]{:S(2)}) async-start(bf16[4,64,1408]{2,1,0:T(8,128)(2,1)} %bitcast.36), calls=%async_computation.4 | async-start | bytes 1441792 | tf_op jit(solution)/shard_map/all_to_all | solution.py:380
  303.9 1.7 add_convert_fusion.5
  307.1 1.7 add_bitcast_fusion.1
  310.1 4.2 %all-to-all-start.5 = ((bf16[4,64,768]{2,1,0:T(8,128)(2,1)}), bf16[4,64,768]{2,1,0:T(8,128)(2,1)S(1)}, u32[]{:S(2)}, u32[]{:S(2)}) async-start(bf16[4,64,768]{2,1,0:T(8,128)(2,1)} %bitcast.37), calls=%async_computation.5 | async-start | bytes 786432 | tf_op jit(solution)/shard_map/all_to_all | solution.py:383
  314.8 3.2 collective-permute-done.60
  318.0 1.9 convert_add_fusion.2
  321.4 2.0 shard_map.189
  (360 shorter events, 105.7 us)
Async XLA Ops:
  2.6 14.4 %collective-permute-start.2 = (bf16[64,1024]{1,0:T(8,128)(2,1)S(1)}, bf16[64,1024]{1,0:T(8,128)(2,1)S(1)}, u32[]{:S(2)}, u32[]{:S(2)}) collective-permute-start(bf16[64,1024]{1,0:T(8,128)(2,1)S(1)} %get-tuple-element.58), channel_id=1, source_target_pairs={{0,3},{1,2},{2,1},{3,0},{4,7},{5,6},{6,5},{7,4},{8,11},{9,10},{10,... | collective-permute-start | bytes 393224 | tf_op jit(solution)/shard_map/ppermute | solution.py:23
  6.6 10.5 %collective-permute-start.1 = (bf16[64,1024]{1,0:T(8,128)(2,1)S(1)}, bf16[64,1024]{1,0:T(8,128)(2,1)S(1)}, u32[]{:S(2)}, u32[]{:S(2)}) collective-permute-start(bf16[64,1024]{1,0:T(8,128)(2,1)S(1)} %get-tuple-element.57), channel_id=1, source_target_pairs={{0,2},{1,3},{2,0},{3,1},{4,6},{5,7},{6,4},{7,5},{8,10},{9,11},{10,... | collective-permute-start | bytes 393224 | tf_op jit(solution)/shard_map/ppermute | solution.py:23
  7.1 10.0 %collective-permute-start = (bf16[64,1024]{1,0:T(8,128)(2,1)S(1)}, bf16[64,1024]{1,0:T(8,128)(2,1)S(1)}, u32[]{:S(2)}, u32[]{:S(2)}) collective-permute-start(bf16[64,1024]{1,0:T(8,128)(2,1)S(1)} %get-tuple-element.56), channel_id=1, source_target_pairs={{0,1},{1,0},{2,3},{3,2},{4,5},{5,4},{6,7},{7,6},{8,9},{9,8},{10,11... | collective-permute-start | bytes 393224 | tf_op jit(solution)/shard_map/ppermute | solution.py:23
  9.1 10.0 %all-to-all-start = ((bf16[4,64,768]{2,1,0:T(8,128)(2,1)}), bf16[4,64,768]{2,1,0:T(8,128)(2,1)S(1)}, u32[]{:S(2)}, u32[]{:S(2)}) async-start(bf16[4,64,768]{2,1,0:T(8,128)(2,1)} %shard_map.178), calls=%async_computation | async-start | bytes 786432 | tf_op jit(solution)/shard_map/all_to_all | solution.py:230
  13.3 9.2 %collective-permute-start.5 = (bf16[528,256]{1,0:T(8,128)(2,1)S(1)}, bf16[528,256]{1,0:T(8,128)(2,1)S(1)}, u32[]{:S(2)}, u32[]{:S(2)}) collective-permute-start(bf16[528,256]{1,0:T(8,128)(2,1)S(1)} %pad_maximum_fusion.8.refs_0_), channel_id=1, source_target_pairs={{0,12},{4,8},{8,4},{12,0},{1,13},{5,9},{9,5},{13,1},{2,14},{6,10},... | collective-permute-start | bytes 811016 | tf_op jit(solution)/shard_map/ppermute | solution.py:32
  19.1 15.2 %collective-permute-start.3 = (bf16[4,64,1024]{2,1,0:T(8,128)(2,1)S(1)}, bf16[4,64,1024]{2,1,0:T(8,128)(2,1)S(1)}, u32[]{:S(2)}, u32[]{:S(2)}) collective-permute-start(bf16[4,64,1024]{2,1,0:T(8,128)(2,1)S(1)} %pad_maximum_fusion.3), channel_id=1, source_target_pairs={{0,16},{16,0},{1,17},{17,1},{2,18},{18,2},{3,19},{19,3},{4,20},{20... | collective-permute-start | bytes 1572872 | tf_op jit(solution)/shard_map/ppermute | solution.py:62
  19.1 9.4 %collective-permute-start.4 = (bf16[528,256]{1,0:T(8,128)(2,1)S(1)}, bf16[528,256]{1,0:T(8,128)(2,1)S(1)}, u32[]{:S(2)}, u32[]{:S(2)}) collective-permute-start(bf16[528,256]{1,0:T(8,128)(2,1)S(1)} %pad_maximum_fusion.8.refs_0_), channel_id=1, source_target_pairs={{0,4},{4,0},{8,12},{12,8},{1,5},{5,1},{9,13},{13,9},{2,6},{6,2},{1... | collective-permute-start | bytes 811016 | tf_op jit(solution)/shard_map/ppermute | solution.py:32
  22.6 11.6 %collective-permute-start.6 = (bf16[528,256]{1,0:T(8,128)(2,1)S(1)}, bf16[528,256]{1,0:T(8,128)(2,1)S(1)}, u32[]{:S(2)}, u32[]{:S(2)}) collective-permute-start(bf16[528,256]{1,0:T(8,128)(2,1)S(1)} %collective-permute-done.5.refs_3_), channel_id=1, source_target_pairs={{0,4},{4,0},{8,12},{12,8},{1,5},{5,1},{9,13},{13,9},{2,6},{6,2},{1... | collective-permute-start | bytes 811016 | tf_op jit(solution)/shard_map/ppermute | solution.py:32
  35.8 12.2 %collective-permute-start.7 = (bf16[144,512]{1,0:T(8,128)(2,1)S(1)}, bf16[144,512]{1,0:T(8,128)(2,1)}, u32[]{:S(2)}, u32[]{:S(2)}) collective-permute-start(bf16[144,512]{1,0:T(8,128)(2,1)S(1)} %get-tuple-element.199), channel_id=1, source_target_pairs={{0,3},{1,2},{2,1},{3,0},{4,7},{5,6},{6,5},{7,4},{8,11},{9,10},{10,... | collective-permute-start | bytes 442376 | tf_op jit(solution)/shard_map/ppermute | solution.py:23
  38.5 10.2 %collective-permute-start.8 = (bf16[144,512]{1,0:T(8,128)(2,1)S(1)}, bf16[144,512]{1,0:T(8,128)(2,1)}, u32[]{:S(2)}, u32[]{:S(2)}) collective-permute-start(bf16[144,512]{1,0:T(8,128)(2,1)S(1)} %get-tuple-element.198), channel_id=1, source_target_pairs={{0,2},{1,3},{2,0},{3,1},{4,6},{5,7},{6,4},{7,5},{8,10},{9,11},{10,... | collective-permute-start | bytes 442376 | tf_op jit(solution)/shard_map/ppermute | solution.py:23
  39.1 10.4 %collective-permute-start.9 = (bf16[144,512]{1,0:T(8,128)(2,1)S(1)}, bf16[144,512]{1,0:T(8,128)(2,1)}, u32[]{:S(2)}, u32[]{:S(2)}) collective-permute-start(bf16[144,512]{1,0:T(8,128)(2,1)S(1)} %get-tuple-element.197), channel_id=1, source_target_pairs={{0,1},{1,0},{2,3},{3,2},{4,5},{5,4},{6,7},{7,6},{8,9},{9,8},{10,11... | collective-permute-start | bytes 442376 | tf_op jit(solution)/shard_map/ppermute | solution.py:23
  39.4 12.2 %collective-permute-start.10 = (bf16[256,768]{1,0:T(8,128)(2,1)S(1)}, bf16[256,768]{1,0:T(8,128)(2,1)S(1)}, u32[]{:S(2)}, u32[]{:S(2)}) collective-permute-start(bf16[256,768]{1,0:T(8,128)(2,1)S(1)} %bitcast.105), channel_id=1, source_target_pairs={{0,4},{4,0},{8,12},{12,8},{1,5},{5,1},{9,13},{13,9},{2,6},{6,2},{1... | collective-permute-start | bytes 1179656 | tf_op jit(solution)/shard_map/ppermute | solution.py:32
  41.1 18.8 %collective-permute-start.11 = (bf16[256,768]{1,0:T(8,128)(2,1)S(1)}, bf16[256,768]{1,0:T(8,128)(2,1)S(1)}, u32[]{:S(2)}, u32[]{:S(2)}) collective-permute-start(bf16[256,768]{1,0:T(8,128)(2,1)S(1)} %bitcast.106), channel_id=1, source_target_pairs={{0,12},{4,8},{8,4},{12,0},{1,13},{5,9},{9,5},{13,1},{2,14},{6,10},... | collective-permute-start | bytes 1179656 | tf_op jit(solution)/shard_map/ppermute | solution.py:32
  44.3 15.5 %all-to-all-start.1 = ((bf16[4,64,1408]{2,1,0:T(8,128)(2,1)}), bf16[4,64,1408]{2,1,0:T(8,128)(2,1)S(1)}, u32[]{:S(2)}, u32[]{:S(2)}) async-start(bf16[4,64,1408]{2,1,0:T(8,128)(2,1)} %shard_map.180), calls=%async_computation.1 | async-start | bytes 1441792 | tf_op jit(solution)/shard_map/all_to_all | solution.py:232
  59.9 11.5 %collective-permute-start.15 = (bf16[256,768]{1,0:T(8,128)(2,1)S(1)}, bf16[256,768]{1,0:T(8,128)(2,1)S(1)}, u32[]{:S(2)}, u32[]{:S(2)}) collective-permute-start(bf16[256,768]{1,0:T(8,128)(2,1)S(1)} %collective-permute-done.11.refs_3_), channel_id=1, source_target_pairs={{0,4},{4,0},{8,12},{12,8},{1,5},{5,1},{9,13},{13,9},{2,6},{6,2},{1... | collective-permute-start | bytes 1179656 | tf_op jit(solution)/shard_map/ppermute | solution.py:32
  62.2 8.4 %collective-permute-start.14 = (bf16[128,1024]{1,0:T(8,128)(2,1)S(1)}, bf16[128,1024]{1,0:T(8,128)(2,1)S(1)}, u32[]{:S(2)}, u32[]{:S(2)}) collective-permute-start(bf16[128,1024]{1,0:T(8,128)(2,1)S(1)} %pad_maximum_fusion.9.refs_0_), channel_id=1, source_target_pairs={{0,2},{1,3},{2,0},{3,1},{4,6},{5,7},{6,4},{7,5},{8,10},{9,11},{10,... | collective-permute-start | bytes 786440 | tf_op jit(solution)/shard_map/ppermute | solution.py:23
  63.9 12.6 %collective-permute-start.13 = (bf16[128,1024]{1,0:T(8,128)(2,1)S(1)}, bf16[128,1024]{1,0:T(8,128)(2,1)S(1)}, u32[]{:S(2)}, u32[]{:S(2)}) collective-permute-start(bf16[128,1024]{1,0:T(8,128)(2,1)S(1)} %pad_maximum_fusion.9.refs_0_), channel_id=1, source_target_pairs={{0,1},{1,0},{2,3},{3,2},{4,5},{5,4},{6,7},{7,6},{8,9},{9,8},{10,11... | collective-permute-start | bytes 786440 | tf_op jit(solution)/shard_map/ppermute | solution.py:23
  73.8 8.2 %collective-permute-start.18 = (bf16[64,1024]{1,0:T(8,128)(2,1)S(1)}, bf16[64,1024]{1,0:T(8,128)(2,1)S(1)}, u32[]{:S(2)}, u32[]{:S(2)}) collective-permute-start(bf16[64,1024]{1,0:T(8,128)(2,1)S(1)} %bitcast.111), channel_id=1, source_target_pairs={{0,12},{4,8},{8,4},{12,0},{1,13},{5,9},{9,5},{13,1},{2,14},{6,10},... | collective-permute-start | bytes 393224 | tf_op jit(solution)/shard_map/ppermute | solution.py:32
  83.1 23.3 %collective-permute-start.19 = (bf16[512,512]{1,0:T(8,128)(2,1)S(1)}, bf16[512,512]{1,0:T(8,128)(2,1)S(1)}, u32[]{:S(2)}, u32[]{:S(2)}) collective-permute-start(bf16[512,512]{1,0:T(8,128)(2,1)S(1)} %slice.255), channel_id=1, source_target_pairs={{0,16},{1,17},{2,18},{3,19},{4,20},{5,21},{6,22},{7,23},{8,24},{9,... | collective-permute-start | bytes 1572872 | tf_op jit(solution)/shard_map/ppermute | solution.py:275
  84.4 23.6 %collective-permute-start.20 = (bf16[256,1408]{1,0:T(8,128)(2,1)S(1)}, bf16[256,1408]{1,0:T(8,128)(2,1)S(1)}, u32[]{:S(2)}, u32[]{:S(2)}) collective-permute-start(bf16[256,1408]{1,0:T(8,128)(2,1)S(1)} %bitcast.102), channel_id=1, source_target_pairs={{0,4},{4,0},{8,12},{12,8},{1,5},{5,1},{9,13},{13,9},{2,6},{6,2},{1... | collective-permute-start | bytes 2162696 | tf_op jit(solution)/shard_map/ppermute | solution.py:32
  84.5 21.8 %collective-permute-start.21 = (bf16[64,1024]{1,0:T(8,128)(2,1)S(1)}, bf16[64,1024]{1,0:T(8,128)(2,1)S(1)}, u32[]{:S(2)}, u32[]{:S(2)}) collective-permute-start(bf16[64,1024]{1,0:T(8,128)(2,1)S(1)} %collective-permute-done.18.refs_4_), channel_id=1, source_target_pairs={{0,4},{4,0},{8,12},{12,8},{1,5},{5,1},{9,13},{13,9},{2,6},{6,2},{1... | collective-permute-start | bytes 393224 | tf_op jit(solution)/shard_map/ppermute | solution.py:32
  86.5 35.8 %collective-permute-start.25 = (bf16[256,1408]{1,0:T(8,128)(2,1)S(1)}, bf16[256,1408]{1,0:T(8,128)(2,1)S(1)}, u32[]{:S(2)}, u32[]{:S(2)}) collective-permute-start(bf16[256,1408]{1,0:T(8,128)(2,1)S(1)} %bitcast.103), channel_id=1, source_target_pairs={{0,12},{4,8},{8,4},{12,0},{1,13},{5,9},{9,5},{13,1},{2,14},{6,10},... | collective-permute-start | bytes 2162696 | tf_op jit(solution)/shard_map/ppermute | solution.py:32
  108.9 13.5 %collective-permute-start.24 = (bf16[128,1024]{1,0:T(8,128)(2,1)S(1)}, bf16[128,1024]{1,0:T(8,128)(2,1)S(1)}, u32[]{:S(2)}, u32[]{:S(2)}) collective-permute-start(bf16[128,1024]{1,0:T(8,128)(2,1)S(1)} %get-tuple-element.166), channel_id=1, source_target_pairs={{0,1},{1,0},{2,3},{3,2},{4,5},{5,4},{6,7},{7,6},{8,9},{9,8},{10,11... | collective-permute-start | bytes 786440 | tf_op jit(solution)/shard_map/ppermute | solution.py:23
  108.9 13.5 %collective-permute-start.23 = (bf16[128,1024]{1,0:T(8,128)(2,1)S(1)}, bf16[128,1024]{1,0:T(8,128)(2,1)S(1)}, u32[]{:S(2)}, u32[]{:S(2)}) collective-permute-start(bf16[128,1024]{1,0:T(8,128)(2,1)S(1)} %get-tuple-element.167), channel_id=1, source_target_pairs={{0,2},{1,3},{2,0},{3,1},{4,6},{5,7},{6,4},{7,5},{8,10},{9,11},{10,... | collective-permute-start | bytes 786440 | tf_op jit(solution)/shard_map/ppermute | solution.py:23
  110.7 11.7 %collective-permute-start.22 = (bf16[128,1024]{1,0:T(8,128)(2,1)S(1)}, bf16[128,1024]{1,0:T(8,128)(2,1)S(1)}, u32[]{:S(2)}, u32[]{:S(2)}) collective-permute-start(bf16[128,1024]{1,0:T(8,128)(2,1)S(1)} %get-tuple-element.165), channel_id=1, source_target_pairs={{0,3},{1,2},{2,1},{3,0},{4,7},{5,6},{6,5},{7,4},{8,11},{9,10},{10,... | collective-permute-start | bytes 786440 | tf_op jit(solution)/shard_map/ppermute | solution.py:23
  112.4 14.8 %collective-permute-start.26 = (bf16[176,1024]{1,0:T(8,128)(2,1)}, bf16[176,1024]{1,0:T(8,128)(2,1)S(1)}, u32[]{:S(2)}, u32[]{:S(2)}) collective-permute-start(bf16[176,1024]{1,0:T(8,128)(2,1)} %bitcast.18.refs_1_), channel_id=1, source_target_pairs={{0,4},{4,0},{8,12},{12,8},{1,5},{5,1},{9,13},{13,9},{2,6},{6,2},{1... | collective-permute-start | bytes 1081352 | tf_op jit(solution)/shard_map/ppermute | solution.py:32
  122.3 23.2 %collective-permute-start.31 = (bf16[256,1408]{1,0:T(8,128)(2,1)S(1)}, bf16[256,1408]{1,0:T(8,128)(2,1)S(1)}, u32[]{:S(2)}, u32[]{:S(2)}) collective-permute-start(bf16[256,1408]{1,0:T(8,128)(2,1)S(1)} %collective-permute-done.25.refs_3_), channel_id=1, source_target_pairs={{0,4},{4,0},{8,12},{12,8},{1,5},{5,1},{9,13},{13,9},{2,6},{6,2},{1... | collective-permute-start | bytes 2162696 | tf_op jit(solution)/shard_map/ppermute | solution.py:32
  129.0 8.3 %collective-permute-start.28 = (bf16[128,1024]{1,0:T(8,128)(2,1)}, bf16[128,1024]{1,0:T(8,128)(2,1)}, u32[]{:S(2)}, u32[]{:S(2)}) collective-permute-start(bf16[128,1024]{1,0:T(8,128)(2,1)} %pad_maximum_fusion.10.refs_0_), channel_id=1, source_target_pairs={{0,2},{1,3},{2,0},{3,1},{4,6},{5,7},{6,4},{7,5},{8,10},{9,11},{10,... | collective-permute-start | bytes 786440 | tf_op jit(solution)/shard_map/ppermute | solution.py:23
  130.5 20.5 %collective-permute-start.30 = (bf16[176,1024]{1,0:T(8,128)(2,1)}, bf16[176,1024]{1,0:T(8,128)(2,1)}, u32[]{:S(2)}, u32[]{:S(2)}) collective-permute-start(bf16[176,1024]{1,0:T(8,128)(2,1)} %bitcast.18.refs_1_), channel_id=1, source_target_pairs={{0,12},{4,8},{8,4},{12,0},{1,13},{5,9},{9,5},{13,1},{2,14},{6,10},... | collective-permute-start | bytes 1081352 | tf_op jit(solution)/shard_map/ppermute | solution.py:32
  133.1 18.1 %collective-permute-start.27 = (bf16[128,1024]{1,0:T(8,128)(2,1)}, bf16[128,1024]{1,0:T(8,128)(2,1)}, u32[]{:S(2)}, u32[]{:S(2)}) collective-permute-start(bf16[128,1024]{1,0:T(8,128)(2,1)} %pad_maximum_fusion.10.refs_0_), channel_id=1, source_target_pairs={{0,1},{1,0},{2,3},{3,2},{4,5},{5,4},{6,7},{7,6},{8,9},{9,8},{10,11... | collective-permute-start | bytes 786440 | tf_op jit(solution)/shard_map/ppermute | solution.py:23
  137.3 13.8 %collective-permute-start.29 = (bf16[128,1024]{1,0:T(8,128)(2,1)}, bf16[128,1024]{1,0:T(8,128)(2,1)}, u32[]{:S(2)}, u32[]{:S(2)}) collective-permute-start(bf16[128,1024]{1,0:T(8,128)(2,1)} %collective-permute-done.28.refs_2_), channel_id=1, source_target_pairs={{0,1},{1,0},{2,3},{3,2},{4,5},{5,4},{6,7},{7,6},{8,9},{9,8},{10,11... | collective-permute-start | bytes 786440 | tf_op jit(solution)/shard_map/ppermute | solution.py:23
  139.1 18.2 %all-to-all-start.2 = ((bf16[4,128,1024]{2,1,0:T(8,128)(2,1)}), bf16[4,128,1024]{2,1,0:T(8,128)(2,1)}, u32[]{:S(2)}, u32[]{:S(2)}) async-start(bf16[4,128,1024]{2,1,0:T(8,128)(2,1)} %broadcast_in_dim.22), calls=%async_computation.2 | async-start | bytes 2097152 | tf_op jit(solution)/shard_map/all_to_all | solution.py:291
  151.0 11.8 %collective-permute-start.32 = (bf16[176,1024]{1,0:T(8,128)(2,1)}, bf16[176,1024]{1,0:T(8,128)(2,1)}, u32[]{:S(2)}, u32[]{:S(2)}) collective-permute-start(bf16[176,1024]{1,0:T(8,128)(2,1)} %collective-permute-done.30.refs_4_), channel_id=1, source_target_pairs={{0,4},{4,0},{8,12},{12,8},{1,5},{5,1},{9,13},{13,9},{2,6},{6,2},{1... | collective-permute-start | bytes 1081352 | tf_op jit(solution)/shard_map/ppermute | solution.py:32
  160.8 14.8 %collective-permute-start.36 = (bf16[176,1024]{1,0:T(8,128)(2,1)S(1)}, bf16[176,1024]{1,0:T(8,128)(2,1)S(1)}, u32[]{:S(2)}, u32[]{:S(2)}) collective-permute-start(bf16[176,1024]{1,0:T(8,128)(2,1)S(1)} %get-tuple-element.145), channel_id=1, source_target_pairs={{0,4},{4,0},{8,12},{12,8},{1,5},{5,1},{9,13},{13,9},{2,6},{6,2},{1... | collective-permute-start | bytes 1081352 | tf_op jit(solution)/shard_map/ppermute | solution.py:32
  168.0 9.3 %collective-permute-start.35 = (bf16[128,1024]{1,0:T(8,128)(2,1)S(1)}, bf16[128,1024]{1,0:T(8,128)(2,1)S(1)}, u32[]{:S(2)}, u32[]{:S(2)}) collective-permute-start(bf16[128,1024]{1,0:T(8,128)(2,1)S(1)} %get-tuple-element.159), channel_id=1, source_target_pairs={{0,1},{1,0},{2,3},{3,2},{4,5},{5,4},{6,7},{7,6},{8,9},{9,8},{10,11... | collective-permute-start | bytes 786440 | tf_op jit(solution)/shard_map/ppermute | solution.py:23
  168.4 8.9 %collective-permute-start.34 = (bf16[128,1024]{1,0:T(8,128)(2,1)S(1)}, bf16[128,1024]{1,0:T(8,128)(2,1)S(1)}, u32[]{:S(2)}, u32[]{:S(2)}) collective-permute-start(bf16[128,1024]{1,0:T(8,128)(2,1)S(1)} %get-tuple-element.160), channel_id=1, source_target_pairs={{0,2},{1,3},{2,0},{3,1},{4,6},{5,7},{6,4},{7,5},{8,10},{9,11},{10,... | collective-permute-start | bytes 786440 | tf_op jit(solution)/shard_map/ppermute | solution.py:23
  170.1 12.1 %collective-permute-start.33 = (bf16[128,1024]{1,0:T(8,128)(2,1)S(1)}, bf16[128,1024]{1,0:T(8,128)(2,1)S(1)}, u32[]{:S(2)}, u32[]{:S(2)}) collective-permute-start(bf16[128,1024]{1,0:T(8,128)(2,1)S(1)} %get-tuple-element.158), channel_id=1, source_target_pairs={{0,3},{1,2},{2,1},{3,0},{4,7},{5,6},{6,5},{7,4},{8,11},{9,10},{10,... | collective-permute-start | bytes 786440 | tf_op jit(solution)/shard_map/ppermute | solution.py:23
  174.8 21.8 %collective-permute-start.40 = (bf16[256,1408]{1,0:T(8,128)(2,1)}, bf16[256,1408]{1,0:T(8,128)(2,1)}, u32[]{:S(2)}, u32[]{:S(2)}) collective-permute-start(bf16[256,1408]{1,0:T(8,128)(2,1)} %get-tuple-element.141), channel_id=1, source_target_pairs={{0,4},{4,0},{8,12},{12,8},{1,5},{5,1},{9,13},{13,9},{2,6},{6,2},{1... | collective-permute-start | bytes 2162696 | tf_op jit(solution)/shard_map/ppermute | solution.py:32
  184.4 9.8 %collective-permute-start.37 = (bf16[128,1024]{1,0:T(8,128)(2,1)S(1)}, bf16[128,1024]{1,0:T(8,128)(2,1)S(1)}, u32[]{:S(2)}, u32[]{:S(2)}) collective-permute-start(bf16[128,1024]{1,0:T(8,128)(2,1)S(1)} %fusion.35.refs_0_), channel_id=1, source_target_pairs={{0,1},{1,0},{2,3},{3,2},{4,5},{5,4},{6,7},{7,6},{8,9},{9,8},{10,11... | collective-permute-start | bytes 786440 | tf_op jit(solution)/shard_map/ppermute | solution.py:23
  190.9 39.2 %collective-permute-start.68 = (bf16[176,1024]{1,0:T(8,128)(2,1)}, bf16[176,1024]{1,0:T(8,128)(2,1)}, u32[]{:S(2)}, u32[]{:S(2)}) collective-permute-start(bf16[176,1024]{1,0:T(8,128)(2,1)} %get-tuple-element.144), channel_id=1, source_target_pairs={{0,4},{4,0},{8,12},{12,8},{1,5},{5,1},{9,13},{13,9},{2,6},{6,2},{1... | collective-permute-start | bytes 1081352 | tf_op jit(solution)/shard_map/ppermute | solution.py:32
  192.3 18.7 %collective-permute-start.69 = (bf16[176,1024]{1,0:T(8,128)(2,1)}, bf16[176,1024]{1,0:T(8,128)(2,1)}, u32[]{:S(2)}, u32[]{:S(2)}) collective-permute-start(bf16[176,1024]{1,0:T(8,128)(2,1)} %add_convert_fusion.4), channel_id=1, source_target_pairs={{0,12},{4,8},{8,4},{12,0},{1,13},{5,9},{9,5},{13,1},{2,14},{6,10},... | collective-permute-start | bytes 1081352 | tf_op jit(solution)/shard_map/ppermute | solution.py:32
  194.3 31.2 %collective-permute-start.42 = (bf16[256,1408]{1,0:T(8,128)(2,1)}, bf16[256,1408]{1,0:T(8,128)(2,1)S(1)}, u32[]{:S(2)}, u32[]{:S(2)}) collective-permute-start(bf16[256,1408]{1,0:T(8,128)(2,1)} %get-tuple-element.82), channel_id=1, source_target_pairs={{0,4},{4,0},{8,12},{12,8},{1,5},{5,1},{9,13},{13,9},{2,6},{6,2},{1... | collective-permute-start | bytes 2162696 | tf_op jit(solution)/shard_map/ppermute | solution.py:32
  199.7 12.5 %collective-permute-start.41 = (bf16[512,512]{1,0:T(8,128)(2,1)S(1)}, bf16[512,512]{1,0:T(8,128)(2,1)S(1)}, u32[]{:S(2)}, u32[]{:S(2)}) collective-permute-start(bf16[512,512]{1,0:T(8,128)(2,1)S(1)} %pad_maximum_fusion.5), channel_id=1, source_target_pairs={{16,0},{17,1},{18,2},{19,3},{20,4},{21,5},{22,6},{23,7},{24,8},{25... | collective-permute-start | bytes 1572872 | tf_op jit(solution)/shard_map/ppermute | solution.py:343
  203.8 60.5 %collective-permute-start.64 = (bf16[256,1408]{1,0:T(8,128)(2,1)}, bf16[256,1408]{1,0:T(8,128)(2,1)}, u32[]{:S(2)}, u32[]{:S(2)}) collective-permute-start(bf16[256,1408]{1,0:T(8,128)(2,1)} %add_convert_fusion.1), channel_id=1, source_target_pairs={{0,12},{4,8},{8,4},{12,0},{1,13},{5,9},{9,5},{13,1},{2,14},{6,10},... | collective-permute-start | bytes 2162696 | tf_op jit(solution)/shard_map/ppermute | solution.py:32
  227.2 8.3 %collective-permute-start.44 = (bf16[128,1024]{1,0:T(8,128)(2,1)S(1)}, bf16[128,1024]{1,0:T(8,128)(2,1)S(1)}, u32[]{:S(2)}, u32[]{:S(2)}) collective-permute-start(bf16[128,1024]{1,0:T(8,128)(2,1)S(1)} %get-tuple-element.155), channel_id=1, source_target_pairs={{0,2},{1,3},{2,0},{3,1},{4,6},{5,7},{6,4},{7,5},{8,10},{9,11},{10,... | collective-permute-start | bytes 786440 | tf_op jit(solution)/shard_map/ppermute | solution.py:23
  246.8 14.8 %collective-permute-start.62 = (bf16[256,768]{1,0:T(8,128)(2,1)}, bf16[256,768]{1,0:T(8,128)(2,1)}, u32[]{:S(2)}, u32[]{:S(2)}) collective-permute-start(bf16[256,768]{1,0:T(8,128)(2,1)} %get-tuple-element.143), channel_id=1, source_target_pairs={{0,4},{4,0},{8,12},{12,8},{1,5},{5,1},{9,13},{13,9},{2,6},{6,2},{1... | collective-permute-start | bytes 1179656 | tf_op jit(solution)/shard_map/ppermute | solution.py:32
  253.8 22.3 %collective-permute-start.61 = (bf16[256,768]{1,0:T(8,128)(2,1)}, bf16[256,768]{1,0:T(8,128)(2,1)S(1)}, u32[]{:S(2)}, u32[]{:S(2)}) collective-permute-start(bf16[256,768]{1,0:T(8,128)(2,1)} %get-tuple-element.91), channel_id=1, source_target_pairs={{0,4},{4,0},{8,12},{12,8},{1,5},{5,1},{9,13},{13,9},{2,6},{6,2},{1... | collective-permute-start | bytes 1179656 | tf_op jit(solution)/shard_map/ppermute | solution.py:32
  258.7 11.0 %collective-permute-start.52 = (bf16[128,1024]{1,0:T(8,128)(2,1)S(1)}, bf16[128,1024]{1,0:T(8,128)(2,1)S(1)}, u32[]{:S(2)}, u32[]{:S(2)}) collective-permute-start(bf16[128,1024]{1,0:T(8,128)(2,1)S(1)} %get-tuple-element.151), channel_id=1, source_target_pairs={{0,1},{1,0},{2,3},{3,2},{4,5},{5,4},{6,7},{7,6},{8,9},{9,8},{10,11... | collective-permute-start | bytes 786440 | tf_op jit(solution)/shard_map/ppermute | solution.py:23
  259.7 10.1 %collective-permute-start.51 = (bf16[128,1024]{1,0:T(8,128)(2,1)S(1)}, bf16[128,1024]{1,0:T(8,128)(2,1)S(1)}, u32[]{:S(2)}, u32[]{:S(2)}) collective-permute-start(bf16[128,1024]{1,0:T(8,128)(2,1)S(1)} %get-tuple-element.152), channel_id=1, source_target_pairs={{0,2},{1,3},{2,0},{3,1},{4,6},{5,7},{6,4},{7,5},{8,10},{9,11},{10,... | collective-permute-start | bytes 786440 | tf_op jit(solution)/shard_map/ppermute | solution.py:23
  261.6 11.0 %collective-permute-start.50 = (bf16[128,1024]{1,0:T(8,128)(2,1)S(1)}, bf16[128,1024]{1,0:T(8,128)(2,1)S(1)}, u32[]{:S(2)}, u32[]{:S(2)}) collective-permute-start(bf16[128,1024]{1,0:T(8,128)(2,1)S(1)} %get-tuple-element.150), channel_id=1, source_target_pairs={{0,3},{1,2},{2,1},{3,0},{4,7},{5,6},{6,5},{7,4},{8,11},{9,10},{10,... | collective-permute-start | bytes 786440 | tf_op jit(solution)/shard_map/ppermute | solution.py:23
  264.3 12.3 %collective-permute-start.63 = (bf16[256,768]{1,0:T(8,128)(2,1)S(1)}, bf16[256,768]{1,0:T(8,128)(2,1)S(1)}, u32[]{:S(2)}, u32[]{:S(2)}) collective-permute-start(bf16[256,768]{1,0:T(8,128)(2,1)S(1)} %add_convert_fusion.3), channel_id=1, source_target_pairs={{0,12},{4,8},{8,4},{12,0},{1,13},{5,9},{9,5},{13,1},{2,14},{6,10},... | collective-permute-start | bytes 1179656 | tf_op jit(solution)/shard_map/ppermute | solution.py:32
  274.0 16.6 %collective-permute-start.66 = (bf16[64,1024]{1,0:T(8,128)(2,1)}, bf16[64,1024]{1,0:T(8,128)(2,1)S(1)}, u32[]{:S(2)}, u32[]{:S(2)}) collective-permute-start(bf16[64,1024]{1,0:T(8,128)(2,1)} %get-tuple-element.98), channel_id=1, source_target_pairs={{0,4},{4,0},{8,12},{12,8},{1,5},{5,1},{9,13},{13,9},{2,6},{6,2},{1... | collective-permute-start | bytes 393224 | tf_op jit(solution)/shard_map/ppermute | solution.py:32
  274.9 32.2 %collective-permute-start.65 = (bf16[64,1024]{1,0:T(8,128)(2,1)}, bf16[64,1024]{1,0:T(8,128)(2,1)}, u32[]{:S(2)}, u32[]{:S(2)}) collective-permute-start(bf16[64,1024]{1,0:T(8,128)(2,1)} %get-tuple-element.97), channel_id=1, source_target_pairs={{0,4},{4,0},{8,12},{12,8},{1,5},{5,1},{9,13},{13,9},{2,6},{6,2},{1... | collective-permute-start | bytes 393224 | tf_op jit(solution)/shard_map/ppermute | solution.py:32
  277.7 15.6 %collective-permute-start.56 = (bf16[64,1024]{1,0:T(8,128)(2,1)S(1)}, bf16[64,1024]{1,0:T(8,128)(2,1)S(1)}, u32[]{:S(2)}, u32[]{:S(2)}) collective-permute-start(bf16[64,1024]{1,0:T(8,128)(2,1)S(1)} %get-tuple-element.171), channel_id=1, source_target_pairs={{0,3},{1,2},{2,1},{3,0},{4,7},{5,6},{6,5},{7,4},{8,11},{9,10},{10,... | collective-permute-start | bytes 393224 | tf_op jit(solution)/shard_map/ppermute | solution.py:23
  279.1 22.3 %collective-permute-start.55 = (bf16[64,1024]{1,0:T(8,128)(2,1)S(1)}, bf16[64,1024]{1,0:T(8,128)(2,1)S(1)}, u32[]{:S(2)}, u32[]{:S(2)}) collective-permute-start(bf16[64,1024]{1,0:T(8,128)(2,1)S(1)} %get-tuple-element.172), channel_id=1, source_target_pairs={{0,2},{1,3},{2,0},{3,1},{4,6},{5,7},{6,4},{7,5},{8,10},{9,11},{10,... | collective-permute-start | bytes 393224 | tf_op jit(solution)/shard_map/ppermute | solution.py:23
  280.2 21.2 %collective-permute-start.54 = (bf16[64,1024]{1,0:T(8,128)(2,1)S(1)}, bf16[64,1024]{1,0:T(8,128)(2,1)S(1)}, u32[]{:S(2)}, u32[]{:S(2)}) collective-permute-start(bf16[64,1024]{1,0:T(8,128)(2,1)S(1)} %get-tuple-element.173), channel_id=1, source_target_pairs={{0,1},{1,0},{2,3},{3,2},{4,5},{5,4},{6,7},{7,6},{8,9},{9,8},{10,11... | collective-permute-start | bytes 393224 | tf_op jit(solution)/shard_map/ppermute | solution.py:23
  282.0 16.0 %all-to-all-start.3 = ((f32[16,1,128]{2,1,0:T(1,128)}), f32[16,1,128]{2,1,0:T(1,128)S(1)}, u32[]{:S(2)}, u32[]{:S(2)}) async-start(f32[16,1,128]{2,1,0:T(1,128)} %reshape.129), calls=%async_computation.3 | async-start | bytes 16384 | tf_op jit(solution)/shard_map/all_to_all | solution.py:401
  290.6 13.3 %collective-permute-start.59 = (bf16[512,256]{1,0:T(8,128)(2,1)}, bf16[512,256]{1,0:T(8,128)(2,1)}, u32[]{:S(2)}, u32[]{:S(2)}) collective-permute-start(bf16[512,256]{1,0:T(8,128)(2,1)} %get-tuple-element.87), channel_id=1, source_target_pairs={{0,4},{4,0},{8,12},{12,8},{1,5},{5,1},{9,13},{13,9},{2,6},{6,2},{1... | collective-permute-start | bytes 786440 | tf_op jit(solution)/shard_map/ppermute | solution.py:32
  293.3 13.8 %collective-permute-start.67 = (bf16[64,1024]{1,0:T(8,128)(2,1)}, bf16[64,1024]{1,0:T(8,128)(2,1)}, u32[]{:S(2)}, u32[]{:S(2)}) collective-permute-start(bf16[64,1024]{1,0:T(8,128)(2,1)} %add_convert_fusion.6), channel_id=1, source_target_pairs={{0,12},{4,8},{8,4},{12,0},{1,13},{5,9},{9,5},{13,1},{2,14},{6,10},... | collective-permute-start | bytes 393224 | tf_op jit(solution)/shard_map/ppermute | solution.py:32
  297.9 12.2 %all-to-all-start.4 = ((bf16[4,64,1408]{2,1,0:T(8,128)(2,1)}), bf16[4,64,1408]{2,1,0:T(8,128)(2,1)S(1)}, u32[]{:S(2)}, u32[]{:S(2)}) async-start(bf16[4,64,1408]{2,1,0:T(8,128)(2,1)} %bitcast.36), calls=%async_computation.4 | async-start | bytes 1441792 | tf_op jit(solution)/shard_map/all_to_all | solution.py:380
  303.2 18.2 %collective-permute-start.57 = (bf16[4,64,1024]{2,1,0:T(8,128)(2,1)S(1)}, bf16[4,64,1024]{2,1,0:T(8,128)(2,1)S(1)}, u32[]{:S(2)}, u32[]{:S(2)}) collective-permute-start(bf16[4,64,1024]{2,1,0:T(8,128)(2,1)S(1)} %pad_maximum_fusion.7.a_ref), channel_id=1, source_target_pairs={{0,16},{16,0},{1,17},{17,1},{2,18},{18,2},{3,19},{19,3},{4,20},{20... | collective-permute-start | bytes 1572872 | tf_op jit(solution)/shard_map/ppermute | solution.py:62
  303.3 11.6 %collective-permute-start.58 = (bf16[512,256]{1,0:T(8,128)(2,1)}, bf16[512,256]{1,0:T(8,128)(2,1)}, u32[]{:S(2)}, u32[]{:S(2)}) collective-permute-start(bf16[512,256]{1,0:T(8,128)(2,1)} %get-tuple-element.86), channel_id=1, source_target_pairs={{0,4},{4,0},{8,12},{12,8},{1,5},{5,1},{9,13},{13,9},{2,6},{6,2},{1... | collective-permute-start | bytes 786440 | tf_op jit(solution)/shard_map/ppermute | solution.py:32
  305.6 12.4 %collective-permute-start.60 = (bf16[512,256]{1,0:T(8,128)(2,1)}, bf16[512,256]{1,0:T(8,128)(2,1)}, u32[]{:S(2)}, u32[]{:S(2)}) collective-permute-start(bf16[512,256]{1,0:T(8,128)(2,1)} %add_convert_fusion.5), channel_id=1, source_target_pairs={{0,12},{4,8},{8,4},{12,0},{1,13},{5,9},{9,5},{13,1},{2,14},{6,10},... | collective-permute-start | bytes 786440 | tf_op jit(solution)/shard_map/ppermute | solution.py:32
  310.1 13.3 %all-to-all-start.5 = ((bf16[4,64,768]{2,1,0:T(8,128)(2,1)}), bf16[4,64,768]{2,1,0:T(8,128)(2,1)S(1)}, u32[]{:S(2)}, u32[]{:S(2)}) async-start(bf16[4,64,768]{2,1,0:T(8,128)(2,1)} %bitcast.37), calls=%async_computation.5 | async-start | bytes 786432 | tf_op jit(solution)/shard_map/all_to_all | solution.py:383
  (82 other events, 541.2 us)

commit v3 on v1

v3 whole, which is shorter than its diff:
```python
import jax
import jax.numpy as jnp
from jax import lax
from jax.experimental import pallas as pl
from jax.experimental.pallas import tpu as pltpu
from jax.sharding import Mesh
from jax.sharding import PartitionSpec as P

HD = 64
F32 = jnp.float32
BF = jnp.bfloat16
NN = (((1,), (0,)), ((), ()))
NT = (((1,), (1,)), ((), ()))
TN = (((0,), (0,)), ((), ()))


def mm(a, b, form=NN):
    return lax.dot_general(a, b, form, preferred_element_type=F32)


DUE = {
    "gu": "half",
    "qkv3": "half",
    "qkv1": "mine1",
    "qkv2": "byy1",
    "up3": "kv",
    "gu1": "byxy1",
    "cot": "parts1",
    "low3": "mid",
    "up2": "byy2",
    "down1": "byy2",
    "g1": "nb2",
    "g2": "branch",
    "u1": "parts3",
    "result": "into",
    "h1": "gpy",
    "u2": "gproj",
    "in1": "got",
    "u3": "both",
    "h2": "got",
    "h3": "gu_out",
    "in2": "gu_out",
    "down3": "hidden",
    "g3": "context",
}
SKIP = (6, 7, 23, 32, 36)
COST = {
    "": 3.0,
    "unpack_columns": 10.0,
    "row_parts": 10.0,
    "pack_pairs": 0.3,
}


def tie(x, *after):
    return lax.optimization_barrier((x,) + after)[0]


def opt(i, x, *after):
    return x if i in SKIP else tie(x, *after)


def corner(i, by_y, x):
    return hop(by_y, 1) if i not in SKIP else hop(x, 3)


class Flying(dict):
    def due(self, point, x):
        after = [v for k, v in self.items() if DUE.get(k) == point]
        return tie(x, *after) if after else x


def hop(x, r):
    return lax.ppermute(x, "t", [(i, i ^ r) for i in range(4)])


def zhop(x, r):
    return lax.ppermute(x, "d1", [(i, i ^ r) for i in range(4)])


def inward(x):
    return lax.ppermute(x, "d1", [(0, 1), (3, 2)])


def across(x):
    return lax.ppermute(x, "d1", [(1, 2), (2, 1)])


def swap(x):
    return lax.ppermute(x, "stream", [(0, 1), (1, 0)])


def collect(parts):
    return [parts[0]] + [hop(parts[r], r) for r in (1, 2, 3)]


def call(body, outs, *args, scalars=None, scratch=()):
    inside = [pl.BlockSpec(memory_space=pltpu.VMEM)] * len(args)
    if scalars is not None:
        inside = [pl.BlockSpec(memory_space=pltpu.SMEM)] + inside
        args = (scalars,) + args
    single = not isinstance(outs, list)
    shapes = [jax.ShapeDtypeStruct(*o) for o in ([outs] if single else outs)]
    got = pl.pallas_call(
        body,
        out_shape=shapes,
        in_specs=inside,
        out_specs=[pl.BlockSpec(memory_space=pltpu.VMEM)] * len(shapes),
        scratch_shapes=[pltpu.VMEM(*x) for x in scratch],
        compiler_params=pltpu.CompilerParams(vmem_limit_bytes=24 << 20),
        cost_estimate=pl.CostEstimate(
            flops=int(COST.get(body.__qualname__.split(".")[0], COST.get("", 3.0)) * 1e9),
            bytes_accessed=5 * 10**6,
            transcendentals=0,
        ),
    )(*args)
    return got[0] if single else list(got)


def total(refs):
    return sum(x[...].astype(F32) for x in refs)


def scale_of(v):
    return lax.rsqrt(jnp.mean(v * v, axis=-1, keepdims=True) + 1e-05)


def turned(d, r, n):
    return pl.ds(pl.multiple_of((d ^ r) * n, n & -n), n)


def pack_columns(w, k):
    rows = w.shape[0]
    c = w.shape[1] // (k * 16)

    def body(w_ref, o_ref):
        x = w_ref[...]
        for t in range(4):
            o_ref[t] = jnp.concatenate(
                [x[:, (i * 4 + t) * c : (i * 4 + t + 1) * c] for i in range(k * 4)], axis=1
            )

    return call(body, ((4, rows, k * 4 * c), w.dtype), w)


def lanes(n):
    return n - n % 128


def pair_up(gate, up):
    n = lanes(gate.shape[1])
    return jnp.concatenate([gate[:, :n], up[:, :n], gate[:, n:], up[:, n:]], axis=1)


def pair_down(x):
    half = x.shape[1] // 2
    n = lanes(half)
    gate = jnp.concatenate([x[:, :n], x[:, 2 * n : n + half]], axis=1)
    up = jnp.concatenate([x[:, n : 2 * n], x[:, n + half :]], axis=1)
    return gate, up


def pack_pairs(w):
    rows = w.shape[0]
    c = w.shape[1] // 32

    def body(w_ref, o_ref):
        x = w_ref[...]
        for t in range(4):
            sides = [
                jnp.concatenate(
                    [x[:, ((k * 4 + i) * 4 + t) * c : ((k * 4 + i) * 4 + t + 1) * c] for i in range(4)],
                    axis=1,
                )
                for k in range(2)
            ]
            o_ref[t] = pair_up(*sides)

    return call(body, ((4, rows, 8 * c), w.dtype), w)


def unpack_columns(blocks, k, scalars):
    rows = blocks[0].shape[0]
    c = blocks[0].shape[1] // (k * 4)

    def body(n_ref, *refs):
        o_ref, hold = refs[4], refs[5]
        for r in range(4):
            hold[n_ref[1] ^ r] = refs[r][...]
        x = [hold[t].astype(F32) for t in range(4)]
        if k == 2:
            x = [jnp.concatenate(pair_down(v), axis=1) for v in x]
        o_ref[...] = jnp.concatenate(
            [x[t][:, i * c : (i + 1) * c] for i in range(k * 4) for t in range(4)], axis=1
        )

    return call(
        body,
        ((rows, k * 16 * c), F32),
        *blocks,
        scalars=scalars,
        scratch=[((4, rows, 4 * k * c), blocks[0].dtype)],
    )


def pack_context(context, scalars):
    half = context.shape[0] // 2
    c = context.shape[1] // 16

    def body(n_ref, x_ref, *o_refs):
        s, t, d = n_ref[0], n_ref[1], n_ref[2]
        row = pl.multiple_of(s * half, half)
        for r in range(4):
            for q in range(4):
                col = pl.multiple_of(((d ^ q) * 4 + (t ^ r)) * c, c)
                o_refs[r][:, q * c : (q + 1) * c] = x_ref[pl.ds(row, half), pl.ds(col, c)]

    return call(body, [((half, 4 * c), context.dtype)] * 4, context, scalars=scalars)


def stack4(parts):
    n, c = parts[0].shape

    def body(*refs):
        for r in range(4):
            refs[4][r] = refs[r][...]

    return call(body, ((4, n, c), parts[0].dtype), *parts)


def unpack_context(own, other, scalars):
    half = own.shape[1]
    c = own.shape[2] // 4

    def body(n_ref, a_ref, b_ref, o_ref):
        s, t, d = n_ref[0], n_ref[1], n_ref[2]
        for ref, place in ((a_ref, s), (b_ref, 1 - s)):
            row = pl.multiple_of(place * half, half)
            for r in range(4):
                for q in range(4):
                    col = pl.multiple_of(((d ^ q) * 4 + (t ^ r)) * c, c)
                    o_ref[pl.ds(row, half), pl.ds(col, c)] = ref[
                        r, :, q * c : (q + 1) * c
                    ].astype(F32)

    return call(body, ((2 * half, 16 * c), F32), own, other, scalars=scalars)


def project(own, other, ins, some, scalars):
    half, feats = own.shape[1:]
    wide = ins[0].shape[0] - 16
    c = ins[0].shape[1]

    def body(n_ref, a_ref, b_ref, *refs):
        w_refs, g_ref, p_refs, w_all = refs[:4], refs[4], refs[5:9], refs[9]
        mine = pl.multiple_of(n_ref[0] * half, half)
        theirs = pl.multiple_of((1 - n_ref[0]) * half, half)
        for r in range(4):
            w_all[:, r * c : (r + 1) * c] = w_refs[r][:wide]
        gains = jnp.concatenate([w[wide:, :some] for w in w_refs], axis=1)
        for r in range(4):
            g_ref[pl.ds(r * 2 * half + mine, half)] = a_ref[r]
            g_ref[pl.ds(r * 2 * half + theirs, half)] = b_ref[r]
        x = mm(g_ref[...], w_all[...], NT).astype(BF)
        for r in range(4):
            p_refs[r][: 2 * half] = x[r * 2 * half : (r + 1) * 2 * half]
            p_refs[r][2 * half :] = gains

    outs = [((8 * half, feats), BF)] + [((2 * half + 16, wide), BF)] * 4
    got = call(body, outs, own, other, *ins, scalars=scalars, scratch=[((wide, feats), BF)])
    return got[0], got[1:]


def half_sum(parts):
    rows = parts[0].shape[0] - 16

    def body(a, b, c, e, o_ref):
        o_ref[...] = sum(x[:rows].astype(F32) for x in (a, b, c, e)).astype(BF)

    return call(body, ((rows, parts[0].shape[1]), BF), *parts)


def first_norm(own, other, parts, tokens, scalars):
    rows, wide = tokens.shape
    q = wide // 4
    some = parts[0].shape[1] // 4
    e = some // 2

    def body(n_ref, a_ref, b_ref, *refs):
        g_refs, t_ref, v_ref, n_out, gain_ref, hold = refs[:4], refs[4], refs[5], refs[6], refs[7], refs[8]
        s, t, d = n_ref[0], n_ref[1], n_ref[2]
        for r in range(4):
            hold[r * 8 : r * 8 + 8] = g_refs[r][rows : rows + 8].astype(F32)
        found = [hold[pl.ds(pl.multiple_of((t ^ j) * 8, 8), 8)][:1] for j in range(4)]
        for i in range(2):
            gain_ref[i : i + 1] = jnp.concatenate(
                [found[j][:, r * some + i * e : r * some + (i + 1) * e] for r in range(4) for j in range(4)],
                axis=1,
            )
        a = a_ref[...].astype(F32)
        b = b_ref[...].astype(F32)
        first = s == 0
        v = t_ref[...].astype(F32) + jnp.concatenate(
            [jnp.where(first, a, b), jnp.where(first, b, a)], axis=1
        )
        v_ref[...] = v
        scale = scale_of(v)
        for r in range(4):
            cols = slice(r * q, (r + 1) * q)
            n_out[:, cols] = (v_ref[:, turned(d, r, q)] * scale * gain_ref[0:1, cols]).astype(BF)

    return call(
        body,
        [((rows, wide), F32), ((rows, wide), BF), ((8, wide), F32)],
        own,
        other,
        *parts,
        tokens,
        scalars=scalars,
        scratch=[((32, 4 * some), F32)],
    )


def second_norm(start, parts, gains, scalars):
    rows, wide = start.shape
    q = wide // 4

    def body(n_ref, v_ref, a, b, c, e, gain_ref, m_ref, n_out):
        m = v_ref[...] + total((a, b, c, e))
        m_ref[...] = m
        scale = scale_of(m)
        for r in range(4):
            cols = slice(r * q, (r + 1) * q)
            n_out[:, cols] = (
                m_ref[:, turned(n_ref[2], r, q)] * scale * gain_ref[1:2, cols]
            ).astype(BF)

    return call(
        body,
        [((rows, wide), F32), ((rows, wide), BF)],
        start,
        *parts,
        gains,
        scalars=scalars,
    )


def norm_back(parts, value, gains, which, base, scalars, split):
    rows, wide = value.shape
    q = wide // 4

    def body(n_ref, a, b, c, e, v_ref, gain_ref, p_ref, o_ref, d_ref, *l_refs):
        s, d = n_ref[0], n_ref[2]
        grad = total((a, b, c, e))
        v = v_ref[...]
        scale = scale_of(v)
        inner = jnp.zeros((rows, 1), F32)
        for r in range(4):
            cols = slice(r * q, (r + 1) * q)
            unit = v_ref[:, turned(d, r, q)] * scale
            piece = grad[:, cols] * unit
            d_ref[0:1, turned(d, r, q)] = jnp.sum(piece, axis=0, keepdims=True)
            inner = inner + jnp.sum(piece * gain_ref[which : which + 1, cols], axis=-1, keepdims=True)
        inner = inner / wide
        for r in range(4):
            cols = slice(r * q, (r + 1) * q)
            at = turned(d, r, q)
            unit = v_ref[:, at] * scale
            o_ref[:, at] = p_ref[:, at].astype(F32) + scale * (
                grad[:, cols] * gain_ref[which : which + 1, cols] - unit * inner
            )
        if split:
            for ref, place in zip(l_refs, (s, 1 - s)):
                ref[...] = o_ref[:, pl.ds(pl.multiple_of(place * (wide // 2), wide // 2), wide // 2)].astype(BF)
        else:
            l_refs[0][...] = o_ref[...].astype(BF)

    low = [((rows, wide // 2), BF)] * 2 if split else [((rows, wide), BF)]
    return call(
        body,
        [((rows, wide), F32), ((8, wide), F32)] + low,
        *parts,
        value,
        gains,
        base,
        scalars=scalars,
    )


def beside(left, right):
    n, c = left.shape
    k, wide = right.shape

    def body(a_ref, b_ref, o_ref):
        o_ref[:, :c] = a_ref[...]
        for j in range(4):
            o_ref[j * k : (j + 1) * k, c:] = b_ref[:, j * (wide // 4) : (j + 1) * (wide // 4)]

    return call(body, ((n, c + wide // 4), left.dtype), left, right)


def query_key_value(chunks, ws):
    n, wide = chunks[0].shape
    k = ws[0].shape[0]
    c = k

    def body(*refs):
        c_refs, w_refs, q_ref, kv_ref, w_ref, all_ref = refs[:4], refs[4:8], refs[8], refs[9], refs[10], refs[11]
        for r in range(4):
            w_ref[r * k : (r + 1) * k] = w_refs[r][:, : 3 * c]
            all_ref[r * n : (r + 1) * n] = c_refs[r][...]
        x = mm(all_ref[...], w_ref[...]).astype(BF)
        q_ref[...] = x[:, :c]
        kv_ref[...] = x[:, c:]

    return call(
        body,
        [((4 * n, c), BF), ((4 * n, 2 * c), BF), ((4 * k, 3 * c), BF)],
        *chunks,
        *ws,
        scratch=[((4 * n, wide), BF)],
    )


def head_mask(c):
    i = lax.broadcasted_iota(jnp.int32, (c, c), 0) // HD
    j = lax.broadcasted_iota(jnp.int32, (c, c), 1) // HD
    return (i == j).astype(F32).astype(BF)


def head_sum(x, mask):
    high = x.astype(BF)
    low = (x - high.astype(F32)).astype(BF)
    return mm(high, mask) + mm(low, mask)


def attend(q, kv, far, ws, scalars):
    rows, c = q.shape
    n = rows // 4
    k, wide = c // 4, 4 * c

    def body(n_ref, q_ref, kv_ref, f_ref, *refs):
        o_refs, m_ref, w_ref, wo_ref, p_refs = refs[:4], refs[4], refs[5], refs[6], refs[7:]
        s, d = n_ref[0], n_ref[2]
        for r in range(4):
            for j in range(4):
                wo_ref[turned(d, r, k), j * c : (j + 1) * c] = o_refs[r][
                    j * k : (j + 1) * k, 3 * c :
                ]
        mask = head_mask(c)
        for r in range(4):
            at = slice(r * n, (r + 1) * n)
            own = kv_ref[at].astype(F32)
            other = f_ref[at].astype(F32)
            diff = head_sum(q_ref[at].astype(F32) * (own[:, :c] - other[:, :c]), mask)
            w = jnp.where(s == 0, 1.0, jax.nn.sigmoid(diff * HD ** (-0.5)))
            w_ref[at] = w
            mixed = (w * own[:, c:] + (1.0 - w) * other[:, c:]).astype(BF)
            m_ref[at] = mixed
        x = mm(m_ref[...], wo_ref[...]).astype(BF)
        for r in range(4):
            p_refs[r][...] = x[r * n : (r + 1) * n]

    return call(
        body,
        [((rows, c), BF), ((rows, c), F32), ((4 * k, wide), BF)] + [((n, wide), BF)] * 4,
        q,
        kv,
        far,
        *ws,
        scalars=scalars,
    )


def attend_back(chunks, wo, w, q, kv, far):
    n, wide = chunks[0].shape
    rows, c = q.shape

    def body(*refs):
        c_refs = refs[:4]
        wo_ref, w_ref, q_ref, kv_ref, f_ref, g_ref, b_ref, all_ref, gm_ref = refs[4:]
        mask = head_mask(c)
        for r in range(4):
            all_ref[r * n : (r + 1) * n] = c_refs[r][...]
        gm_ref[...] = mm(all_ref[...], wo_ref[...], NT)
        for r in range(4):
            at = slice(r * n, (r + 1) * n)
            gm = gm_ref[at]
            own = kv_ref[at].astype(F32)
            other = f_ref[at].astype(F32)
            w_own = w_ref[at]
            gs = (
                w_own
                * (1.0 - w_own)
                * head_sum(gm * (own[:, c:] - other[:, c:]), mask)
                * HD ** (-0.5)
            )
            gk = gs * q_ref[at].astype(F32)
            g_ref[at, :c] = gs * (own[:, :c] - other[:, :c])
            g_ref[at, c : 2 * c] = gk
            g_ref[at, 2 * c :] = w_own * gm
            b_ref[at, :c] = (-gk).astype(BF)
            b_ref[at, c:] = ((1.0 - w_own) * gm).astype(BF)

    return call(
        body,
        [((rows, 3 * c), F32), ((rows, 2 * c), BF)],
        *chunks,
        wo,
        w,
        q,
        kv,
        far,
        scratch=[((rows, wide), BF), ((rows, c), F32)],
    )


def into_normed(grad, back, w):
    rows, cols = grad.shape
    n, c = rows // 4, cols // 3

    def body(g_ref, b_ref, w_ref, l_ref, *p_refs):
        l_ref[:, :c] = g_ref[:, :c].astype(BF)
        l_ref[:, c:] = (g_ref[:, c:] + b_ref[...].astype(F32)).astype(BF)
        x = mm(l_ref[...], w_ref[...], NT).astype(BF)
        for r in range(4):
            p_refs[r][...] = x[r * n : (r + 1) * n]

    return call(
        body, [((rows, cols), BF)] + [((n, w.shape[0]), BF)] * 4, grad, back, w
    )


def parts_of(k, cols):
    return [((k, cols), BF), ((k, cols), BF), ((2 * k, cols), BF)]


def put_part(refs, r, value, cols=slice(None)):
    k = refs[0].shape[0]
    if r < 2:
        refs[r][:, cols] = value
    else:
        refs[2][(r - 2) * k : (r - 1) * k, cols] = value


def weight_parts(chunks, right):
    n, wide = chunks[0].shape
    q = wide // 4
    cols = right.shape[1]

    def body(*refs):
        c_refs, g_ref, o_refs, all_ref = refs[:4], refs[4], refs[5:8], refs[8]
        for r in range(4):
            all_ref[r * n : (r + 1) * n] = c_refs[r][...]
        for r in range(4):
            put_part(o_refs, r, mm(all_ref[:, r * q : (r + 1) * q], g_ref[...], TN).astype(BF))

    return call(body, parts_of(q, cols), *chunks, right, scratch=[((4 * n, wide), BF)])


def attention_parts(chunks, right, left, others, scalars):
    n, wide = chunks[0].shape
    q = wide // 4
    cols, c = right.shape[1], left.shape[1]
    k = c // 4

    def body(n_ref, *refs):
        c_refs, g_ref, l_ref, e_refs, o_refs, all_ref, x_ref = (
            refs[:4],
            refs[4],
            refs[5],
            refs[6:10],
            refs[10:13],
            refs[13],
            refs[14],
        )
        for r in range(4):
            all_ref[r * n : (r + 1) * n] = c_refs[r][...]
        for r in range(4):
            x = mm(all_ref[:, r * q : (r + 1) * q], g_ref[...], TN).astype(BF)
            put_part(o_refs, r, x, slice(0, cols))
        for r in range(4):
            all_ref[r * n : (r + 1) * n] = e_refs[r][...]
        x_ref[...] = mm(l_ref[...], all_ref[...], TN).astype(BF)
        for r in range(4):
            x = x_ref[turned(n_ref[2], r, k)]
            x = jnp.concatenate([x[:, j * c : (j + 1) * c] for j in range(4)], axis=0)
            put_part(o_refs, r, x, slice(cols, cols + c))

    return call(
        body,
        parts_of(q, cols + c),
        *chunks,
        right,
        left,
        *others,
        scalars=scalars,
        scratch=[((4 * n, wide), BF), ((c, wide), BF)],
    )


def row_parts(left, chunks, scalars):
    n, wide = chunks[0].shape
    k = left.shape[1]

    def body(n_ref, l_ref, *refs):
        c_refs, o_refs, all_ref, sum_ref = refs[:4], refs[4:7], refs[7], refs[8]
        for r in range(4):
            all_ref[r * n : (r + 1) * n] = c_refs[r][...]
        sum_ref[...] = mm(l_ref[...], all_ref[...], TN).astype(BF)
        for r in range(4):
            put_part(o_refs, r, sum_ref[turned(n_ref[2], r, k // 4)])

    return call(
        body,
        parts_of(k // 4, wide),
        left,
        *chunks,
        scalars=scalars,
        scratch=[((4 * n, wide), BF), ((k, wide), BF)],
    )


def for_far(pair, got):
    n = pair.shape[0] // 2

    def body(a_ref, b_ref, o_ref):
        o_ref[:n] = (a_ref[n:].astype(F32) + b_ref[:n].astype(F32)).astype(BF)
        o_ref[n:] = (a_ref[:n].astype(F32) + b_ref[n:].astype(F32)).astype(BF)

    return call(body, (pair.shape, BF), pair, got)


def for_near(near, got):
    n = near.shape[0]

    def body(a_ref, b_ref, o_ref):
        o_ref[...] = (a_ref[...].astype(F32) + b_ref[n:].astype(F32)).astype(BF)

    return call(body, (near.shape, BF), near, got)


def finished(own, near, far, dtype=F32):
    n = own.shape[0]

    def body(a_ref, b_ref, c_ref, o_ref):
        o_ref[...] = (
            a_ref[...].astype(F32) + b_ref[...].astype(F32) + c_ref[:n].astype(F32)
        ).astype(dtype)

    return call(body, (own.shape, dtype), own, near, far)


def finished_rows(own, near, far, scalars):
    n, cols = own.shape
    k = n // 4

    def body(n_ref, a_ref, b_ref, c_ref, *refs):
        refs[4][...] = (
            a_ref[...].astype(F32) + b_ref[...].astype(F32) + c_ref[:n].astype(F32)
        ).astype(BF)
        for r in range(4):
            refs[r][...] = refs[4][turned(n_ref[1], r, k)]

    return call(
        body,
        [((k, cols), BF)] * 4,
        own,
        near,
        far,
        scalars=scalars,
        scratch=[((n, cols), BF)],
    )


def finished_pair(own, near, far, scalars):
    n, cols = own.shape
    c = cols // 4
    k = n // 4

    def body(n_ref, a_ref, b_ref, c_ref, *refs):
        x = a_ref[...].astype(F32) + b_ref[...].astype(F32) + c_ref[:n].astype(F32)
        refs[5][...] = x[:, : 3 * c].astype(BF)
        for r in range(4):
            refs[r][...] = refs[5][turned(n_ref[1], r, k)]
        for j in range(4):
            refs[4][:, j * c : (j + 1) * c] = x[j * k : (j + 1) * k, 3 * c :]

    return call(
        body,
        [((k, 3 * c), BF)] * 4 + [((k, 4 * c), F32)],
        own,
        near,
        far,
        scalars=scalars,
        scratch=[((n, 3 * c), BF)],
    )


def finished_in(own, near, far):
    n = own.shape[0]
    k = n - 16

    def body(a_ref, b_ref, c_ref, o_ref, g_ref):
        o_ref[...] = (
            a_ref[:k].astype(F32) + b_ref[:k].astype(F32) + c_ref[:k].astype(F32)
        )
        g_ref[...] = (
            a_ref[k:].astype(F32) + b_ref[k:].astype(F32) + c_ref[k:n].astype(F32)
        )

    return call(body, [((k, own.shape[1]), F32), ((16, own.shape[1]), F32)], own, near, far)


def gate_and_up(chunks, ws):
    n, wide = chunks[0].shape
    cols = ws[0].shape[1]
    ff = cols // 2
    sizes = [x.shape[0] for x in ws]

    def body(*refs):
        c_refs, w_refs = refs[:4], refs[4 : 4 + len(ws)]
        w_ref, h_ref, a_ref, b_ref, all_ref, x_ref = refs[4 + len(ws) :]
        at = 0
        for ref, size in zip(w_refs, sizes):
            w_ref[at : at + size] = ref[...]
            at += size
        for r in range(4):
            all_ref[r * n : (r + 1) * n] = c_refs[r][...]
        x_ref[...] = mm(all_ref[...], w_ref[...])
        for r in range(4):
            rows = slice(r * n, (r + 1) * n)
            gate, up = pair_down(x_ref[rows])
            sig = jax.nn.sigmoid(gate)
            b = gate * sig
            h_ref[rows] = (b * up).astype(BF)
            a_ref[rows] = up * sig * (1.0 + gate * (1.0 - sig))
            b_ref[rows] = b

    return call(
        body,
        [((wide, cols), BF), ((4 * n, ff), BF), ((4 * n, ff), F32), ((4 * n, ff), F32)],
        *chunks,
        *ws,
        scratch=[((4 * n, wide), BF), ((4 * n, cols), F32)],
    )


def pick_chunks(cot, scalars):
    n, wide = cot.shape[1:]

    def body(n_ref, x_ref, *o_refs):
        for r in range(4):
            o_refs[r][...] = x_ref[n_ref[1] ^ r]

    return call(body, [((n, wide), BF)] * 4, cot, scalars=scalars)


def feed_back(chunks, downs, a, b, w, scalars):
    n, wide = chunks[0].shape
    k = downs[0].shape[0]
    ff = 4 * k

    def body(n_ref, *refs):
        c_refs, d_refs = refs[:4], refs[4:8]
        a_ref, b_ref, w_ref, dw_ref, g_ref = refs[8:13]
        p_refs, all_ref, x_ref = refs[13:17], refs[17], refs[18]
        for r in range(4):
            dw_ref[turned(n_ref[2], r, k)] = d_refs[r][...]
            all_ref[r * n : (r + 1) * n] = c_refs[r][...]
        x_ref[...] = mm(all_ref[...], dw_ref[...], NT)
        for r in range(4):
            rows = slice(r * n, (r + 1) * n)
            x = x_ref[rows]
            g_ref[rows] = pair_up(x * a_ref[rows], x * b_ref[rows]).astype(BF)
        all_ref[...] = mm(g_ref[...], w_ref[...], NT).astype(BF)
        for r in range(4):
            p_refs[r][...] = all_ref[r * n : (r + 1) * n]

    return call(
        body,
        [((ff, wide), BF), ((4 * n, 2 * ff), BF)] + [((n, wide), BF)] * 4,
        *chunks,
        *downs,
        a,
        b,
        w,
        scalars=scalars,
        scratch=[((4 * n, wide), BF), ((4 * n, ff), F32)],
    )


def down_parts(hidden, w):
    rows = hidden.shape[0]
    n = rows // 4

    def body(h_ref, w_ref, *p_refs):
        for r in range(4):
            p_refs[r][...] = mm(h_ref[r * n : (r + 1) * n], w_ref[...]).astype(BF)

    return call(body, [((n, w.shape[1]), BF)] * 4, hidden, w)


def proj_rows(keep, got, gain_one, gain_two):
    rows, c = keep.shape

    def body(a_ref, b_ref, g_ref, h_ref, o_ref):
        o_ref[:rows] = (a_ref[...].astype(F32) + b_ref[...].astype(F32)).astype(BF)
        gains = [x[0:1, i * c : (i + 1) * c] for x in (g_ref, h_ref) for i in range(2)]
        o_ref[rows:] = jnp.concatenate(gains + [jnp.zeros((12, c), F32)], axis=0).astype(BF)

    return call(body, ((rows + 16, c), BF), keep, got, gain_one, gain_two)


def context_terms(chunks, ins, scalars):
    n, wide = chunks[0].shape[0] - 16, chunks[0].shape[1]
    c = ins[0].shape[1]
    half = n // 2

    def body(n_ref, *refs):
        c_refs, w_refs, keep_ref, give_ref, w_all, x_ref, all_ref = (
            refs[:4],
            refs[4:8],
            refs[8],
            refs[9],
            refs[10],
            refs[11],
            refs[12],
        )
        mine = pl.multiple_of(n_ref[0] * half, half)
        theirs = pl.multiple_of((1 - n_ref[0]) * half, half)
        for r in range(4):
            w_all[:, r * c : (r + 1) * c] = w_refs[r][:wide]
            all_ref[r * n : (r + 1) * n] = c_refs[r][:n]
        x_ref[...] = mm(all_ref[...], w_all[...]).astype(BF)
        for r in range(4):
            keep_ref[r] = x_ref[pl.ds(r * n + mine, half)]
            give_ref[r] = x_ref[pl.ds(r * n + theirs, half)]

    return call(
        body,
        [((4, half, 4 * c), BF)] * 2,
        *chunks,
        *ins,
        scalars=scalars,
        scratch=[((wide, 4 * c), BF), ((4 * n, 4 * c), BF), ((4 * n, wide), BF)],
    )


def both_terms(keep, got):
    half, feats = keep.shape[1:]

    def body(a_ref, b_ref, *o_refs):
        for r in range(4):
            o_refs[r][...] = (a_ref[r].astype(F32) + b_ref[r].astype(F32)).astype(BF)

    return call(body, [((half, feats), BF)] * 4, keep, got)


def in_parts(chunks, group, scalars):
    n, wide = chunks[0].shape[0] - 16, chunks[0].shape[1]
    c = group.shape[1] // 4

    def body(n_ref, *refs):
        c_refs, g_ref, o_refs, all_ref, hold = refs[:4], refs[4], refs[5:8], refs[8], refs[9]
        for r in range(4):
            all_ref[r * n : (r + 1) * n] = c_refs[r][:n]
        gains = sum(x[n:].astype(F32) for x in c_refs)
        for i in range(4):
            for k in range(2):
                row = gains[2 * k + i // 2 : 2 * k + i // 2 + 1, (i % 2) * c : (i % 2 + 1) * c]
                hold[i, k : k + 1] = row
            hold[i, 2:] = jnp.zeros((14, c), F32)
        x = mm(all_ref[...], g_ref[...], TN).astype(BF)
        for r in range(4):
            below = hold[n_ref[2] ^ r].astype(BF)
            put_part(
                o_refs, r, jnp.concatenate([x[:, r * c : (r + 1) * c], below], axis=0)
            )

    return call(
        body,
        parts_of(wide + 16, c),
        *chunks,
        group,
        scalars=scalars,
        scratch=[((4 * n, wide), BF), ((4, 16, c), F32)],
    )


def add(*parts, dtype=F32):
    def body(*refs):
        refs[-1][...] = total(refs[:-1]).astype(dtype)

    return call(body, (parts[0].shape, dtype), *parts)


def on_device(
    tokens, context, w_in, attn_gain, w_qkv, w_out, ffn_gain, w_gate_up, w_down, cotangent
):
    s = lax.axis_index("stream")
    t = lax.axis_index("t")
    d = lax.axis_index("d1")
    many = lax.axis_size("d2") > 1
    frames = tokens.shape[0]
    wide = tokens.shape[2]
    scalars = jnp.stack([s, t, d]).astype(jnp.int32)

    def near(w, axis=0):
        return lax.all_gather(w, "d2", axis=axis, tiled=True) if many else w

    def near_sum(g, axis=0):
        return lax.psum_scatter(g, "d2", scatter_dimension=axis, tiled=True) if many else g

    tokens = tokens[:, 0]
    cotangent = cotangent[:, 0]

    gains = jnp.concatenate([near(attn_gain[0]), near(ffn_gain[0])])
    some = gains.shape[0]
    in_mine = near(w_in, 1)
    in_mine = jnp.concatenate(
        [in_mine, jnp.pad(gains[None], ((0, 15), (0, in_mine.shape[1] - some)))]
    )
    fly = Flying()
    in_one, in_three = zhop(in_mine, 1), zhop(in_mine, 3)
    parts = pack_context(context, scalars)
    got = {r: hop(parts[r], r) for r in (3, 2, 1)}
    packed = pack_columns(tie(near(w_qkv[0]), parts[0]), 3)
    if 26 in SKIP:
        packed = tie(packed, in_three)
    qkv_mine = lax.all_to_all(packed, "t", 0, 0, tiled=True).reshape(-1, packed.shape[2])
    packed = pack_pairs(tie(near(w_gate_up[0]), qkv_mine))
    gu_mine = lax.all_to_all(packed, "t", 0, 0, tiled=True).reshape(-1, packed.shape[2])
    fly["gu"] = gu_mine
    own = tie(stack4([parts[0], got[1], got[2], got[3]]), qkv_mine)
    other = swap(own)
    in_two = zhop(opt(0, in_three, own), 1)
    ins = [in_mine, in_one, in_two, in_three]
    qkv_mine = beside(qkv_mine, near(w_out[0]))
    fly["qkv1"], fly["qkv3"] = zhop(qkv_mine, 1), zhop(qkv_mine, 3)
    group, parts = project(own, fly.due("group", other), ins, some, scalars)

    parts[0] = fly.due("parts0", parts[0])
    parts = collect(parts)
    proj_half = fly.due("half", half_sum(parts))
    start, mine, gains = first_norm(proj_half, swap(proj_half), parts, tokens, scalars)
    mine = fly.due("mine1", mine)
    by_x, by_y = hop(mine, 1), hop(mine, 2)
    fly["qkv2"] = zhop(opt(1, fly["qkv3"], mine), 1)
    by_y = fly.due("byy1", by_y)
    by_xy = corner(30, by_y, mine)
    gu_mine = opt(2, gu_mine, by_y)
    upper, lower = gu_mine[: gu_mine.shape[0] // 2], gu_mine[gu_mine.shape[0] // 2 :]
    whole = 37 in SKIP
    fly["gu1"], fly["up3"] = zhop(gu_mine, 1), zhop(gu_mine if whole else upper, 3)
    ws = [qkv_mine, fly["qkv1"], fly["qkv2"], fly["qkv3"]]
    chunks_one = [mine, by_x, by_y, fly.due("byxy1", by_xy)]
    q, kv, qkv_w = query_key_value(chunks_one, ws)
    if 36 in SKIP:
        cot = opt(3, cotangent, q)
        fly["coty"], fly["cotx"] = hop(cot, 2), hop(cot, 1)
    else:
        fly["cot"] = lax.all_to_all(
            jnp.broadcast_to(opt(3, cotangent, q)[None], (4, frames, wide)), "t", 0, 0, tiled=True
        )
    far = lax.ppermute(fly.due("kv", kv), "stream", [(0, 1)])
    if not whole:
        fly["low3"] = zhop(opt(4, lower, q), 3)
    mixed, w_own, out_w, *parts = attend(q, kv, far, ws, scalars)
    fly["up2"] = zhop(opt(5, fly["up3"], mixed), 1)
    parts[0] = fly.due("parts1", parts[0])
    parts = collect(parts)
    parts[0] = fly.due("mid", parts[0])
    middle, mine = second_norm(start, parts, gains, scalars)
    if not whole:
        fly["low2"] = zhop(opt(6, fly["low3"], middle), 1)
    if 36 in SKIP:
        fly["cotxy"] = corner(38, opt(39, fly["coty"], middle), cot)
    down_mine = near(w_down[0])
    fly["down1"] = zhop(opt(7, down_mine, middle), 1)

    mine = fly.due("mine2", mine)
    by_x, by_y = hop(mine, 1), hop(mine, 2)
    by_y = fly.due("byy2", by_y)
    by_xy = corner(31, by_y, mine)
    fly["down3"] = zhop(opt(8, down_mine, mine), 3)
    chunks_two = [mine, by_x, by_y, fly.due("byxy2", by_xy)]
    gus = [gu_mine, fly["gu1"], fly["up2"], fly["up3"]]
    if not whole:
        gus = [gu_mine, fly["gu1"], fly["up2"], fly["low2"], fly["up3"], fly["low3"]]
    gu_w, hidden, a, b = gate_and_up(chunks_two, gus)
    fly["down2"] = zhop(opt(9, fly["down3"], by_xy), 1)
    hidden = fly.due("hidden", hidden)
    if 36 in SKIP:
        cot = [cot, fly["cotx"], fly["coty"], fly["cotxy"]]
    else:
        cot = pick_chunks(fly["cot"].reshape(4, frames, wide), scalars)
    g = row_parts(hidden, cot, scalars)
    far_g = inward(opt(10, g[2], fly["down2"]))
    fly["g1"] = far_g
    downs = [down_mine, fly["down1"], fly["down2"], fly["down3"]]
    down_w, grad_gu, *parts = feed_back([opt(11, cot[0], g[0])] + cot[1:], downs, a, b, gu_w, scalars)
    u = weight_parts(chunks_two, opt(12, grad_gu, parts[0]))
    far_u = inward(u[2])
    fly["u1"] = far_u
    parts[0] = fly.due("parts2", parts[0])
    parts = collect(parts)
    parts[0] = fly.due("nb2", parts[0])
    far_g = across(for_far(g[2], opt(13, far_g, parts[0])))
    fly["g2"] = far_g
    grad_middle, gain_two, mine = norm_back(
        parts, middle, gains, 1, cotangent, scalars, False
    )
    mine = fly.due("mine3", mine)
    branch = [mine, hop(mine, 1), hop(mine, 2)]
    branch[2] = fly.due("byy3", branch[2])
    branch.append(fly.due("branch", corner(32, branch[2], mine)))
    near_g = zhop(for_near(g[1], opt(14, far_g, branch[3])), 1)
    fly["g3"] = near_g

    grad, back = attend_back(branch, out_w, w_own, q, kv, far)
    back = lax.ppermute(fly.due("back", back), "stream", [(1, 0)])
    parts = collect(down_parts(opt(15, hidden, branch[3]), down_w))
    result = add(middle, *parts)
    fly["result"] = result
    far_u = across(for_far(u[2], opt(16, far_u, back)))
    fly["u2"] = far_u
    grad_qkv, *parts = into_normed(grad, fly.due("into", back), qkv_w)
    parts[0] = fly.due("parts3", parts[0])
    h = attention_parts(chunks_one, opt(17, grad_qkv, parts[0]), mixed, branch, scalars)
    far_h = inward(h[2])
    fly["h1"] = far_h
    parts = collect(parts)
    parts[0] = fly.due("nb1", parts[0])
    grad_start, gain_one, keep, give = norm_back(
        parts, start, gains, 0, grad_middle, scalars, True
    )
    grad_proj = proj_rows(fly.due("keep", keep), swap(give), gain_one, gain_two)
    far_h = across(for_far(h[2], opt(18, far_h, grad_proj)))
    fly["h2"] = far_h
    gproj = [grad_proj, hop(grad_proj, 1), hop(grad_proj, 2)]
    gproj[2] = fly.due("gpy", gproj[2])
    gproj.append(fly.due("gproj", corner(33, gproj[2], grad_proj)))
    near_u = zhop(for_near(u[1], opt(19, far_u, gproj[3])), 1)
    fly["u3"] = near_u

    g_in = in_parts(gproj, group, scalars)
    far_in = inward(g_in[2])
    fly["in1"] = far_in
    keep, give = context_terms([opt(20, gproj[0], g_in[0])] + gproj[1:], ins, scalars)
    both = both_terms(keep, fly.due("both", swap(fly.due("give", give))))
    got = [both[0]] + [hop(both[r], r) for r in (1, 2, 3)]
    got = fly.due("got", stack4(got))
    blocks = finished_rows(u[0], near_u, opt(21, far_u, got), scalars)
    g_gu = [blocks[0]] + [hop(blocks[r], r) for r in (1, 2, 3)]
    far_in = across(for_far(g_in[2], opt(22, far_in, got)))
    fly["in2"] = far_in
    near_h = zhop(for_near(h[1], opt(23, far_h, got)), 1)
    fly["h3"] = near_h
    other = swap(got)
    g_gu[0] = fly.due("gu_out", g_gu[0])
    grad_gate_up = unpack_columns(g_gu, 2, scalars)
    near_in = zhop(for_near(g_in[1], opt(24, far_in, grad_gate_up)), 1)
    fly["in3"] = near_in
    *blocks, grad_out = finished_pair(h[0], near_h, opt(25, far_h, grad_gate_up), scalars)
    g_qkv = [blocks[0]] + [hop(blocks[r], r) for r in (1, 2, 3)]
    grad_context = unpack_context(got, fly.due("context", other), scalars)
    grad_gate_up = near_sum(grad_gate_up)
    grad_qkv = near_sum(unpack_columns(g_qkv, 3, scalars))
    grad_out = near_sum(grad_out)
    grad_down = near_sum(finished(g[0], near_g, fly["g2"]))
    grad_in, found = finished_in(g_in[0], near_in, far_in)
    grad_in = near_sum(grad_in, 1)
    found = lax.dynamic_slice_in_dim(found[:2], t * (some // 2), some // 2, 1)
    gains = near_sum(found, 1)
    return (
        result[:, None],
        grad_start[:, None],
        grad_context,
        grad_in,
        gains[:1],
        grad_qkv[None],
        grad_out[None],
        gains[1:],
        grad_gate_up[None],
        grad_down[None],
    )


def solution(mesh):
    n = mesh.shape["frames"]
    grid = Mesh(mesh.devices.reshape(2, 4, 4, n // 16), ("stream", "d1", "t", "d2"))
    f = ("d1", "t", "d2")
    return jax.shard_map(
        on_device,
        mesh=grid,
        in_specs=(
            P(f, "stream", None),
            P(f, None),
            P("stream", f),
            P("stream", f),
            P("stream", f, None),
            P("stream", f, None),
            P("stream", f),
            P("stream", f, None),
            P("stream", f, None),
            P(f, "stream", None),
        ),
        out_specs=(
            P(f, "stream", None),
            P(f, "stream", None),
            P(f, None),
            P("stream", f),
            P("stream", f),
            P("stream", f, None),
            P("stream", f, None),
            P("stream", f),
            P("stream", f, None),
            P("stream", f, None),
        ),
        check_vma=False,
    )
```

time: 526 us -> 299 us (0.57); the launches traced: 520 us -> 298 us
  waiting for transfers between devices: 267 us -> 135 us
  blocking collectives: 86.7 us -> 0 us
  starting transfers between devices: 54.1 us -> 104 us
  Pallas kernels: 0 us -> 48.1 us
  matrix products: 40.9 us -> 0 us
  local copies, waits for them, and re-layouts: 41.4 us -> 10.1 us
  between operations: 16 us -> 1.28 us
  other arithmetic: 13.9 us -> 0.17 us
    reduce_scatter x5 -> x0, waiting for transfers between devices: 131 us -> none  [sum_d(): lax.psum_scatter(g.astype(BF), 'd1', scatter_dimension=axis, tiled=True)]
    ppermute x38 -> x70, starting transfers between devices: 45.4 us -> 96.1 us  [the longest x42 51.4 us: hop(): return lax.ppermute(x, 't', [(i, i ^ r) for i in range(4)])]
    pallas_call x0 -> x42, Pallas kernels: none -> 48.1 us  [call(): pl.pallas_call(body, out_shape=shapes, in_specs=inside, out_specs=[pl.Blo...]
    ppermute x38 -> x70, waiting for transfers between devices: 83.7 us -> 130 us  [the longest x42 63.4 us: hop(): return lax.ppermute(x, 't', [(i, i ^ r) for i in range(4)])]
    unnamed x11 -> x0, waiting for transfers between devices: 45 us -> none
    unnamed x1 -> x0, blocking collectives: 42.1 us -> none
    dot_general x17 -> x0, matrix products: 40.9 us -> none  [the longest x15 37.7 us: dot(): return jnp.einsum(form, a, b, preferred_element_type=F32)]
    all_to_all x2 -> x0, blocking collectives: 24.8 us -> none  [columns_to_t(): return lax.all_to_all(w, 't', 0, 0, tiled=True).reshape(4 * rows, k * 4 * c)]
  transfers between devices with their start and end apart: 55 -> 77, of which waited for: 36 -> 35; matrix products, arithmetic and copies ran while one was open for 13% -> 1% of each run, Pallas kernels for 0% -> 14%
where the time goes in v3:
time: 299 us; the launch traced here: 298 us
  waiting for transfers between devices  135 us (45%)
  starting transfers between devices  104 us (35%)
  Pallas kernels  48.1 us (16%)
  local copies, waits for them, and re-layouts  10.1 us (3%)
    ppermute x42, waiting for transfers between devices, hop(): return lax.ppermute(x, 't', [(i, i ^ r) for i in range(4)])  63.4 us
    ppermute x42, starting transfers between devices, hop(): return lax.ppermute(x, 't', [(i, i ^ r) for i in range(4)])  51.4 us
    pallas_call x42, Pallas kernels, call(): pl.pallas_call(body, out_shape=shapes, in_specs=inside, out_specs=[pl.Blo...  48.1 us
    ppermute x18, waiting for transfers between devices, zhop(): return lax.ppermute(x, 'd1', [(i, i ^ r) for i in range(4)])  46.2 us
    ppermute x18, starting transfers between devices, zhop(): return lax.ppermute(x, 'd1', [(i, i ^ r) for i in range(4)])  27.7 us
    ppermute x4, waiting for transfers between devices, inward(): return lax.ppermute(x, 'd1', [(0, 1), (3, 2)])  19.2 us
    ppermute x4, starting transfers between devices, inward(): return lax.ppermute(x, 'd1', [(0, 1), (3, 2)])  10.3 us
    unnamed x74, local copies, waits for them, and re-layouts  9.42 us
  transfers between devices with their start and end apart: 77, of which 35 were waited for; matrix products, arithmetic and copies ran while one was open for 1% of the time, Pallas kernels for 14%

profile of v3, /device:TPU:0, one launch (start us, length us, event | category | flops | bytes accessed | tf_op | source)
XLA Modules:
  0.0 298.5 jit_solution(10618608958510345670)
XLA Ops:
  2.6 3.0 %collective-permute-start = (bf16[64,1024]{1,0:T(8,128)(2,1)S(1)}, bf16[64,1024]{1,0:T(8,128)(2,1)S(1)}, u32[]{:S(2)}, u32[]{:S(2)}) collective-permute-start(bf16[64,1024]{1,0:T(8,128)(2,1)S(1)} %get-tuple-element.137), channel_id=1, source_target_pairs={{0,1},{1,0},{2,3},{3,2},{4,5},{5,4},{6,7},{7,6},{8,9},{9,8},{10,11... | collective-permute-start | bytes 393224 | tf_op jit(solution)/shard_map/ppermute | solution.py:74
  5.6 1.5 collective-permute-start.1
  8.1 4.2 %all-to-all-start = ((bf16[4,64,768]{2,1,0:T(8,128)(2,1)}), bf16[4,64,768]{2,1,0:T(8,128)(2,1)S(1)}, u32[]{:S(2)}, u32[]{:S(2)}) async-start(bf16[4,64,768]{2,1,0:T(8,128)(2,1)} %shard_map.179), calls=%async_computation | async-start | bytes 786432 | tf_op jit(solution)/shard_map/all_to_all | solution.py:931
  12.3 3.7 %collective-permute-start.5 = (bf16[528,256]{1,0:T(8,128)(2,1)S(1)}, bf16[528,256]{1,0:T(8,128)(2,1)S(1)}, u32[]{:S(2)}, u32[]{:S(2)}) collective-permute-start(bf16[528,256]{1,0:T(8,128)(2,1)S(1)} %fusion.1.refs_0_.refs_4_), channel_id=1, source_target_pairs={{0,12},{4,8},{8,4},{12,0},{1,13},{5,9},{9,5},{13,1},{2,14},{6,10},... | collective-permute-start | bytes 811016 | tf_op jit(solution)/shard_map/ppermute | solution.py:78
  16.1 2.1 all-to-all-done
  18.2 1.6 collective-permute-start.4
  19.7 1.8 collective-permute-done.5.refs_3_.refs_7_
  21.6 5.4 %collective-permute-start.6 = (bf16[528,256]{1,0:T(8,128)(2,1)S(1)}, bf16[528,256]{1,0:T(8,128)(2,1)}, u32[]{:S(2)}, u32[]{:S(2)}) collective-permute-start(bf16[528,256]{1,0:T(8,128)(2,1)S(1)} %collective-permute-done.5.refs_3_.refs_7_), channel_id=1, source_target_pairs={{0,4},{4,0},{8,12},{12,8},{1,5},{5,1},{9,13},{13,9},{2,6},{6,2},{1... | collective-permute-start | bytes 811016 | tf_op jit(solution)/shard_map/ppermute | solution.py:78
  27.0 2.5 collective-permute-start.10
  30.9 3.9 %all-to-all-start.1 = ((bf16[4,64,1408]{2,1,0:T(8,128)(2,1)}), bf16[4,64,1408]{2,1,0:T(8,128)(2,1)S(1)}, u32[]{:S(2)}, u32[]{:S(2)}) async-start(bf16[4,64,1408]{2,1,0:T(8,128)(2,1)} %shard_map.182), calls=%async_computation.1 | async-start | bytes 1441792 | tf_op jit(solution)/shard_map/all_to_all | solution.py:933
  34.8 2.0 shard_map.180
  36.8 2.1 collective-permute-start.7
  38.9 1.8 collective-permute-start.8
  41.9 5.3 %collective-permute-done.7.b.refs_1_ = bf16[144,512]{1,0:T(8,128)(2,1)S(1)} collective-permute-done((bf16[144,512]{1,0:T(8,128)(2,1)S(1)}, bf16[144,512]{1,0:T(8,128)(2,1)S(1)}, u32[]{:S(2)}, u32[]{:S(2)}) %collective-permute-start.7) | collective-permute-done | bytes 147488 | tf_op jit(solution)/shard_map/ppermute | solution.py:74
  47.2 2.5 collective-permute-done.9.e.refs_3_
  53.0 4.5 %collective-permute-done.12.refs_5_.refs_1_ = bf16[256,1024]{1,0:T(8,128)(2,1)S(1)} collective-permute-done((bf16[256,1024]{1,0:T(8,128)(2,1)S(1)}, bf16[256,1024]{1,0:T(8,128)(2,1)S(1)}, u32[]{:S(2)}, u32[]{:S(2)}) %collective-permute-start.12) | collective-permute-done | bytes 524320 | tf_op jit(solution)/shard_map/ppermute | solution.py:78
  57.4 1.6 collective-permute-start.14
  59.0 6.7 %collective-permute-done.14.refs_2_ = bf16[128,1024]{1,0:T(8,128)(2,1)S(1)} collective-permute-done((bf16[128,1024]{1,0:T(8,128)(2,1)S(1)}, bf16[128,1024]{1,0:T(8,128)(2,1)S(1)}, u32[]{:S(2)}, u32[]{:S(2)}) %collective-permute-start.14) | collective-permute-done | bytes 262176 | tf_op jit(solution)/shard_map/ppermute | solution.py:74
  65.7 5.6 %collective-permute-done.15.refs_6_.refs_2_ = bf16[256,1024]{1,0:T(8,128)(2,1)S(1)} collective-permute-done((bf16[256,1024]{1,0:T(8,128)(2,1)S(1)}, bf16[256,1024]{1,0:T(8,128)(2,1)S(1)}, u32[]{:S(2)}, u32[]{:S(2)}) %collective-permute-start.15) | collective-permute-done | bytes 524320 | tf_op jit(solution)/shard_map/ppermute | solution.py:78
  75.0 9.6 %collective-permute-done.16.refs_3_ = bf16[128,1024]{1,0:T(8,128)(2,1)S(1)} collective-permute-done((bf16[128,1024]{1,0:T(8,128)(2,1)S(1)}, bf16[128,1024]{1,0:T(8,128)(2,1)S(1)}, u32[]{:S(2)}, u32[]{:S(2)}) %collective-permute-start.16) | collective-permute-done | bytes 262176 | tf_op jit(solution)/shard_map/ppermute | solution.py:74
  84.6 11.6 %collective-permute-done.17.refs_5_ = bf16[256,1408]{1,0:T(8,128)(2,1)S(1)} collective-permute-done((bf16[256,1408]{1,0:T(8,128)(2,1)S(1)}, bf16[256,1408]{1,0:T(8,128)(2,1)S(1)}, u32[]{:S(2)}, u32[]{:S(2)}) %collective-permute-start.17) | collective-permute-done | bytes 720928 | tf_op jit(solution)/shard_map/ppermute | solution.py:78
  102.6 2.5 collective-permute-start.22
  106.1 4.7 %collective-permute-done.20.refs_9_ = bf16[128,1408]{1,0:T(8,128)(2,1)S(1)} collective-permute-done((bf16[128,1408]{1,0:T(8,128)(2,1)S(1)}, bf16[128,1408]{1,0:T(8,128)(2,1)S(1)}, u32[]{:S(2)}, u32[]{:S(2)}) %collective-permute-start.20) | collective-permute-done | bytes 360480 | tf_op jit(solution)/shard_map/ppermute | solution.py:78
  111.8 5.7 %collective-permute-done.23.e = bf16[128,1024]{1,0:T(8,128)(2,1)S(1)} collective-permute-done((bf16[128,1024]{1,0:T(8,128)(2,1)S(1)}, bf16[128,1024]{1,0:T(8,128)(2,1)S(1)}, u32[]{:S(2)}, u32[]{:S(2)}) %collective-permute-start.23) | collective-permute-done | bytes 262176 | tf_op jit(solution)/shard_map/ppermute | solution.py:74
  119.1 2.2 collective-permute-start.30
  121.6 11.4 %collective-permute-done.26.refs_6_ = bf16[128,1408]{1,0:T(8,128)(2,1)S(1)} collective-permute-done((bf16[128,1408]{1,0:T(8,128)(2,1)S(1)}, bf16[128,1408]{1,0:T(8,128)(2,1)S(1)}, u32[]{:S(2)}, u32[]{:S(2)}) %collective-permute-start.26) | collective-permute-done | bytes 360480 | tf_op jit(solution)/shard_map/ppermute | solution.py:78
  133.1 2.0 collective-permute-start.24
  135.1 2.0 collective-permute-start.33
  137.1 5.0 %collective-permute-done.28.refs_3_ = bf16[128,1024]{1,0:T(8,128)(2,1)S(1)} collective-permute-done((bf16[128,1024]{1,0:T(8,128)(2,1)S(1)}, bf16[128,1024]{1,0:T(8,128)(2,1)S(1)}, u32[]{:S(2)}, u32[]{:S(2)}) %collective-permute-start.28) | collective-permute-done | bytes 262176 | tf_op jit(solution)/shard_map/ppermute | solution.py:74
  142.2 2.8 collective-permute-done.24.refs_1_
  145.0 2.1 shard_map.188
  147.8 2.8 collective-permute-done.33.refs_3_
  150.6 1.6 shard_map.189
  153.5 3.5 %shard_map.190 = (bf16[704,1024]{1,0:T(8,128)(2,1)S(1)}, bf16[512,1408]{1,0:T(8,128)(2,1)S(1)}, bf16[128,1024]{1,0:T(8,128)(2,1)S(1)}, bf16[128,1024]{1,0:T(8,12...) custom-call(s32[3]{0:T(128)S(1)} %pad_add_fusion.n_ref, bf16[128,1024]{1,0:T(8,128)(2,1)S(1)} %bitcast.36, ...), custom_call_target="tpu_custom_call" | custom-call | flops 3000000000 | bytes 5000000 | tf_op jit(solution)/shard_map/pallas_call | solution.py:104
  158.5 2.1 collective-permute-start.38
  160.6 1.9 collective-permute-done.35.b_ref
  165.0 4.5 %collective-permute-done.38.e = bf16[128,1024]{1,0:T(8,128)(2,1)S(1)} collective-permute-done((bf16[128,1024]{1,0:T(8,128)(2,1)S(1)}, bf16[128,1024]{1,0:T(8,128)(2,1)S(1)}, u32[]{:S(2)}, u32[]{:S(2)}) %collective-permute-start.38) | collective-permute-done | bytes 262176 | tf_op jit(solution)/shard_map/ppermute | solution.py:74
  170.5 2.9 collective-permute-start.39
  173.4 1.9 shard_map.197
  178.1 2.7 collective-permute-done.39.refs_3_.refs_9_
  181.8 2.3 collective-permute-start.41
  188.4 4.8 %collective-permute-done.42.refs_3_ = bf16[128,1024]{1,0:T(8,128)(2,1)S(1)} collective-permute-done((bf16[128,1024]{1,0:T(8,128)(2,1)S(1)}, bf16[128,1024]{1,0:T(8,128)(2,1)S(1)}, u32[]{:S(2)}, u32[]{:S(2)}) %collective-permute-start.42) | collective-permute-done | bytes 262176 | tf_op jit(solution)/shard_map/ppermute | solution.py:74
  196.0 2.0 collective-permute-start.50
  199.1 1.9 shard_map.200
  201.9 5.1 %collective-permute-start.54 = (bf16[512,1024]{1,0:T(8,128)(2,1)S(1)}, bf16[512,1024]{1,0:T(8,128)(2,1)S(1)}, u32[]{:S(2)}, u32[]{:S(2)}) collective-permute-start(bf16[512,1024]{1,0:T(8,128)(2,1)S(1)} %get-tuple-element.220.a_ref), channel_id=1, source_target_pairs={{0,4},{12,8},{1,5},{13,9},{2,6},{14,10},{3,7},{15,11},{16,20},{28,... | collective-permute-start | bytes 3145736 | tf_op jit(solution)/shard_map/ppermute | solution.py:82
  211.6 2.0 collective-permute-start.52
  213.6 15.5 %collective-permute-done.54.b_ref = bf16[512,1024]{1,0:T(8,128)(2,1)S(1)} collective-permute-done((bf16[512,1024]{1,0:T(8,128)(2,1)S(1)}, bf16[512,1024]{1,0:T(8,128)(2,1)S(1)}, u32[]{:S(2)}, u32[]{:S(2)}) %collective-permute-start.54) | collective-permute-done | bytes 1048608 | tf_op jit(solution)/shard_map/ppermute | solution.py:82
  231.6 1.6 collective-permute-start.62
  237.4 2.8 collective-permute-start.58
  240.2 2.5 shard_map.203
  245.9 2.0 shard_map.218
  249.2 2.5 collective-permute-start.63
  259.4 2.8 collective-permute-done.60.refs_2_
  262.3 1.8 collective-permute-done.63.b_ref
  264.9 1.7 shard_map.211
  270.1 2.0 shard_map.209
  272.2 2.7 collective-permute-done.67.b_ref
  274.9 3.3 %collective-permute-done.69.refs_2_ = bf16[64,1408]{1,0:T(8,128)(2,1)S(1)} collective-permute-done((bf16[64,1408]{1,0:T(8,128)(2,1)S(1)}, bf16[64,1408]{1,0:T(8,128)(2,1)S(1)}, u32[]{:S(2)}, u32[]{:S(2)}) %collective-permute-start.69) | collective-permute-done | bytes 180256 | tf_op jit(solution)/shard_map/ppermute | solution.py:74
  278.2 2.3 shard_map.213
  280.4 2.3 shard_map.216
  284.5 1.7 collective-permute-start.74
  286.3 5.1 %collective-permute-start.71 = (bf16[528,256]{1,0:T(8,128)(2,1)S(1)}, bf16[528,256]{1,0:T(8,128)(2,1)S(1)}, u32[]{:S(2)}, u32[]{:S(2)}) collective-permute-start(bf16[528,256]{1,0:T(8,128)(2,1)S(1)} %shard_map.214), channel_id=1, source_target_pairs={{0,4},{4,0},{8,12},{12,8},{1,5},{5,1},{9,13},{13,9},{2,6},{6,2},{1... | collective-permute-start | bytes 811016 | tf_op jit(solution)/shard_map/ppermute | solution.py:78
  291.5 1.6 shard_map.217
  293.1 3.9 %collective-permute-done.71.b_ref = bf16[528,256]{1,0:T(8,128)(2,1)S(1)} collective-permute-done((bf16[528,256]{1,0:T(8,128)(2,1)S(1)}, bf16[528,256]{1,0:T(8,128)(2,1)S(1)}, u32[]{:S(2)}, u32[]{:S(2)}) %collective-permute-start.71) | collective-permute-done | bytes 270368 | tf_op jit(solution)/shard_map/ppermute | solution.py:78
  (213 shorter events, 73.8 us)
Async XLA Ops:
  2.6 13.4 %collective-permute-start = (bf16[64,1024]{1,0:T(8,128)(2,1)S(1)}, bf16[64,1024]{1,0:T(8,128)(2,1)S(1)}, u32[]{:S(2)}, u32[]{:S(2)}) collective-permute-start(bf16[64,1024]{1,0:T(8,128)(2,1)S(1)} %get-tuple-element.137), channel_id=1, source_target_pairs={{0,1},{1,0},{2,3},{3,2},{4,5},{5,4},{6,7},{7,6},{8,9},{9,8},{10,11... | collective-permute-start | bytes 393224 | tf_op jit(solution)/shard_map/ppermute | solution.py:74
  5.6 10.4 %collective-permute-start.1 = (bf16[64,1024]{1,0:T(8,128)(2,1)S(1)}, bf16[64,1024]{1,0:T(8,128)(2,1)S(1)}, u32[]{:S(2)}, u32[]{:S(2)}) collective-permute-start(bf16[64,1024]{1,0:T(8,128)(2,1)S(1)} %get-tuple-element.138), channel_id=1, source_target_pairs={{0,2},{1,3},{2,0},{3,1},{4,6},{5,7},{6,4},{7,5},{8,10},{9,11},{10,... | collective-permute-start | bytes 393224 | tf_op jit(solution)/shard_map/ppermute | solution.py:74
  7.1 8.9 %collective-permute-start.2 = (bf16[64,1024]{1,0:T(8,128)(2,1)S(1)}, bf16[64,1024]{1,0:T(8,128)(2,1)S(1)}, u32[]{:S(2)}, u32[]{:S(2)}) collective-permute-start(bf16[64,1024]{1,0:T(8,128)(2,1)S(1)} %get-tuple-element.139), channel_id=1, source_target_pairs={{0,3},{1,2},{2,1},{3,0},{4,7},{5,6},{6,5},{7,4},{8,11},{9,10},{10,... | collective-permute-start | bytes 393224 | tf_op jit(solution)/shard_map/ppermute | solution.py:74
  8.1 10.1 %all-to-all-start = ((bf16[4,64,768]{2,1,0:T(8,128)(2,1)}), bf16[4,64,768]{2,1,0:T(8,128)(2,1)S(1)}, u32[]{:S(2)}, u32[]{:S(2)}) async-start(bf16[4,64,768]{2,1,0:T(8,128)(2,1)} %shard_map.179), calls=%async_computation | async-start | bytes 786432 | tf_op jit(solution)/shard_map/all_to_all | solution.py:931
  12.3 9.2 %collective-permute-start.5 = (bf16[528,256]{1,0:T(8,128)(2,1)S(1)}, bf16[528,256]{1,0:T(8,128)(2,1)S(1)}, u32[]{:S(2)}, u32[]{:S(2)}) collective-permute-start(bf16[528,256]{1,0:T(8,128)(2,1)S(1)} %fusion.1.refs_0_.refs_4_), channel_id=1, source_target_pairs={{0,12},{4,8},{8,4},{12,0},{1,13},{5,9},{9,5},{13,1},{2,14},{6,10},... | collective-permute-start | bytes 811016 | tf_op jit(solution)/shard_map/ppermute | solution.py:78
  18.1 16.6 %collective-permute-start.3 = (bf16[4,64,1024]{2,1,0:T(8,128)(2,1)S(1)}, bf16[4,64,1024]{2,1,0:T(8,128)(2,1)}, u32[]{:S(2)}, u32[]{:S(2)}) collective-permute-start(bf16[4,64,1024]{2,1,0:T(8,128)(2,1)S(1)} %shard_map.178.a_ref), channel_id=1, source_target_pairs={{0,16},{16,0},{1,17},{17,1},{2,18},{18,2},{3,19},{19,3},{4,20},{20... | collective-permute-start | bytes 1572872 | tf_op jit(solution)/shard_map/ppermute | solution.py:90
  18.2 16.6 %collective-permute-start.4 = (bf16[528,256]{1,0:T(8,128)(2,1)S(1)}, bf16[528,256]{1,0:T(8,128)(2,1)S(1)}, u32[]{:S(2)}, u32[]{:S(2)}) collective-permute-start(bf16[528,256]{1,0:T(8,128)(2,1)S(1)} %fusion.1.refs_0_.refs_4_), channel_id=1, source_target_pairs={{0,4},{4,0},{8,12},{12,8},{1,5},{5,1},{9,13},{13,9},{2,6},{6,2},{1... | collective-permute-start | bytes 811016 | tf_op jit(solution)/shard_map/ppermute | solution.py:78
  21.6 13.2 %collective-permute-start.6 = (bf16[528,256]{1,0:T(8,128)(2,1)S(1)}, bf16[528,256]{1,0:T(8,128)(2,1)}, u32[]{:S(2)}, u32[]{:S(2)}) collective-permute-start(bf16[528,256]{1,0:T(8,128)(2,1)S(1)} %collective-permute-done.5.refs_3_.refs_7_), channel_id=1, source_target_pairs={{0,4},{4,0},{8,12},{12,8},{1,5},{5,1},{9,13},{13,9},{2,6},{6,2},{1... | collective-permute-start | bytes 811016 | tf_op jit(solution)/shard_map/ppermute | solution.py:78
  27.0 22.8 %collective-permute-start.10 = (bf16[256,1024]{1,0:T(8,128)(2,1)S(1)}, bf16[256,1024]{1,0:T(8,128)(2,1)S(1)}, u32[]{:S(2)}, u32[]{:S(2)}) collective-permute-start(bf16[256,1024]{1,0:T(8,128)(2,1)S(1)} %shard_map.183.refs_4_.refs_0_), channel_id=1, source_target_pairs={{0,12},{4,8},{8,4},{12,0},{1,13},{5,9},{9,5},{13,1},{2,14},{6,10},... | collective-permute-start | bytes 1572872 | tf_op jit(solution)/shard_map/ppermute | solution.py:78
  30.9 19.0 %all-to-all-start.1 = ((bf16[4,64,1408]{2,1,0:T(8,128)(2,1)}), bf16[4,64,1408]{2,1,0:T(8,128)(2,1)S(1)}, u32[]{:S(2)}, u32[]{:S(2)}) async-start(bf16[4,64,1408]{2,1,0:T(8,128)(2,1)} %shard_map.182), calls=%async_computation.1 | async-start | bytes 1441792 | tf_op jit(solution)/shard_map/all_to_all | solution.py:933
  36.8 10.5 %collective-permute-start.7 = (bf16[144,512]{1,0:T(8,128)(2,1)S(1)}, bf16[144,512]{1,0:T(8,128)(2,1)S(1)}, u32[]{:S(2)}, u32[]{:S(2)}) collective-permute-start(bf16[144,512]{1,0:T(8,128)(2,1)S(1)} %get-tuple-element.144), channel_id=1, source_target_pairs={{0,1},{1,0},{2,3},{3,2},{4,5},{5,4},{6,7},{7,6},{8,9},{9,8},{10,11... | collective-permute-start | bytes 442376 | tf_op jit(solution)/shard_map/ppermute | solution.py:74
  38.9 8.4 %collective-permute-start.8 = (bf16[144,512]{1,0:T(8,128)(2,1)S(1)}, bf16[144,512]{1,0:T(8,128)(2,1)S(1)}, u32[]{:S(2)}, u32[]{:S(2)}) collective-permute-start(bf16[144,512]{1,0:T(8,128)(2,1)S(1)} %get-tuple-element.145), channel_id=1, source_target_pairs={{0,2},{1,3},{2,0},{3,1},{4,6},{5,7},{6,4},{7,5},{8,10},{9,11},{10,... | collective-permute-start | bytes 442376 | tf_op jit(solution)/shard_map/ppermute | solution.py:74
  40.7 9.1 %collective-permute-start.9 = (bf16[144,512]{1,0:T(8,128)(2,1)S(1)}, bf16[144,512]{1,0:T(8,128)(2,1)S(1)}, u32[]{:S(2)}, u32[]{:S(2)}) collective-permute-start(bf16[144,512]{1,0:T(8,128)(2,1)S(1)} %get-tuple-element.146), channel_id=1, source_target_pairs={{0,3},{1,2},{2,1},{3,0},{4,7},{5,6},{6,5},{7,4},{8,11},{9,10},{10,... | collective-permute-start | bytes 442376 | tf_op jit(solution)/shard_map/ppermute | solution.py:74
  40.7 16.8 %collective-permute-start.12 = (bf16[256,1024]{1,0:T(8,128)(2,1)S(1)}, bf16[256,1024]{1,0:T(8,128)(2,1)S(1)}, u32[]{:S(2)}, u32[]{:S(2)}) collective-permute-start(bf16[256,1024]{1,0:T(8,128)(2,1)S(1)} %shard_map.183.refs_4_.refs_0_), channel_id=1, source_target_pairs={{0,4},{4,0},{8,12},{12,8},{1,5},{5,1},{9,13},{13,9},{2,6},{6,2},{1... | collective-permute-start | bytes 1572872 | tf_op jit(solution)/shard_map/ppermute | solution.py:78
  57.4 13.8 %collective-permute-start.15 = (bf16[256,1024]{1,0:T(8,128)(2,1)S(1)}, bf16[256,1024]{1,0:T(8,128)(2,1)S(1)}, u32[]{:S(2)}, u32[]{:S(2)}) collective-permute-start(bf16[256,1024]{1,0:T(8,128)(2,1)S(1)} %collective-permute-done.10.refs_7_.refs_3_), channel_id=1, source_target_pairs={{0,4},{4,0},{8,12},{12,8},{1,5},{5,1},{9,13},{13,9},{2,6},{6,2},{1... | collective-permute-start | bytes 1572872 | tf_op jit(solution)/shard_map/ppermute | solution.py:78
  57.4 8.2 %collective-permute-start.14 = (bf16[128,1024]{1,0:T(8,128)(2,1)S(1)}, bf16[128,1024]{1,0:T(8,128)(2,1)S(1)}, u32[]{:S(2)}, u32[]{:S(2)}) collective-permute-start(bf16[128,1024]{1,0:T(8,128)(2,1)S(1)} %get-tuple-element.151.refs_0_), channel_id=1, source_target_pairs={{0,2},{1,3},{2,0},{3,1},{4,6},{5,7},{6,4},{7,5},{8,10},{9,11},{10,... | collective-permute-start | bytes 786440 | tf_op jit(solution)/shard_map/ppermute | solution.py:74
  71.3 24.9 %collective-permute-start.17 = (bf16[256,1408]{1,0:T(8,128)(2,1)S(1)}, bf16[256,1408]{1,0:T(8,128)(2,1)S(1)}, u32[]{:S(2)}, u32[]{:S(2)}) collective-permute-start(bf16[256,1408]{1,0:T(8,128)(2,1)S(1)} %bitcast.21), channel_id=1, source_target_pairs={{0,4},{4,0},{8,12},{12,8},{1,5},{5,1},{9,13},{13,9},{2,6},{6,2},{1... | collective-permute-start | bytes 2162696 | tf_op jit(solution)/shard_map/ppermute | solution.py:78
  71.6 24.7 %collective-permute-start.13 = (bf16[128,1024]{1,0:T(8,128)(2,1)S(1)}, bf16[128,1024]{1,0:T(8,128)(2,1)S(1)}, u32[]{:S(2)}, u32[]{:S(2)}) collective-permute-start(bf16[128,1024]{1,0:T(8,128)(2,1)S(1)} %get-tuple-element.151.refs_0_), channel_id=1, source_target_pairs={{0,1},{1,0},{2,3},{3,2},{4,5},{5,4},{6,7},{7,6},{8,9},{9,8},{10,11... | collective-permute-start | bytes 786440 | tf_op jit(solution)/shard_map/ppermute | solution.py:74
  72.8 11.8 %collective-permute-start.16 = (bf16[128,1024]{1,0:T(8,128)(2,1)S(1)}, bf16[128,1024]{1,0:T(8,128)(2,1)S(1)}, u32[]{:S(2)}, u32[]{:S(2)}) collective-permute-start(bf16[128,1024]{1,0:T(8,128)(2,1)S(1)} %collective-permute-done.14.refs_2_), channel_id=1, source_target_pairs={{0,1},{1,0},{2,3},{3,2},{4,5},{5,4},{6,7},{7,6},{8,9},{9,8},{10,11... | collective-permute-start | bytes 786440 | tf_op jit(solution)/shard_map/ppermute | solution.py:74
  73.7 24.6 %collective-permute-start.18 = (bf16[128,1408]{1,0:T(8,128)(2,1)S(1)}, bf16[128,1408]{1,0:T(8,128)(2,1)S(1)}, u32[]{:S(2)}, u32[]{:S(2)}) collective-permute-start(bf16[128,1408]{1,0:T(8,128)(2,1)S(1)} %get-tuple-element.273), channel_id=1, source_target_pairs={{0,12},{4,8},{8,4},{12,0},{1,13},{5,9},{9,5},{13,1},{2,14},{6,10},... | collective-permute-start | bytes 1081352 | tf_op jit(solution)/shard_map/ppermute | solution.py:78
  99.6 11.1 %collective-permute-start.20 = (bf16[128,1408]{1,0:T(8,128)(2,1)S(1)}, bf16[128,1408]{1,0:T(8,128)(2,1)S(1)}, u32[]{:S(2)}, u32[]{:S(2)}) collective-permute-start(bf16[128,1408]{1,0:T(8,128)(2,1)S(1)} %get-tuple-element.160), channel_id=1, source_target_pairs={{0,12},{4,8},{8,4},{12,0},{1,13},{5,9},{9,5},{13,1},{2,14},{6,10},... | collective-permute-start | bytes 1081352 | tf_op jit(solution)/shard_map/ppermute | solution.py:78
  102.5 9.3 %collective-permute-start.21 = (bf16[128,1024]{1,0:T(8,128)(2,1)S(1)}, bf16[128,1024]{1,0:T(8,128)(2,1)S(1)}, u32[]{:S(2)}, u32[]{:S(2)}) collective-permute-start(bf16[128,1024]{1,0:T(8,128)(2,1)S(1)} %get-tuple-element.162), channel_id=1, source_target_pairs={{0,1},{1,0},{2,3},{3,2},{4,5},{5,4},{6,7},{7,6},{8,9},{9,8},{10,11... | collective-permute-start | bytes 786440 | tf_op jit(solution)/shard_map/ppermute | solution.py:74
  102.6 9.2 %collective-permute-start.22 = (bf16[128,1024]{1,0:T(8,128)(2,1)S(1)}, bf16[128,1024]{1,0:T(8,128)(2,1)S(1)}, u32[]{:S(2)}, u32[]{:S(2)}) collective-permute-start(bf16[128,1024]{1,0:T(8,128)(2,1)S(1)} %get-tuple-element.163), channel_id=1, source_target_pairs={{0,2},{1,3},{2,0},{3,1},{4,6},{5,7},{6,4},{7,5},{8,10},{9,11},{10,... | collective-permute-start | bytes 786440 | tf_op jit(solution)/shard_map/ppermute | solution.py:74
  105.1 12.3 %collective-permute-start.23 = (bf16[128,1024]{1,0:T(8,128)(2,1)S(1)}, bf16[128,1024]{1,0:T(8,128)(2,1)S(1)}, u32[]{:S(2)}, u32[]{:S(2)}) collective-permute-start(bf16[128,1024]{1,0:T(8,128)(2,1)S(1)} %get-tuple-element.164), channel_id=1, source_target_pairs={{0,3},{1,2},{2,1},{3,0},{4,7},{5,6},{6,5},{7,4},{8,11},{9,10},{10,... | collective-permute-start | bytes 786440 | tf_op jit(solution)/shard_map/ppermute | solution.py:74
  106.1 15.2 %collective-permute-start.27 = (bf16[176,1024]{1,0:T(8,128)(2,1)S(1)}, bf16[176,1024]{1,0:T(8,128)(2,1)S(1)}, u32[]{:S(2)}, u32[]{:S(2)}) collective-permute-start(bf16[176,1024]{1,0:T(8,128)(2,1)S(1)} %bitcast.29), channel_id=1, source_target_pairs={{0,4},{4,0},{8,12},{12,8},{1,5},{5,1},{9,13},{13,9},{2,6},{6,2},{1... | collective-permute-start | bytes 1081352 | tf_op jit(solution)/shard_map/ppermute | solution.py:78
  110.7 22.3 %collective-permute-start.26 = (bf16[128,1408]{1,0:T(8,128)(2,1)S(1)}, bf16[128,1408]{1,0:T(8,128)(2,1)S(1)}, u32[]{:S(2)}, u32[]{:S(2)}) collective-permute-start(bf16[128,1408]{1,0:T(8,128)(2,1)S(1)} %collective-permute-done.18.refs_8_), channel_id=1, source_target_pairs={{0,4},{4,0},{8,12},{12,8},{1,5},{5,1},{9,13},{13,9},{2,6},{6,2},{1... | collective-permute-start | bytes 1081352 | tf_op jit(solution)/shard_map/ppermute | solution.py:78
  118.2 14.8 %collective-permute-start.25 = (bf16[128,1024]{1,0:T(8,128)(2,1)S(1)}, bf16[128,1024]{1,0:T(8,128)(2,1)S(1)}, u32[]{:S(2)}, u32[]{:S(2)}) collective-permute-start(bf16[128,1024]{1,0:T(8,128)(2,1)S(1)} %get-tuple-element.167.refs_0_), channel_id=1, source_target_pairs={{0,2},{1,3},{2,0},{3,1},{4,6},{5,7},{6,4},{7,5},{8,10},{9,11},{10,... | collective-permute-start | bytes 786440 | tf_op jit(solution)/shard_map/ppermute | solution.py:74
  119.1 16.0 %collective-permute-start.30 = (bf16[176,1024]{1,0:T(8,128)(2,1)S(1)}, bf16[176,1024]{1,0:T(8,128)(2,1)S(1)}, u32[]{:S(2)}, u32[]{:S(2)}) collective-permute-start(bf16[176,1024]{1,0:T(8,128)(2,1)S(1)} %bitcast.30), channel_id=1, source_target_pairs={{0,12},{4,8},{8,4},{12,0},{1,13},{5,9},{9,5},{13,1},{2,14},{6,10},... | collective-permute-start | bytes 1081352 | tf_op jit(solution)/shard_map/ppermute | solution.py:78
  121.3 20.9 %collective-permute-start.29 = (bf16[128,1408]{1,0:T(8,128)(2,1)S(1)}, bf16[128,1408]{1,0:T(8,128)(2,1)S(1)}, u32[]{:S(2)}, u32[]{:S(2)}) collective-permute-start(bf16[128,1408]{1,0:T(8,128)(2,1)S(1)} %collective-permute-done.20.refs_9_), channel_id=1, source_target_pairs={{0,4},{4,0},{8,12},{12,8},{1,5},{5,1},{9,13},{13,9},{2,6},{6,2},{1... | collective-permute-start | bytes 1081352 | tf_op jit(solution)/shard_map/ppermute | solution.py:78
  121.3 13.8 %collective-permute-start.32 = (bf16[128,1024]{1,0:T(8,128)(2,1)S(1)}, bf16[128,1024]{1,0:T(8,128)(2,1)S(1)}, u32[]{:S(2)}, u32[]{:S(2)}) collective-permute-start(bf16[128,1024]{1,0:T(8,128)(2,1)S(1)} %bitcast.33), channel_id=1, source_target_pairs={{0,2},{1,3},{2,0},{3,1},{4,6},{5,7},{6,4},{7,5},{8,10},{9,11},{10,... | collective-permute-start | bytes 786440 | tf_op jit(solution)/shard_map/ppermute | solution.py:74
  133.1 9.1 %collective-permute-start.28 = (bf16[128,1024]{1,0:T(8,128)(2,1)S(1)}, bf16[128,1024]{1,0:T(8,128)(2,1)S(1)}, u32[]{:S(2)}, u32[]{:S(2)}) collective-permute-start(bf16[128,1024]{1,0:T(8,128)(2,1)S(1)} %collective-permute-done.25.refs_2_), channel_id=1, source_target_pairs={{0,1},{1,0},{2,3},{3,2},{4,5},{5,4},{6,7},{7,6},{8,9},{9,8},{10,11... | collective-permute-start | bytes 786440 | tf_op jit(solution)/shard_map/ppermute | solution.py:74
  133.1 11.9 %collective-permute-start.24 = (bf16[128,1024]{1,0:T(8,128)(2,1)S(1)}, bf16[128,1024]{1,0:T(8,128)(2,1)S(1)}, u32[]{:S(2)}, u32[]{:S(2)}) collective-permute-start(bf16[128,1024]{1,0:T(8,128)(2,1)S(1)} %get-tuple-element.167.refs_0_), channel_id=1, source_target_pairs={{0,1},{1,0},{2,3},{3,2},{4,5},{5,4},{6,7},{7,6},{8,9},{9,8},{10,11... | collective-permute-start | bytes 786440 | tf_op jit(solution)/shard_map/ppermute | solution.py:74
  135.1 12.7 %collective-permute-start.31 = (bf16[128,1024]{1,0:T(8,128)(2,1)S(1)}, bf16[128,1024]{1,0:T(8,128)(2,1)S(1)}, u32[]{:S(2)}, u32[]{:S(2)}) collective-permute-start(bf16[128,1024]{1,0:T(8,128)(2,1)S(1)} %bitcast.34), channel_id=1, source_target_pairs={{0,1},{1,0},{2,3},{3,2},{4,5},{5,4},{6,7},{7,6},{8,9},{9,8},{10,11... | collective-permute-start | bytes 786440 | tf_op jit(solution)/shard_map/ppermute | solution.py:74
  135.1 15.4 %collective-permute-start.33 = (bf16[128,1024]{1,0:T(8,128)(2,1)S(1)}, bf16[128,1024]{1,0:T(8,128)(2,1)S(1)}, u32[]{:S(2)}, u32[]{:S(2)}) collective-permute-start(bf16[128,1024]{1,0:T(8,128)(2,1)S(1)} %collective-permute-done.32.refs_2_), channel_id=1, source_target_pairs={{0,1},{1,0},{2,3},{3,2},{4,5},{5,4},{6,7},{7,6},{8,9},{9,8},{10,11... | collective-permute-start | bytes 786440 | tf_op jit(solution)/shard_map/ppermute | solution.py:74
  142.2 10.0 %collective-permute-start.34 = (bf16[176,1024]{1,0:T(8,128)(2,1)S(1)}, bf16[176,1024]{1,0:T(8,128)(2,1)S(1)}, u32[]{:S(2)}, u32[]{:S(2)}) collective-permute-start(bf16[176,1024]{1,0:T(8,128)(2,1)S(1)} %collective-permute-done.30.refs_7_), channel_id=1, source_target_pairs={{0,4},{4,0},{8,12},{12,8},{1,5},{5,1},{9,13},{13,9},{2,6},{6,2},{1... | collective-permute-start | bytes 1081352 | tf_op jit(solution)/shard_map/ppermute | solution.py:78
  152.2 10.4 %collective-permute-start.35 = (bf16[352,1024]{1,0:T(8,128)(2,1)S(1)}, bf16[352,1024]{1,0:T(8,128)(2,1)S(1)}, u32[]{:S(2)}, u32[]{:S(2)}) collective-permute-start(bf16[352,1024]{1,0:T(8,128)(2,1)S(1)} %get-tuple-element.184.a_ref), channel_id=1, source_target_pairs={{0,4},{12,8},{1,5},{13,9},{2,6},{14,10},{3,7},{15,11},{16,20},{28,... | collective-permute-start | bytes 2162696 | tf_op jit(solution)/shard_map/ppermute | solution.py:82
  158.5 10.9 %collective-permute-start.38 = (bf16[128,1024]{1,0:T(8,128)(2,1)S(1)}, bf16[128,1024]{1,0:T(8,128)(2,1)S(1)}, u32[]{:S(2)}, u32[]{:S(2)}) collective-permute-start(bf16[128,1024]{1,0:T(8,128)(2,1)S(1)} %get-tuple-element.188), channel_id=1, source_target_pairs={{0,3},{1,2},{2,1},{3,0},{4,7},{5,6},{6,5},{7,4},{8,11},{9,10},{10,... | collective-permute-start | bytes 786440 | tf_op jit(solution)/shard_map/ppermute | solution.py:74
  162.7 18.1 %collective-permute-start.40 = (bf16[352,1024]{1,0:T(8,128)(2,1)S(1)}, bf16[352,1024]{1,0:T(8,128)(2,1)S(1)}, u32[]{:S(2)}, u32[]{:S(2)}) collective-permute-start(bf16[352,1024]{1,0:T(8,128)(2,1)S(1)} %shard_map.192), channel_id=1, source_target_pairs={{4,8},{8,4},{5,9},{9,5},{6,10},{10,6},{7,11},{11,7},{20,24},{24,20... | collective-permute-start | bytes 2162696 | tf_op jit(solution)/shard_map/ppermute | solution.py:86
  170.5 10.3 %collective-permute-start.39 = (bf16[128,1024]{1,0:T(8,128)(2,1)S(1)}, bf16[128,1024]{1,0:T(8,128)(2,1)S(1)}, u32[]{:S(2)}, u32[]{:S(2)}) collective-permute-start(bf16[128,1024]{1,0:T(8,128)(2,1)S(1)} %get-tuple-element.189.refs_0_.refs_6_), channel_id=1, source_target_pairs={{0,3},{1,2},{2,1},{3,0},{4,7},{5,6},{6,5},{7,4},{8,11},{9,10},{10,... | collective-permute-start | bytes 786440 | tf_op jit(solution)/shard_map/ppermute | solution.py:74
  175.2 22.8 %collective-permute-start.47 = (bf16[512,1408]{1,0:T(8,128)(2,1)S(1)}, bf16[512,1408]{1,0:T(8,128)(2,1)S(1)}, u32[]{:S(2)}, u32[]{:S(2)}) collective-permute-start(bf16[512,1408]{1,0:T(8,128)(2,1)S(1)} %get-tuple-element.207.a_ref), channel_id=1, source_target_pairs={{0,4},{12,8},{1,5},{13,9},{2,6},{14,10},{3,7},{15,11},{16,20},{28,... | collective-permute-start | bytes 4325384 | tf_op jit(solution)/shard_map/ppermute | solution.py:82
  176.6 8.2 %collective-permute-start.45 = (bf16[128,1024]{1,0:T(8,128)(2,1)S(1)}, bf16[128,1024]{1,0:T(8,128)(2,1)S(1)}, u32[]{:S(2)}, u32[]{:S(2)}) collective-permute-start(bf16[128,1024]{1,0:T(8,128)(2,1)S(1)} %get-tuple-element.189.refs_0_.refs_6_), channel_id=1, source_target_pairs={{0,2},{1,3},{2,0},{3,1},{4,6},{5,7},{6,4},{7,5},{8,10},{9,11},{10,... | collective-permute-start | bytes 786440 | tf_op jit(solution)/shard_map/ppermute | solution.py:74
  178.1 7.9 %collective-permute-start.44 = (bf16[128,1024]{1,0:T(8,128)(2,1)S(1)}, bf16[128,1024]{1,0:T(8,128)(2,1)S(1)}, u32[]{:S(2)}, u32[]{:S(2)}) collective-permute-start(bf16[128,1024]{1,0:T(8,128)(2,1)S(1)} %get-tuple-element.189.refs_0_.refs_6_), channel_id=1, source_target_pairs={{0,1},{1,0},{2,3},{3,2},{4,5},{5,4},{6,7},{7,6},{8,9},{9,8},{10,11... | collective-permute-start | bytes 786440 | tf_op jit(solution)/shard_map/ppermute | solution.py:74
  184.1 9.2 %collective-permute-start.42 = (bf16[128,1024]{1,0:T(8,128)(2,1)S(1)}, bf16[128,1024]{1,0:T(8,128)(2,1)S(1)}, u32[]{:S(2)}, u32[]{:S(2)}) collective-permute-start(bf16[128,1024]{1,0:T(8,128)(2,1)S(1)} %get-tuple-element.196), channel_id=1, source_target_pairs={{0,2},{1,3},{2,0},{3,1},{4,6},{5,7},{6,4},{7,5},{8,10},{9,11},{10,... | collective-permute-start | bytes 786440 | tf_op jit(solution)/shard_map/ppermute | solution.py:74
  184.9 8.4 %collective-permute-start.43 = (bf16[128,1024]{1,0:T(8,128)(2,1)S(1)}, bf16[128,1024]{1,0:T(8,128)(2,1)S(1)}, u32[]{:S(2)}, u32[]{:S(2)}) collective-permute-start(bf16[128,1024]{1,0:T(8,128)(2,1)S(1)} %get-tuple-element.197), channel_id=1, source_target_pairs={{0,3},{1,2},{2,1},{3,0},{4,7},{5,6},{6,5},{7,4},{8,11},{9,10},{10,... | collective-permute-start | bytes 786440 | tf_op jit(solution)/shard_map/ppermute | solution.py:74
  194.5 12.5 %collective-permute-start.48 = (bf16[128,1024]{1,0:T(8,128)(2,1)S(1)}, bf16[128,1024]{1,0:T(8,128)(2,1)S(1)}, u32[]{:S(2)}, u32[]{:S(2)}) collective-permute-start(bf16[128,1024]{1,0:T(8,128)(2,1)S(1)} %get-tuple-element.209), channel_id=1, source_target_pairs={{0,1},{1,0},{2,3},{3,2},{4,5},{5,4},{6,7},{7,6},{8,9},{9,8},{10,11... | collective-permute-start | bytes 786440 | tf_op jit(solution)/shard_map/ppermute | solution.py:74
  194.8 12.4 %collective-permute-start.49 = (bf16[128,1024]{1,0:T(8,128)(2,1)S(1)}, bf16[128,1024]{1,0:T(8,128)(2,1)S(1)}, u32[]{:S(2)}, u32[]{:S(2)}) collective-permute-start(bf16[128,1024]{1,0:T(8,128)(2,1)S(1)} %get-tuple-element.210), channel_id=1, source_target_pairs={{0,2},{1,3},{2,0},{3,1},{4,6},{5,7},{6,4},{7,5},{8,10},{9,11},{10,... | collective-permute-start | bytes 786440 | tf_op jit(solution)/shard_map/ppermute | solution.py:74
  196.0 11.1 %collective-permute-start.50 = (bf16[128,1024]{1,0:T(8,128)(2,1)S(1)}, bf16[128,1024]{1,0:T(8,128)(2,1)S(1)}, u32[]{:S(2)}, u32[]{:S(2)}) collective-permute-start(bf16[128,1024]{1,0:T(8,128)(2,1)S(1)} %get-tuple-element.211), channel_id=1, source_target_pairs={{0,3},{1,2},{2,1},{3,0},{4,7},{5,6},{6,5},{7,4},{8,11},{9,10},{10,... | collective-permute-start | bytes 786440 | tf_op jit(solution)/shard_map/ppermute | solution.py:74
  198.4 35.9 %collective-permute-start.56 = (bf16[512,1408]{1,0:T(8,128)(2,1)S(1)}, bf16[512,1408]{1,0:T(8,128)(2,1)S(1)}, u32[]{:S(2)}, u32[]{:S(2)}) collective-permute-start(bf16[512,1408]{1,0:T(8,128)(2,1)S(1)} %shard_map.201), channel_id=1, source_target_pairs={{4,8},{8,4},{5,9},{9,5},{6,10},{10,6},{7,11},{11,7},{20,24},{24,20... | collective-permute-start | bytes 4325384 | tf_op jit(solution)/shard_map/ppermute | solution.py:86
  201.9 27.2 %collective-permute-start.54 = (bf16[512,1024]{1,0:T(8,128)(2,1)S(1)}, bf16[512,1024]{1,0:T(8,128)(2,1)S(1)}, u32[]{:S(2)}, u32[]{:S(2)}) collective-permute-start(bf16[512,1024]{1,0:T(8,128)(2,1)S(1)} %get-tuple-element.220.a_ref), channel_id=1, source_target_pairs={{0,4},{12,8},{1,5},{13,9},{2,6},{14,10},{3,7},{15,11},{16,20},{28,... | collective-permute-start | bytes 3145736 | tf_op jit(solution)/shard_map/ppermute | solution.py:82
  209.6 19.5 %collective-permute-start.53 = (bf16[144,512]{1,0:T(8,128)(2,1)S(1)}, bf16[144,512]{1,0:T(8,128)(2,1)S(1)}, u32[]{:S(2)}, u32[]{:S(2)}) collective-permute-start(bf16[144,512]{1,0:T(8,128)(2,1)S(1)} %shard_map.199.refs_0_), channel_id=1, source_target_pairs={{0,2},{1,3},{2,0},{3,1},{4,6},{5,7},{6,4},{7,5},{8,10},{9,11},{10,... | collective-permute-start | bytes 442376 | tf_op jit(solution)/shard_map/ppermute | solution.py:74
  211.6 33.3 %collective-permute-start.65 = (bf16[176,1024]{1,0:T(8,128)(2,1)}, bf16[176,1024]{1,0:T(8,128)(2,1)}, u32[]{:S(2)}, u32[]{:S(2)}) collective-permute-start(bf16[176,1024]{1,0:T(8,128)(2,1)} %shard_map.208), channel_id=1, source_target_pairs={{0,4},{4,0},{8,12},{12,8},{1,5},{5,1},{9,13},{13,9},{2,6},{6,2},{1... | collective-permute-start | bytes 1081352 | tf_op jit(solution)/shard_map/ppermute | solution.py:78
  211.6 22.7 %collective-permute-start.52 = (bf16[144,512]{1,0:T(8,128)(2,1)S(1)}, bf16[144,512]{1,0:T(8,128)(2,1)S(1)}, u32[]{:S(2)}, u32[]{:S(2)}) collective-permute-start(bf16[144,512]{1,0:T(8,128)(2,1)S(1)} %shard_map.199.refs_0_), channel_id=1, source_target_pairs={{0,1},{1,0},{2,3},{3,2},{4,5},{5,4},{6,7},{7,6},{8,9},{9,8},{10,11... | collective-permute-start | bytes 442376 | tf_op jit(solution)/shard_map/ppermute | solution.py:74
  231.6 25.0 %collective-permute-start.62 = (bf16[512,1024]{1,0:T(8,128)(2,1)}, bf16[512,1024]{1,0:T(8,128)(2,1)}, u32[]{:S(2)}, u32[]{:S(2)}) collective-permute-start(bf16[512,1024]{1,0:T(8,128)(2,1)} %shard_map.207), channel_id=1, source_target_pairs={{4,8},{8,4},{5,9},{9,5},{6,10},{10,6},{7,11},{11,7},{20,24},{24,20... | collective-permute-start | bytes 3145736 | tf_op jit(solution)/shard_map/ppermute | solution.py:86
  237.4 14.3 %collective-permute-start.58 = (bf16[256,1408]{1,0:T(8,128)(2,1)}, bf16[256,1408]{1,0:T(8,128)(2,1)}, u32[]{:S(2)}, u32[]{:S(2)}) collective-permute-start(bf16[256,1408]{1,0:T(8,128)(2,1)} %shard_map.204), channel_id=1, source_target_pairs={{0,4},{4,0},{8,12},{12,8},{1,5},{5,1},{9,13},{13,9},{2,6},{6,2},{1... | collective-permute-start | bytes 2162696 | tf_op jit(solution)/shard_map/ppermute | solution.py:78
  243.5 8.2 %collective-permute-start.57 = (bf16[4,64,1024]{2,1,0:T(8,128)(2,1)}, bf16[4,64,1024]{2,1,0:T(8,128)(2,1)}, u32[]{:S(2)}, u32[]{:S(2)}) collective-permute-start(bf16[4,64,1024]{2,1,0:T(8,128)(2,1)} %get-tuple-element.228), channel_id=1, source_target_pairs={{0,16},{16,0},{1,17},{17,1},{2,18},{18,2},{3,19},{19,3},{4,20},{20... | collective-permute-start | bytes 1572872 | tf_op jit(solution)/shard_map/ppermute | solution.py:90
  249.2 14.8 %collective-permute-start.63 = (bf16[1056,256]{1,0:T(8,128)(2,1)S(1)}, bf16[1056,256]{1,0:T(8,128)(2,1)S(1)}, u32[]{:S(2)}, u32[]{:S(2)}) collective-permute-start(bf16[1056,256]{1,0:T(8,128)(2,1)S(1)} %copy-done.3), channel_id=1, source_target_pairs={{0,4},{12,8},{1,5},{13,9},{2,6},{14,10},{3,7},{15,11},{16,20},{28,... | collective-permute-start | bytes 1622024 | tf_op jit(solution)/shard_map/ppermute | solution.py:82
  254.0 8.2 %collective-permute-start.60 = (bf16[64,1024]{1,0:T(8,128)(2,1)S(1)}, bf16[64,1024]{1,0:T(8,128)(2,1)S(1)}, u32[]{:S(2)}, u32[]{:S(2)}) collective-permute-start(bf16[64,1024]{1,0:T(8,128)(2,1)S(1)} %get-tuple-element.234), channel_id=1, source_target_pairs={{0,2},{1,3},{2,0},{3,1},{4,6},{5,7},{6,4},{7,5},{8,10},{9,11},{10,... | collective-permute-start | bytes 393224 | tf_op jit(solution)/shard_map/ppermute | solution.py:74
  257.9 17.0 %collective-permute-start.67 = (bf16[256,1024]{1,0:T(8,128)(2,1)S(1)}, bf16[256,1024]{1,0:T(8,128)(2,1)S(1)}, u32[]{:S(2)}, u32[]{:S(2)}) collective-permute-start(bf16[256,1024]{1,0:T(8,128)(2,1)S(1)} %shard_map.212), channel_id=1, source_target_pairs={{0,4},{4,0},{8,12},{12,8},{1,5},{5,1},{9,13},{13,9},{2,6},{6,2},{1... | collective-permute-start | bytes 1572872 | tf_op jit(solution)/shard_map/ppermute | solution.py:78
  264.2 10.7 %collective-permute-start.66 = (bf16[1056,256]{1,0:T(8,128)(2,1)S(1)}, bf16[1056,256]{1,0:T(8,128)(2,1)S(1)}, u32[]{:S(2)}, u32[]{:S(2)}) collective-permute-start(bf16[1056,256]{1,0:T(8,128)(2,1)S(1)} %shard_map.210), channel_id=1, source_target_pairs={{4,8},{8,4},{5,9},{9,5},{6,10},{10,6},{7,11},{11,7},{20,24},{24,20... | collective-permute-start | bytes 1622024 | tf_op jit(solution)/shard_map/ppermute | solution.py:86
  266.6 8.3 %collective-permute-start.68 = (bf16[64,1408]{1,0:T(8,128)(2,1)S(1)}, bf16[64,1408]{1,0:T(8,128)(2,1)S(1)}, u32[]{:S(2)}, u32[]{:S(2)}) collective-permute-start(bf16[64,1408]{1,0:T(8,128)(2,1)S(1)} %get-tuple-element.249), channel_id=1, source_target_pairs={{0,1},{1,0},{2,3},{3,2},{4,5},{5,4},{6,7},{7,6},{8,9},{9,8},{10,11... | collective-permute-start | bytes 540680 | tf_op jit(solution)/shard_map/ppermute | solution.py:74
  267.6 10.5 %collective-permute-start.69 = (bf16[64,1408]{1,0:T(8,128)(2,1)S(1)}, bf16[64,1408]{1,0:T(8,128)(2,1)S(1)}, u32[]{:S(2)}, u32[]{:S(2)}) collective-permute-start(bf16[64,1408]{1,0:T(8,128)(2,1)S(1)} %get-tuple-element.250), channel_id=1, source_target_pairs={{0,2},{1,3},{2,0},{3,1},{4,6},{5,7},{6,4},{7,5},{8,10},{9,11},{10,... | collective-permute-start | bytes 540680 | tf_op jit(solution)/shard_map/ppermute | solution.py:74
  269.0 9.2 %collective-permute-start.70 = (bf16[64,1408]{1,0:T(8,128)(2,1)S(1)}, bf16[64,1408]{1,0:T(8,128)(2,1)S(1)}, u32[]{:S(2)}, u32[]{:S(2)}) collective-permute-start(bf16[64,1408]{1,0:T(8,128)(2,1)S(1)} %get-tuple-element.251), channel_id=1, source_target_pairs={{0,3},{1,2},{2,1},{3,0},{4,7},{5,6},{6,5},{7,4},{8,11},{9,10},{10,... | collective-permute-start | bytes 540680 | tf_op jit(solution)/shard_map/ppermute | solution.py:74
  282.7 8.7 %collective-permute-start.72 = (bf16[64,768]{1,0:T(8,128)(2,1)S(1)}, bf16[64,768]{1,0:T(8,128)(2,1)S(1)}, u32[]{:S(2)}, u32[]{:S(2)}) collective-permute-start(bf16[64,768]{1,0:T(8,128)(2,1)S(1)} %get-tuple-element.258), channel_id=1, source_target_pairs={{0,1},{1,0},{2,3},{3,2},{4,5},{5,4},{6,7},{7,6},{8,9},{9,8},{10,11... | collective-permute-start | bytes 294920 | tf_op jit(solution)/shard_map/ppermute | solution.py:74
  286.3 10.7 %collective-permute-start.71 = (bf16[528,256]{1,0:T(8,128)(2,1)S(1)}, bf16[528,256]{1,0:T(8,128)(2,1)S(1)}, u32[]{:S(2)}, u32[]{:S(2)}) collective-permute-start(bf16[528,256]{1,0:T(8,128)(2,1)S(1)} %shard_map.214), channel_id=1, source_target_pairs={{0,4},{4,0},{8,12},{12,8},{1,5},{5,1},{9,13},{13,9},{2,6},{6,2},{1... | collective-permute-start | bytes 811016 | tf_op jit(solution)/shard_map/ppermute | solution.py:78
  (49 other events, 294.1 us)

commit v4 on v3

--- a/solution.py
+++ b/solution.py
@@ -25,17 +25,17 @@
     "qkv2": "byy1",
     "up3": "kv",
     "gu1": "byxy1",
-    "cot": "parts1",
+    "cot": "mid",
     "low3": "mid",
     "up2": "byy2",
-    "down1": "byy2",
+    "down1": "mine2",
     "g1": "nb2",
     "g2": "branch",
-    "u1": "parts3",
+    "u1": "nb1",
     "result": "into",
     "h1": "gpy",
-    "u2": "gproj",
-    "in1": "got",
+    "u2": "give",
+    "in1": "context",
     "u3": "both",
     "h2": "got",
     "h3": "gu_out",
@@ -43,12 +43,13 @@
     "down3": "hidden",
     "g3": "context",
 }
-SKIP = (6, 7, 23, 32, 36)
+SKIP = (6, 7, 14, 20, 23, 32, 33, 36)
 COST = {
     "": 3.0,
     "unpack_columns": 10.0,
     "row_parts": 10.0,
     "pack_pairs": 0.3,
+    "stack4": 1.0,
 }
 
 

time: 299 us -> 295 us (0.987)
  waiting for transfers between devices: 135 us -> 130 us
  starting transfers between devices: 104 us -> 107 us
    ppermute x42, waiting for transfers between devices: 63.4 us -> 58.3 us  [hop(): return lax.ppermute(x, 't', [(i, i ^ r) for i in range(4)])]
    ppermute x18, starting transfers between devices: 27.7 us -> 31 us  [zhop(): return lax.ppermute(x, 'd1', [(i, i ^ r) for i in range(4)])]
    unnamed x74 -> x70, local copies, waits for them, and re-layouts: 9.42 us -> 9.85 us
  transfers between devices with their start and end apart: 77 -> 77, of which waited for: 35 -> 33; matrix products, arithmetic and copies ran while one was open for 1% -> 1% of each run, Pallas kernels for 14% -> 14%
where the time goes in v4:
time: 295 us; the launch traced here: 294 us
  waiting for transfers between devices  130 us (44%)
  starting transfers between devices  107 us (36%)
  Pallas kernels  45.4 us (15%)
  local copies, waits for them, and re-layouts  10.5 us (4%)
    ppermute x42, waiting for transfers between devices, hop(): return lax.ppermute(x, 't', [(i, i ^ r) for i in range(4)])  58.3 us
    ppermute x42, starting transfers between devices, hop(): return lax.ppermute(x, 't', [(i, i ^ r) for i in range(4)])  51.3 us
    ppermute x18, waiting for transfers between devices, zhop(): return lax.ppermute(x, 'd1', [(i, i ^ r) for i in range(4)])  47.8 us
    pallas_call x42, Pallas kernels, call(): pl.pallas_call(body, out_shape=shapes, in_specs=inside, out_specs=[pl.Blo...  45.4 us
    ppermute x18, starting transfers between devices, zhop(): return lax.ppermute(x, 'd1', [(i, i ^ r) for i in range(4)])  31 us
    ppermute x4, waiting for transfers between devices, inward(): return lax.ppermute(x, 'd1', [(0, 1), (3, 2)])  17.5 us
    ppermute x4, starting transfers between devices, inward(): return lax.ppermute(x, 'd1', [(0, 1), (3, 2)])  11.2 us
    unnamed x70, local copies, waits for them, and re-layouts  9.85 us
  transfers between devices with their start and end apart: 77, of which 33 were waited for; matrix products, arithmetic and copies ran while one was open for 1% of the time, Pallas kernels for 14%

profile of v4, /device:TPU:0, one launch (start us, length us, event | category | flops | bytes accessed | tf_op | source)
XLA Modules:
  0.0 294.5 jit_solution(5800099704694230943)
XLA Ops:
  2.6 3.0 %collective-permute-start = (bf16[64,1024]{1,0:T(8,128)(2,1)S(1)}, bf16[64,1024]{1,0:T(8,128)(2,1)S(1)}, u32[]{:S(2)}, u32[]{:S(2)}) collective-permute-start(bf16[64,1024]{1,0:T(8,128)(2,1)S(1)} %get-tuple-element.136), channel_id=1, source_target_pairs={{0,1},{1,0},{2,3},{3,2},{4,5},{5,4},{6,7},{7,6},{8,9},{9,8},{10,11... | collective-permute-start | bytes 393224 | tf_op jit(solution)/shard_map/ppermute | solution.py:75
  8.1 4.2 %all-to-all-start = ((bf16[4,64,768]{2,1,0:T(8,128)(2,1)}), bf16[4,64,768]{2,1,0:T(8,128)(2,1)S(1)}, u32[]{:S(2)}, u32[]{:S(2)}) async-start(bf16[4,64,768]{2,1,0:T(8,128)(2,1)} %shard_map.179), calls=%async_computation | async-start | bytes 786432 | tf_op jit(solution)/shard_map/all_to_all | solution.py:932
  12.3 3.7 %collective-permute-start.5 = (bf16[528,256]{1,0:T(8,128)(2,1)S(1)}, bf16[528,256]{1,0:T(8,128)(2,1)S(1)}, u32[]{:S(2)}, u32[]{:S(2)}) collective-permute-start(bf16[528,256]{1,0:T(8,128)(2,1)S(1)} %fusion.1.refs_0_.refs_4_), channel_id=1, source_target_pairs={{0,12},{4,8},{8,4},{12,0},{1,13},{5,9},{9,5},{13,1},{2,14},{6,10},... | collective-permute-start | bytes 811016 | tf_op jit(solution)/shard_map/ppermute | solution.py:79
  16.1 2.1 all-to-all-done
  18.2 1.6 collective-permute-start.4
  19.7 1.8 collective-permute-done.5.refs_3_.refs_7_
  21.6 5.4 %collective-permute-start.6 = (bf16[528,256]{1,0:T(8,128)(2,1)S(1)}, bf16[528,256]{1,0:T(8,128)(2,1)}, u32[]{:S(2)}, u32[]{:S(2)}) collective-permute-start(bf16[528,256]{1,0:T(8,128)(2,1)S(1)} %collective-permute-done.5.refs_3_.refs_7_), channel_id=1, source_target_pairs={{0,4},{4,0},{8,12},{12,8},{1,5},{5,1},{9,13},{13,9},{2,6},{6,2},{1... | collective-permute-start | bytes 811016 | tf_op jit(solution)/shard_map/ppermute | solution.py:79
  27.0 2.5 collective-permute-start.10
  30.9 3.9 %all-to-all-start.1 = ((bf16[4,64,1408]{2,1,0:T(8,128)(2,1)}), bf16[4,64,1408]{2,1,0:T(8,128)(2,1)S(1)}, u32[]{:S(2)}, u32[]{:S(2)}) async-start(bf16[4,64,1408]{2,1,0:T(8,128)(2,1)} %shard_map.182), calls=%async_computation.1 | async-start | bytes 1441792 | tf_op jit(solution)/shard_map/all_to_all | solution.py:934
  34.8 2.0 shard_map.180
  36.8 2.1 collective-permute-start.7
  38.9 1.8 collective-permute-start.8
  41.9 5.3 %collective-permute-done.7.b.refs_1_ = bf16[144,512]{1,0:T(8,128)(2,1)S(1)} collective-permute-done((bf16[144,512]{1,0:T(8,128)(2,1)S(1)}, bf16[144,512]{1,0:T(8,128)(2,1)S(1)}, u32[]{:S(2)}, u32[]{:S(2)}) %collective-permute-start.7) | collective-permute-done | bytes 147488 | tf_op jit(solution)/shard_map/ppermute | solution.py:75
  47.2 2.5 collective-permute-done.9.e.refs_3_
  53.0 4.5 %collective-permute-done.12.refs_5_.refs_1_ = bf16[256,1024]{1,0:T(8,128)(2,1)S(1)} collective-permute-done((bf16[256,1024]{1,0:T(8,128)(2,1)S(1)}, bf16[256,1024]{1,0:T(8,128)(2,1)S(1)}, u32[]{:S(2)}, u32[]{:S(2)}) %collective-permute-start.12) | collective-permute-done | bytes 524320 | tf_op jit(solution)/shard_map/ppermute | solution.py:79
  59.0 6.7 %collective-permute-done.14.refs_2_ = bf16[128,1024]{1,0:T(8,128)(2,1)S(1)} collective-permute-done((bf16[128,1024]{1,0:T(8,128)(2,1)S(1)}, bf16[128,1024]{1,0:T(8,128)(2,1)S(1)}, u32[]{:S(2)}, u32[]{:S(2)}) %collective-permute-start.14) | collective-permute-done | bytes 262176 | tf_op jit(solution)/shard_map/ppermute | solution.py:75
  65.7 5.6 %collective-permute-done.15.refs_6_.refs_2_ = bf16[256,1024]{1,0:T(8,128)(2,1)S(1)} collective-permute-done((bf16[256,1024]{1,0:T(8,128)(2,1)S(1)}, bf16[256,1024]{1,0:T(8,128)(2,1)S(1)}, u32[]{:S(2)}, u32[]{:S(2)}) %collective-permute-start.15) | collective-permute-done | bytes 524320 | tf_op jit(solution)/shard_map/ppermute | solution.py:79
  75.0 9.6 %collective-permute-done.16.refs_3_ = bf16[128,1024]{1,0:T(8,128)(2,1)S(1)} collective-permute-done((bf16[128,1024]{1,0:T(8,128)(2,1)S(1)}, bf16[128,1024]{1,0:T(8,128)(2,1)S(1)}, u32[]{:S(2)}, u32[]{:S(2)}) %collective-permute-start.16) | collective-permute-done | bytes 262176 | tf_op jit(solution)/shard_map/ppermute | solution.py:75
  84.6 11.6 %collective-permute-done.17.refs_5_ = bf16[256,1408]{1,0:T(8,128)(2,1)S(1)} collective-permute-done((bf16[256,1408]{1,0:T(8,128)(2,1)S(1)}, bf16[256,1408]{1,0:T(8,128)(2,1)S(1)}, u32[]{:S(2)}, u32[]{:S(2)}) %collective-permute-start.17) | collective-permute-done | bytes 720928 | tf_op jit(solution)/shard_map/ppermute | solution.py:79
  102.6 2.5 collective-permute-start.22
  106.1 4.7 %collective-permute-done.20.refs_9_ = bf16[128,1408]{1,0:T(8,128)(2,1)S(1)} collective-permute-done((bf16[128,1408]{1,0:T(8,128)(2,1)S(1)}, bf16[128,1408]{1,0:T(8,128)(2,1)S(1)}, u32[]{:S(2)}, u32[]{:S(2)}) %collective-permute-start.20) | collective-permute-done | bytes 360480 | tf_op jit(solution)/shard_map/ppermute | solution.py:79
  111.8 5.7 %collective-permute-done.23.e = bf16[128,1024]{1,0:T(8,128)(2,1)S(1)} collective-permute-done((bf16[128,1024]{1,0:T(8,128)(2,1)S(1)}, bf16[128,1024]{1,0:T(8,128)(2,1)S(1)}, u32[]{:S(2)}, u32[]{:S(2)}) %collective-permute-start.23) | collective-permute-done | bytes 262176 | tf_op jit(solution)/shard_map/ppermute | solution.py:75
  119.1 2.2 collective-permute-start.30
  121.9 11.2 %collective-permute-done.27.refs_6_ = bf16[128,1408]{1,0:T(8,128)(2,1)S(1)} collective-permute-done((bf16[128,1408]{1,0:T(8,128)(2,1)S(1)}, bf16[128,1408]{1,0:T(8,128)(2,1)S(1)}, u32[]{:S(2)}, u32[]{:S(2)}) %collective-permute-start.27) | collective-permute-done | bytes 360480 | tf_op jit(solution)/shard_map/ppermute | solution.py:79
  133.1 2.0 collective-permute-start.25
  135.1 2.0 collective-permute-start.33
  137.1 5.0 %collective-permute-done.28.refs_3_ = bf16[128,1024]{1,0:T(8,128)(2,1)S(1)} collective-permute-done((bf16[128,1024]{1,0:T(8,128)(2,1)S(1)}, bf16[128,1024]{1,0:T(8,128)(2,1)S(1)}, u32[]{:S(2)}, u32[]{:S(2)}) %collective-permute-start.28) | collective-permute-done | bytes 262176 | tf_op jit(solution)/shard_map/ppermute | solution.py:75
  142.1 2.8 collective-permute-done.25.refs_1_
  144.9 2.1 shard_map.188
  147.8 2.8 collective-permute-done.33.refs_3_
  150.6 1.6 shard_map.189
  154.2 3.6 %shard_map.190 = (bf16[704,1024]{1,0:T(8,128)(2,1)S(1)}, bf16[512,1408]{1,0:T(8,128)(2,1)S(1)}, bf16[128,1024]{1,0:T(8,128)(2,1)S(1)}, bf16[128,1024]{1,0:T(8,12...) custom-call(s32[3]{0:T(128)S(1)} %pad_add_fusion.n_ref, bf16[128,1024]{1,0:T(8,128)(2,1)S(1)} %bitcast.36, ...), custom_call_target="tpu_custom_call" | custom-call | flops 3000000000 | bytes 5000000 | tf_op jit(solution)/shard_map/pallas_call | solution.py:105
  159.2 2.1 collective-permute-start.38
  161.4 1.6 collective-permute-done.35.b_ref
  166.1 4.1 %collective-permute-done.38.e = bf16[128,1024]{1,0:T(8,128)(2,1)S(1)} collective-permute-done((bf16[128,1024]{1,0:T(8,128)(2,1)S(1)}, bf16[128,1024]{1,0:T(8,128)(2,1)S(1)}, u32[]{:S(2)}, u32[]{:S(2)}) %collective-permute-start.38) | collective-permute-done | bytes 262176 | tf_op jit(solution)/shard_map/ppermute | solution.py:75
  171.2 2.9 collective-permute-start.39
  174.1 1.9 shard_map.197
  178.9 2.7 collective-permute-done.39.refs_3_.refs_9_
  182.5 2.3 collective-permute-start.41
  189.2 4.8 %collective-permute-done.42.refs_3_ = bf16[128,1024]{1,0:T(8,128)(2,1)S(1)} collective-permute-done((bf16[128,1024]{1,0:T(8,128)(2,1)S(1)}, bf16[128,1024]{1,0:T(8,128)(2,1)S(1)}, u32[]{:S(2)}, u32[]{:S(2)}) %collective-permute-start.42) | collective-permute-done | bytes 262176 | tf_op jit(solution)/shard_map/ppermute | solution.py:75
  196.7 2.0 collective-permute-start.50
  201.0 2.9 shard_map.200
  205.5 5.6 %collective-permute-start.54 = (bf16[512,1024]{1,0:T(8,128)(2,1)}, bf16[512,1024]{1,0:T(8,128)(2,1)}, u32[]{:S(2)}, u32[]{:S(2)}) collective-permute-start(bf16[512,1024]{1,0:T(8,128)(2,1)} %get-tuple-element.220.a_ref), channel_id=1, source_target_pairs={{0,4},{12,8},{1,5},{13,9},{2,6},{14,10},{3,7},{15,11},{16,20},{28,... | collective-permute-start | bytes 3145736 | tf_op jit(solution)/shard_map/ppermute | solution.py:83
  211.0 1.7 shard_map.198
  213.4 1.7 collective-permute-done.51.b_ref
  219.1 2.1 collective-permute-start.55
  221.1 12.7 %collective-permute-done.54.b_ref = bf16[512,1024]{1,0:T(8,128)(2,1)} collective-permute-done((bf16[512,1024]{1,0:T(8,128)(2,1)}, bf16[512,1024]{1,0:T(8,128)(2,1)}, u32[]{:S(2)}, u32[]{:S(2)}) %collective-permute-start.54) | collective-permute-done | bytes 1048608 | tf_op jit(solution)/shard_map/ppermute | solution.py:83
  235.1 1.8 shard_map.206
  237.9 3.7 %collective-permute-start.58 = (bf16[256,1408]{1,0:T(8,128)(2,1)S(1)}, bf16[256,1408]{1,0:T(8,128)(2,1)S(1)}, u32[]{:S(2)}, u32[]{:S(2)}) collective-permute-start(bf16[256,1408]{1,0:T(8,128)(2,1)S(1)} %shard_map.203), channel_id=1, source_target_pairs={{0,4},{4,0},{8,12},{12,8},{1,5},{5,1},{9,13},{13,9},{2,6},{6,2},{1... | collective-permute-start | bytes 2162696 | tf_op jit(solution)/shard_map/ppermute | solution.py:79
  241.6 1.7 shard_map.201
  247.1 2.9 collective-permute-start.65
  250.0 3.4 %collective-permute-done.58.b_ref = bf16[256,1408]{1,0:T(8,128)(2,1)S(1)} collective-permute-done((bf16[256,1408]{1,0:T(8,128)(2,1)S(1)}, bf16[256,1408]{1,0:T(8,128)(2,1)S(1)}, u32[]{:S(2)}, u32[]{:S(2)}) %collective-permute-start.58) | collective-permute-done | bytes 720928 | tf_op jit(solution)/shard_map/ppermute | solution.py:79
  253.6 1.8 collective-permute-start.59
  257.3 2.5 collective-permute-start.67
  259.8 1.9 collective-permute-done.60.refs_2_
  261.9 3.2 %collective-permute-done.65.b_ref = bf16[1056,256]{1,0:T(8,128)(2,1)S(1)} collective-permute-done((bf16[1056,256]{1,0:T(8,128)(2,1)S(1)}, bf16[1056,256]{1,0:T(8,128)(2,1)S(1)}, u32[]{:S(2)}, u32[]{:S(2)}) %collective-permute-start.65) | collective-permute-done | bytes 540704 | tf_op jit(solution)/shard_map/ppermute | solution.py:83
  267.0 1.8 collective-permute-start.68
  270.6 2.0 shard_map.209
  272.6 2.2 collective-permute-done.67.b_ref
  276.2 2.3 shard_map.213
  281.9 1.6 collective-permute-start.74
  283.6 4.9 %collective-permute-start.71 = (bf16[528,256]{1,0:T(8,128)(2,1)S(1)}, bf16[528,256]{1,0:T(8,128)(2,1)S(1)}, u32[]{:S(2)}, u32[]{:S(2)}) collective-permute-start(bf16[528,256]{1,0:T(8,128)(2,1)S(1)} %shard_map.214), channel_id=1, source_target_pairs={{0,4},{4,0},{8,12},{12,8},{1,5},{5,1},{9,13},{13,9},{2,6},{6,2},{1... | collective-permute-start | bytes 811016 | tf_op jit(solution)/shard_map/ppermute | solution.py:79
  288.6 1.6 shard_map.217
  290.2 2.8 collective-permute-done.71.b_ref
  (209 shorter events, 72.3 us)
Async XLA Ops:
  2.6 13.4 %collective-permute-start = (bf16[64,1024]{1,0:T(8,128)(2,1)S(1)}, bf16[64,1024]{1,0:T(8,128)(2,1)S(1)}, u32[]{:S(2)}, u32[]{:S(2)}) collective-permute-start(bf16[64,1024]{1,0:T(8,128)(2,1)S(1)} %get-tuple-element.136), channel_id=1, source_target_pairs={{0,1},{1,0},{2,3},{3,2},{4,5},{5,4},{6,7},{7,6},{8,9},{9,8},{10,11... | collective-permute-start | bytes 393224 | tf_op jit(solution)/shard_map/ppermute | solution.py:75
  5.6 10.4 %collective-permute-start.1 = (bf16[64,1024]{1,0:T(8,128)(2,1)S(1)}, bf16[64,1024]{1,0:T(8,128)(2,1)S(1)}, u32[]{:S(2)}, u32[]{:S(2)}) collective-permute-start(bf16[64,1024]{1,0:T(8,128)(2,1)S(1)} %get-tuple-element.137), channel_id=1, source_target_pairs={{0,2},{1,3},{2,0},{3,1},{4,6},{5,7},{6,4},{7,5},{8,10},{9,11},{10,... | collective-permute-start | bytes 393224 | tf_op jit(solution)/shard_map/ppermute | solution.py:75
  7.1 8.9 %collective-permute-start.2 = (bf16[64,1024]{1,0:T(8,128)(2,1)S(1)}, bf16[64,1024]{1,0:T(8,128)(2,1)S(1)}, u32[]{:S(2)}, u32[]{:S(2)}) collective-permute-start(bf16[64,1024]{1,0:T(8,128)(2,1)S(1)} %get-tuple-element.138), channel_id=1, source_target_pairs={{0,3},{1,2},{2,1},{3,0},{4,7},{5,6},{6,5},{7,4},{8,11},{9,10},{10,... | collective-permute-start | bytes 393224 | tf_op jit(solution)/shard_map/ppermute | solution.py:75
  8.1 10.1 %all-to-all-start = ((bf16[4,64,768]{2,1,0:T(8,128)(2,1)}), bf16[4,64,768]{2,1,0:T(8,128)(2,1)S(1)}, u32[]{:S(2)}, u32[]{:S(2)}) async-start(bf16[4,64,768]{2,1,0:T(8,128)(2,1)} %shard_map.179), calls=%async_computation | async-start | bytes 786432 | tf_op jit(solution)/shard_map/all_to_all | solution.py:932
  12.3 9.2 %collective-permute-start.5 = (bf16[528,256]{1,0:T(8,128)(2,1)S(1)}, bf16[528,256]{1,0:T(8,128)(2,1)S(1)}, u32[]{:S(2)}, u32[]{:S(2)}) collective-permute-start(bf16[528,256]{1,0:T(8,128)(2,1)S(1)} %fusion.1.refs_0_.refs_4_), channel_id=1, source_target_pairs={{0,12},{4,8},{8,4},{12,0},{1,13},{5,9},{9,5},{13,1},{2,14},{6,10},... | collective-permute-start | bytes 811016 | tf_op jit(solution)/shard_map/ppermute | solution.py:79
  18.1 16.6 %collective-permute-start.3 = (bf16[4,64,1024]{2,1,0:T(8,128)(2,1)S(1)}, bf16[4,64,1024]{2,1,0:T(8,128)(2,1)}, u32[]{:S(2)}, u32[]{:S(2)}) collective-permute-start(bf16[4,64,1024]{2,1,0:T(8,128)(2,1)S(1)} %shard_map.178.a_ref), channel_id=1, source_target_pairs={{0,16},{16,0},{1,17},{17,1},{2,18},{18,2},{3,19},{19,3},{4,20},{20... | collective-permute-start | bytes 1572872 | tf_op jit(solution)/shard_map/ppermute | solution.py:91
  18.2 16.6 %collective-permute-start.4 = (bf16[528,256]{1,0:T(8,128)(2,1)S(1)}, bf16[528,256]{1,0:T(8,128)(2,1)S(1)}, u32[]{:S(2)}, u32[]{:S(2)}) collective-permute-start(bf16[528,256]{1,0:T(8,128)(2,1)S(1)} %fusion.1.refs_0_.refs_4_), channel_id=1, source_target_pairs={{0,4},{4,0},{8,12},{12,8},{1,5},{5,1},{9,13},{13,9},{2,6},{6,2},{1... | collective-permute-start | bytes 811016 | tf_op jit(solution)/shard_map/ppermute | solution.py:79
  21.6 13.2 %collective-permute-start.6 = (bf16[528,256]{1,0:T(8,128)(2,1)S(1)}, bf16[528,256]{1,0:T(8,128)(2,1)}, u32[]{:S(2)}, u32[]{:S(2)}) collective-permute-start(bf16[528,256]{1,0:T(8,128)(2,1)S(1)} %collective-permute-done.5.refs_3_.refs_7_), channel_id=1, source_target_pairs={{0,4},{4,0},{8,12},{12,8},{1,5},{5,1},{9,13},{13,9},{2,6},{6,2},{1... | collective-permute-start | bytes 811016 | tf_op jit(solution)/shard_map/ppermute | solution.py:79
  27.0 22.8 %collective-permute-start.10 = (bf16[256,1024]{1,0:T(8,128)(2,1)S(1)}, bf16[256,1024]{1,0:T(8,128)(2,1)S(1)}, u32[]{:S(2)}, u32[]{:S(2)}) collective-permute-start(bf16[256,1024]{1,0:T(8,128)(2,1)S(1)} %shard_map.183.refs_4_.refs_0_), channel_id=1, source_target_pairs={{0,12},{4,8},{8,4},{12,0},{1,13},{5,9},{9,5},{13,1},{2,14},{6,10},... | collective-permute-start | bytes 1572872 | tf_op jit(solution)/shard_map/ppermute | solution.py:79
  30.9 19.0 %all-to-all-start.1 = ((bf16[4,64,1408]{2,1,0:T(8,128)(2,1)}), bf16[4,64,1408]{2,1,0:T(8,128)(2,1)S(1)}, u32[]{:S(2)}, u32[]{:S(2)}) async-start(bf16[4,64,1408]{2,1,0:T(8,128)(2,1)} %shard_map.182), calls=%async_computation.1 | async-start | bytes 1441792 | tf_op jit(solution)/shard_map/all_to_all | solution.py:934
  36.8 10.5 %collective-permute-start.7 = (bf16[144,512]{1,0:T(8,128)(2,1)S(1)}, bf16[144,512]{1,0:T(8,128)(2,1)S(1)}, u32[]{:S(2)}, u32[]{:S(2)}) collective-permute-start(bf16[144,512]{1,0:T(8,128)(2,1)S(1)} %get-tuple-element.143), channel_id=1, source_target_pairs={{0,1},{1,0},{2,3},{3,2},{4,5},{5,4},{6,7},{7,6},{8,9},{9,8},{10,11... | collective-permute-start | bytes 442376 | tf_op jit(solution)/shard_map/ppermute | solution.py:75
  38.9 8.4 %collective-permute-start.8 = (bf16[144,512]{1,0:T(8,128)(2,1)S(1)}, bf16[144,512]{1,0:T(8,128)(2,1)S(1)}, u32[]{:S(2)}, u32[]{:S(2)}) collective-permute-start(bf16[144,512]{1,0:T(8,128)(2,1)S(1)} %get-tuple-element.144), channel_id=1, source_target_pairs={{0,2},{1,3},{2,0},{3,1},{4,6},{5,7},{6,4},{7,5},{8,10},{9,11},{10,... | collective-permute-start | bytes 442376 | tf_op jit(solution)/shard_map/ppermute | solution.py:75
  40.7 9.1 %collective-permute-start.9 = (bf16[144,512]{1,0:T(8,128)(2,1)S(1)}, bf16[144,512]{1,0:T(8,128)(2,1)S(1)}, u32[]{:S(2)}, u32[]{:S(2)}) collective-permute-start(bf16[144,512]{1,0:T(8,128)(2,1)S(1)} %get-tuple-element.145), channel_id=1, source_target_pairs={{0,3},{1,2},{2,1},{3,0},{4,7},{5,6},{6,5},{7,4},{8,11},{9,10},{10,... | collective-permute-start | bytes 442376 | tf_op jit(solution)/shard_map/ppermute | solution.py:75
  40.7 16.8 %collective-permute-start.12 = (bf16[256,1024]{1,0:T(8,128)(2,1)S(1)}, bf16[256,1024]{1,0:T(8,128)(2,1)S(1)}, u32[]{:S(2)}, u32[]{:S(2)}) collective-permute-start(bf16[256,1024]{1,0:T(8,128)(2,1)S(1)} %shard_map.183.refs_4_.refs_0_), channel_id=1, source_target_pairs={{0,4},{4,0},{8,12},{12,8},{1,5},{5,1},{9,13},{13,9},{2,6},{6,2},{1... | collective-permute-start | bytes 1572872 | tf_op jit(solution)/shard_map/ppermute | solution.py:79
  57.4 13.8 %collective-permute-start.15 = (bf16[256,1024]{1,0:T(8,128)(2,1)S(1)}, bf16[256,1024]{1,0:T(8,128)(2,1)S(1)}, u32[]{:S(2)}, u32[]{:S(2)}) collective-permute-start(bf16[256,1024]{1,0:T(8,128)(2,1)S(1)} %collective-permute-done.10.refs_7_.refs_3_), channel_id=1, source_target_pairs={{0,4},{4,0},{8,12},{12,8},{1,5},{5,1},{9,13},{13,9},{2,6},{6,2},{1... | collective-permute-start | bytes 1572872 | tf_op jit(solution)/shard_map/ppermute | solution.py:79
  57.4 8.2 %collective-permute-start.14 = (bf16[128,1024]{1,0:T(8,128)(2,1)S(1)}, bf16[128,1024]{1,0:T(8,128)(2,1)S(1)}, u32[]{:S(2)}, u32[]{:S(2)}) collective-permute-start(bf16[128,1024]{1,0:T(8,128)(2,1)S(1)} %get-tuple-element.150.refs_0_), channel_id=1, source_target_pairs={{0,2},{1,3},{2,0},{3,1},{4,6},{5,7},{6,4},{7,5},{8,10},{9,11},{10,... | collective-permute-start | bytes 786440 | tf_op jit(solution)/shard_map/ppermute | solution.py:75
  71.3 24.9 %collective-permute-start.17 = (bf16[256,1408]{1,0:T(8,128)(2,1)S(1)}, bf16[256,1408]{1,0:T(8,128)(2,1)S(1)}, u32[]{:S(2)}, u32[]{:S(2)}) collective-permute-start(bf16[256,1408]{1,0:T(8,128)(2,1)S(1)} %bitcast.21), channel_id=1, source_target_pairs={{0,4},{4,0},{8,12},{12,8},{1,5},{5,1},{9,13},{13,9},{2,6},{6,2},{1... | collective-permute-start | bytes 2162696 | tf_op jit(solution)/shard_map/ppermute | solution.py:79
  71.6 24.7 %collective-permute-start.13 = (bf16[128,1024]{1,0:T(8,128)(2,1)S(1)}, bf16[128,1024]{1,0:T(8,128)(2,1)S(1)}, u32[]{:S(2)}, u32[]{:S(2)}) collective-permute-start(bf16[128,1024]{1,0:T(8,128)(2,1)S(1)} %get-tuple-element.150.refs_0_), channel_id=1, source_target_pairs={{0,1},{1,0},{2,3},{3,2},{4,5},{5,4},{6,7},{7,6},{8,9},{9,8},{10,11... | collective-permute-start | bytes 786440 | tf_op jit(solution)/shard_map/ppermute | solution.py:75
  72.8 11.8 %collective-permute-start.16 = (bf16[128,1024]{1,0:T(8,128)(2,1)S(1)}, bf16[128,1024]{1,0:T(8,128)(2,1)S(1)}, u32[]{:S(2)}, u32[]{:S(2)}) collective-permute-start(bf16[128,1024]{1,0:T(8,128)(2,1)S(1)} %collective-permute-done.14.refs_2_), channel_id=1, source_target_pairs={{0,1},{1,0},{2,3},{3,2},{4,5},{5,4},{6,7},{7,6},{8,9},{9,8},{10,11... | collective-permute-start | bytes 786440 | tf_op jit(solution)/shard_map/ppermute | solution.py:75
  73.7 24.6 %collective-permute-start.18 = (bf16[128,1408]{1,0:T(8,128)(2,1)S(1)}, bf16[128,1408]{1,0:T(8,128)(2,1)S(1)}, u32[]{:S(2)}, u32[]{:S(2)}) collective-permute-start(bf16[128,1408]{1,0:T(8,128)(2,1)S(1)} %get-tuple-element.271), channel_id=1, source_target_pairs={{0,12},{4,8},{8,4},{12,0},{1,13},{5,9},{9,5},{13,1},{2,14},{6,10},... | collective-permute-start | bytes 1081352 | tf_op jit(solution)/shard_map/ppermute | solution.py:79
  99.6 11.1 %collective-permute-start.20 = (bf16[128,1408]{1,0:T(8,128)(2,1)S(1)}, bf16[128,1408]{1,0:T(8,128)(2,1)S(1)}, u32[]{:S(2)}, u32[]{:S(2)}) collective-permute-start(bf16[128,1408]{1,0:T(8,128)(2,1)S(1)} %get-tuple-element.159), channel_id=1, source_target_pairs={{0,12},{4,8},{8,4},{12,0},{1,13},{5,9},{9,5},{13,1},{2,14},{6,10},... | collective-permute-start | bytes 1081352 | tf_op jit(solution)/shard_map/ppermute | solution.py:79
  102.5 9.3 %collective-permute-start.21 = (bf16[128,1024]{1,0:T(8,128)(2,1)S(1)}, bf16[128,1024]{1,0:T(8,128)(2,1)S(1)}, u32[]{:S(2)}, u32[]{:S(2)}) collective-permute-start(bf16[128,1024]{1,0:T(8,128)(2,1)S(1)} %get-tuple-element.161), channel_id=1, source_target_pairs={{0,1},{1,0},{2,3},{3,2},{4,5},{5,4},{6,7},{7,6},{8,9},{9,8},{10,11... | collective-permute-start | bytes 786440 | tf_op jit(solution)/shard_map/ppermute | solution.py:75
  102.6 9.2 %collective-permute-start.22 = (bf16[128,1024]{1,0:T(8,128)(2,1)S(1)}, bf16[128,1024]{1,0:T(8,128)(2,1)S(1)}, u32[]{:S(2)}, u32[]{:S(2)}) collective-permute-start(bf16[128,1024]{1,0:T(8,128)(2,1)S(1)} %get-tuple-element.162), channel_id=1, source_target_pairs={{0,2},{1,3},{2,0},{3,1},{4,6},{5,7},{6,4},{7,5},{8,10},{9,11},{10,... | collective-permute-start | bytes 786440 | tf_op jit(solution)/shard_map/ppermute | solution.py:75
  105.1 12.3 %collective-permute-start.23 = (bf16[128,1024]{1,0:T(8,128)(2,1)S(1)}, bf16[128,1024]{1,0:T(8,128)(2,1)S(1)}, u32[]{:S(2)}, u32[]{:S(2)}) collective-permute-start(bf16[128,1024]{1,0:T(8,128)(2,1)S(1)} %get-tuple-element.163), channel_id=1, source_target_pairs={{0,3},{1,2},{2,1},{3,0},{4,7},{5,6},{6,5},{7,4},{8,11},{9,10},{10,... | collective-permute-start | bytes 786440 | tf_op jit(solution)/shard_map/ppermute | solution.py:75
  106.1 12.2 %collective-permute-start.24 = (bf16[176,1024]{1,0:T(8,128)(2,1)S(1)}, bf16[176,1024]{1,0:T(8,128)(2,1)S(1)}, u32[]{:S(2)}, u32[]{:S(2)}) collective-permute-start(bf16[176,1024]{1,0:T(8,128)(2,1)S(1)} %bitcast.29), channel_id=1, source_target_pairs={{0,4},{4,0},{8,12},{12,8},{1,5},{5,1},{9,13},{13,9},{2,6},{6,2},{1... | collective-permute-start | bytes 1081352 | tf_op jit(solution)/shard_map/ppermute | solution.py:79
  110.7 22.3 %collective-permute-start.27 = (bf16[128,1408]{1,0:T(8,128)(2,1)S(1)}, bf16[128,1408]{1,0:T(8,128)(2,1)S(1)}, u32[]{:S(2)}, u32[]{:S(2)}) collective-permute-start(bf16[128,1408]{1,0:T(8,128)(2,1)S(1)} %collective-permute-done.18.refs_8_), channel_id=1, source_target_pairs={{0,4},{4,0},{8,12},{12,8},{1,5},{5,1},{9,13},{13,9},{2,6},{6,2},{1... | collective-permute-start | bytes 1081352 | tf_op jit(solution)/shard_map/ppermute | solution.py:79
  118.2 14.8 %collective-permute-start.26 = (bf16[128,1024]{1,0:T(8,128)(2,1)S(1)}, bf16[128,1024]{1,0:T(8,128)(2,1)S(1)}, u32[]{:S(2)}, u32[]{:S(2)}) collective-permute-start(bf16[128,1024]{1,0:T(8,128)(2,1)S(1)} %get-tuple-element.167.refs_0_), channel_id=1, source_target_pairs={{0,2},{1,3},{2,0},{3,1},{4,6},{5,7},{6,4},{7,5},{8,10},{9,11},{10,... | collective-permute-start | bytes 786440 | tf_op jit(solution)/shard_map/ppermute | solution.py:75
  119.1 16.0 %collective-permute-start.30 = (bf16[176,1024]{1,0:T(8,128)(2,1)S(1)}, bf16[176,1024]{1,0:T(8,128)(2,1)S(1)}, u32[]{:S(2)}, u32[]{:S(2)}) collective-permute-start(bf16[176,1024]{1,0:T(8,128)(2,1)S(1)} %bitcast.30), channel_id=1, source_target_pairs={{0,12},{4,8},{8,4},{12,0},{1,13},{5,9},{9,5},{13,1},{2,14},{6,10},... | collective-permute-start | bytes 1081352 | tf_op jit(solution)/shard_map/ppermute | solution.py:79
  121.3 20.9 %collective-permute-start.29 = (bf16[128,1408]{1,0:T(8,128)(2,1)S(1)}, bf16[128,1408]{1,0:T(8,128)(2,1)S(1)}, u32[]{:S(2)}, u32[]{:S(2)}) collective-permute-start(bf16[128,1408]{1,0:T(8,128)(2,1)S(1)} %collective-permute-done.20.refs_9_), channel_id=1, source_target_pairs={{0,4},{4,0},{8,12},{12,8},{1,5},{5,1},{9,13},{13,9},{2,6},{6,2},{1... | collective-permute-start | bytes 1081352 | tf_op jit(solution)/shard_map/ppermute | solution.py:79
  121.3 13.8 %collective-permute-start.32 = (bf16[128,1024]{1,0:T(8,128)(2,1)S(1)}, bf16[128,1024]{1,0:T(8,128)(2,1)S(1)}, u32[]{:S(2)}, u32[]{:S(2)}) collective-permute-start(bf16[128,1024]{1,0:T(8,128)(2,1)S(1)} %bitcast.33), channel_id=1, source_target_pairs={{0,2},{1,3},{2,0},{3,1},{4,6},{5,7},{6,4},{7,5},{8,10},{9,11},{10,... | collective-permute-start | bytes 786440 | tf_op jit(solution)/shard_map/ppermute | solution.py:75
  133.1 9.1 %collective-permute-start.28 = (bf16[128,1024]{1,0:T(8,128)(2,1)S(1)}, bf16[128,1024]{1,0:T(8,128)(2,1)S(1)}, u32[]{:S(2)}, u32[]{:S(2)}) collective-permute-start(bf16[128,1024]{1,0:T(8,128)(2,1)S(1)} %collective-permute-done.26.refs_2_), channel_id=1, source_target_pairs={{0,1},{1,0},{2,3},{3,2},{4,5},{5,4},{6,7},{7,6},{8,9},{9,8},{10,11... | collective-permute-start | bytes 786440 | tf_op jit(solution)/shard_map/ppermute | solution.py:75
  133.1 11.9 %collective-permute-start.25 = (bf16[128,1024]{1,0:T(8,128)(2,1)S(1)}, bf16[128,1024]{1,0:T(8,128)(2,1)S(1)}, u32[]{:S(2)}, u32[]{:S(2)}) collective-permute-start(bf16[128,1024]{1,0:T(8,128)(2,1)S(1)} %get-tuple-element.167.refs_0_), channel_id=1, source_target_pairs={{0,1},{1,0},{2,3},{3,2},{4,5},{5,4},{6,7},{7,6},{8,9},{9,8},{10,11... | collective-permute-start | bytes 786440 | tf_op jit(solution)/shard_map/ppermute | solution.py:75
  135.1 12.7 %collective-permute-start.31 = (bf16[128,1024]{1,0:T(8,128)(2,1)S(1)}, bf16[128,1024]{1,0:T(8,128)(2,1)S(1)}, u32[]{:S(2)}, u32[]{:S(2)}) collective-permute-start(bf16[128,1024]{1,0:T(8,128)(2,1)S(1)} %bitcast.34), channel_id=1, source_target_pairs={{0,1},{1,0},{2,3},{3,2},{4,5},{5,4},{6,7},{7,6},{8,9},{9,8},{10,11... | collective-permute-start | bytes 786440 | tf_op jit(solution)/shard_map/ppermute | solution.py:75
  135.1 15.4 %collective-permute-start.33 = (bf16[128,1024]{1,0:T(8,128)(2,1)S(1)}, bf16[128,1024]{1,0:T(8,128)(2,1)S(1)}, u32[]{:S(2)}, u32[]{:S(2)}) collective-permute-start(bf16[128,1024]{1,0:T(8,128)(2,1)S(1)} %collective-permute-done.32.refs_2_), channel_id=1, source_target_pairs={{0,1},{1,0},{2,3},{3,2},{4,5},{5,4},{6,7},{7,6},{8,9},{9,8},{10,11... | collective-permute-start | bytes 786440 | tf_op jit(solution)/shard_map/ppermute | solution.py:75
  142.1 10.8 %collective-permute-start.34 = (bf16[176,1024]{1,0:T(8,128)(2,1)S(1)}, bf16[176,1024]{1,0:T(8,128)(2,1)S(1)}, u32[]{:S(2)}, u32[]{:S(2)}) collective-permute-start(bf16[176,1024]{1,0:T(8,128)(2,1)S(1)} %collective-permute-done.30.refs_7_), channel_id=1, source_target_pairs={{0,4},{4,0},{8,12},{12,8},{1,5},{5,1},{9,13},{13,9},{2,6},{6,2},{1... | collective-permute-start | bytes 1081352 | tf_op jit(solution)/shard_map/ppermute | solution.py:79
  152.9 10.1 %collective-permute-start.35 = (bf16[352,1024]{1,0:T(8,128)(2,1)S(1)}, bf16[352,1024]{1,0:T(8,128)(2,1)S(1)}, u32[]{:S(2)}, u32[]{:S(2)}) collective-permute-start(bf16[352,1024]{1,0:T(8,128)(2,1)S(1)} %get-tuple-element.184.a_ref), channel_id=1, source_target_pairs={{0,4},{12,8},{1,5},{13,9},{2,6},{14,10},{3,7},{15,11},{16,20},{28,... | collective-permute-start | bytes 2162696 | tf_op jit(solution)/shard_map/ppermute | solution.py:83
  157.8 7.7 %collective-permute-start.36 = (bf16[128,1024]{1,0:T(8,128)(2,1)S(1)}, bf16[128,1024]{1,0:T(8,128)(2,1)S(1)}, u32[]{:S(2)}, u32[]{:S(2)}) collective-permute-start(bf16[128,1024]{1,0:T(8,128)(2,1)S(1)} %get-tuple-element.186), channel_id=1, source_target_pairs={{0,1},{1,0},{2,3},{3,2},{4,5},{5,4},{6,7},{7,6},{8,9},{9,8},{10,11... | collective-permute-start | bytes 786440 | tf_op jit(solution)/shard_map/ppermute | solution.py:75
  158.2 8.0 %collective-permute-start.37 = (bf16[128,1024]{1,0:T(8,128)(2,1)S(1)}, bf16[128,1024]{1,0:T(8,128)(2,1)S(1)}, u32[]{:S(2)}, u32[]{:S(2)}) collective-permute-start(bf16[128,1024]{1,0:T(8,128)(2,1)S(1)} %get-tuple-element.187), channel_id=1, source_target_pairs={{0,2},{1,3},{2,0},{3,1},{4,6},{5,7},{6,4},{7,5},{8,10},{9,11},{10,... | collective-permute-start | bytes 786440 | tf_op jit(solution)/shard_map/ppermute | solution.py:75
  159.2 11.0 %collective-permute-start.38 = (bf16[128,1024]{1,0:T(8,128)(2,1)S(1)}, bf16[128,1024]{1,0:T(8,128)(2,1)S(1)}, u32[]{:S(2)}, u32[]{:S(2)}) collective-permute-start(bf16[128,1024]{1,0:T(8,128)(2,1)S(1)} %get-tuple-element.188), channel_id=1, source_target_pairs={{0,3},{1,2},{2,1},{3,0},{4,7},{5,6},{6,5},{7,4},{8,11},{9,10},{10,... | collective-permute-start | bytes 786440 | tf_op jit(solution)/shard_map/ppermute | solution.py:75
  163.1 18.4 %collective-permute-start.40 = (bf16[352,1024]{1,0:T(8,128)(2,1)S(1)}, bf16[352,1024]{1,0:T(8,128)(2,1)S(1)}, u32[]{:S(2)}, u32[]{:S(2)}) collective-permute-start(bf16[352,1024]{1,0:T(8,128)(2,1)S(1)} %shard_map.192), channel_id=1, source_target_pairs={{4,8},{8,4},{5,9},{9,5},{6,10},{10,6},{7,11},{11,7},{20,24},{24,20... | collective-permute-start | bytes 2162696 | tf_op jit(solution)/shard_map/ppermute | solution.py:87
  171.2 10.3 %collective-permute-start.39 = (bf16[128,1024]{1,0:T(8,128)(2,1)S(1)}, bf16[128,1024]{1,0:T(8,128)(2,1)S(1)}, u32[]{:S(2)}, u32[]{:S(2)}) collective-permute-start(bf16[128,1024]{1,0:T(8,128)(2,1)S(1)} %get-tuple-element.189.refs_0_.refs_6_), channel_id=1, source_target_pairs={{0,3},{1,2},{2,1},{3,0},{4,7},{5,6},{6,5},{7,4},{8,11},{9,10},{10,... | collective-permute-start | bytes 786440 | tf_op jit(solution)/shard_map/ppermute | solution.py:75
  176.0 22.8 %collective-permute-start.47 = (bf16[512,1408]{1,0:T(8,128)(2,1)S(1)}, bf16[512,1408]{1,0:T(8,128)(2,1)S(1)}, u32[]{:S(2)}, u32[]{:S(2)}) collective-permute-start(bf16[512,1408]{1,0:T(8,128)(2,1)S(1)} %get-tuple-element.207.a_ref), channel_id=1, source_target_pairs={{0,4},{12,8},{1,5},{13,9},{2,6},{14,10},{3,7},{15,11},{16,20},{28,... | collective-permute-start | bytes 4325384 | tf_op jit(solution)/shard_map/ppermute | solution.py:83
  177.4 8.2 %collective-permute-start.45 = (bf16[128,1024]{1,0:T(8,128)(2,1)S(1)}, bf16[128,1024]{1,0:T(8,128)(2,1)S(1)}, u32[]{:S(2)}, u32[]{:S(2)}) collective-permute-start(bf16[128,1024]{1,0:T(8,128)(2,1)S(1)} %get-tuple-element.189.refs_0_.refs_6_), channel_id=1, source_target_pairs={{0,2},{1,3},{2,0},{3,1},{4,6},{5,7},{6,4},{7,5},{8,10},{9,11},{10,... | collective-permute-start | bytes 786440 | tf_op jit(solution)/shard_map/ppermute | solution.py:75
  178.9 7.8 %collective-permute-start.44 = (bf16[128,1024]{1,0:T(8,128)(2,1)S(1)}, bf16[128,1024]{1,0:T(8,128)(2,1)S(1)}, u32[]{:S(2)}, u32[]{:S(2)}) collective-permute-start(bf16[128,1024]{1,0:T(8,128)(2,1)S(1)} %get-tuple-element.189.refs_0_.refs_6_), channel_id=1, source_target_pairs={{0,1},{1,0},{2,3},{3,2},{4,5},{5,4},{6,7},{7,6},{8,9},{9,8},{10,11... | collective-permute-start | bytes 786440 | tf_op jit(solution)/shard_map/ppermute | solution.py:75
  184.8 9.2 %collective-permute-start.42 = (bf16[128,1024]{1,0:T(8,128)(2,1)S(1)}, bf16[128,1024]{1,0:T(8,128)(2,1)S(1)}, u32[]{:S(2)}, u32[]{:S(2)}) collective-permute-start(bf16[128,1024]{1,0:T(8,128)(2,1)S(1)} %get-tuple-element.196), channel_id=1, source_target_pairs={{0,2},{1,3},{2,0},{3,1},{4,6},{5,7},{6,4},{7,5},{8,10},{9,11},{10,... | collective-permute-start | bytes 786440 | tf_op jit(solution)/shard_map/ppermute | solution.py:75
  185.6 8.4 %collective-permute-start.43 = (bf16[128,1024]{1,0:T(8,128)(2,1)S(1)}, bf16[128,1024]{1,0:T(8,128)(2,1)S(1)}, u32[]{:S(2)}, u32[]{:S(2)}) collective-permute-start(bf16[128,1024]{1,0:T(8,128)(2,1)S(1)} %get-tuple-element.197), channel_id=1, source_target_pairs={{0,3},{1,2},{2,1},{3,0},{4,7},{5,6},{6,5},{7,4},{8,11},{9,10},{10,... | collective-permute-start | bytes 786440 | tf_op jit(solution)/shard_map/ppermute | solution.py:75
  195.2 15.8 %collective-permute-start.48 = (bf16[128,1024]{1,0:T(8,128)(2,1)S(1)}, bf16[128,1024]{1,0:T(8,128)(2,1)S(1)}, u32[]{:S(2)}, u32[]{:S(2)}) collective-permute-start(bf16[128,1024]{1,0:T(8,128)(2,1)S(1)} %get-tuple-element.209), channel_id=1, source_target_pairs={{0,1},{1,0},{2,3},{3,2},{4,5},{5,4},{6,7},{7,6},{8,9},{9,8},{10,11... | collective-permute-start | bytes 786440 | tf_op jit(solution)/shard_map/ppermute | solution.py:75
  195.5 15.5 %collective-permute-start.49 = (bf16[128,1024]{1,0:T(8,128)(2,1)S(1)}, bf16[128,1024]{1,0:T(8,128)(2,1)S(1)}, u32[]{:S(2)}, u32[]{:S(2)}) collective-permute-start(bf16[128,1024]{1,0:T(8,128)(2,1)S(1)} %get-tuple-element.210), channel_id=1, source_target_pairs={{0,2},{1,3},{2,0},{3,1},{4,6},{5,7},{6,4},{7,5},{8,10},{9,11},{10,... | collective-permute-start | bytes 786440 | tf_op jit(solution)/shard_map/ppermute | solution.py:75
  196.7 14.3 %collective-permute-start.50 = (bf16[128,1024]{1,0:T(8,128)(2,1)S(1)}, bf16[128,1024]{1,0:T(8,128)(2,1)S(1)}, u32[]{:S(2)}, u32[]{:S(2)}) collective-permute-start(bf16[128,1024]{1,0:T(8,128)(2,1)S(1)} %get-tuple-element.211), channel_id=1, source_target_pairs={{0,3},{1,2},{2,1},{3,0},{4,7},{5,6},{6,5},{7,4},{8,11},{9,10},{10,... | collective-permute-start | bytes 786440 | tf_op jit(solution)/shard_map/ppermute | solution.py:75
  200.2 37.5 %collective-permute-start.56 = (bf16[512,1408]{1,0:T(8,128)(2,1)}, bf16[512,1408]{1,0:T(8,128)(2,1)S(1)}, u32[]{:S(2)}, u32[]{:S(2)}) collective-permute-start(bf16[512,1408]{1,0:T(8,128)(2,1)} %shard_map.202), channel_id=1, source_target_pairs={{4,8},{8,4},{5,9},{9,5},{6,10},{10,6},{7,11},{11,7},{20,24},{24,20... | collective-permute-start | bytes 4325384 | tf_op jit(solution)/shard_map/ppermute | solution.py:87
  205.5 28.4 %collective-permute-start.54 = (bf16[512,1024]{1,0:T(8,128)(2,1)}, bf16[512,1024]{1,0:T(8,128)(2,1)}, u32[]{:S(2)}, u32[]{:S(2)}) collective-permute-start(bf16[512,1024]{1,0:T(8,128)(2,1)} %get-tuple-element.220.a_ref), channel_id=1, source_target_pairs={{0,4},{12,8},{1,5},{13,9},{2,6},{14,10},{3,7},{15,11},{16,20},{28,... | collective-permute-start | bytes 3145736 | tf_op jit(solution)/shard_map/ppermute | solution.py:83
  216.9 18.2 %collective-permute-start.53 = (bf16[144,512]{1,0:T(8,128)(2,1)S(1)}, bf16[144,512]{1,0:T(8,128)(2,1)S(1)}, u32[]{:S(2)}, u32[]{:S(2)}) collective-permute-start(bf16[144,512]{1,0:T(8,128)(2,1)S(1)} %shard_map.199.refs_0_), channel_id=1, source_target_pairs={{0,2},{1,3},{2,0},{3,1},{4,6},{5,7},{6,4},{7,5},{8,10},{9,11},{10,... | collective-permute-start | bytes 442376 | tf_op jit(solution)/shard_map/ppermute | solution.py:75
  217.7 25.8 %collective-permute-start.64 = (bf16[176,1024]{1,0:T(8,128)(2,1)S(1)}, bf16[176,1024]{1,0:T(8,128)(2,1)S(1)}, u32[]{:S(2)}, u32[]{:S(2)}) collective-permute-start(bf16[176,1024]{1,0:T(8,128)(2,1)S(1)} %shard_map.207), channel_id=1, source_target_pairs={{0,4},{4,0},{8,12},{12,8},{1,5},{5,1},{9,13},{13,9},{2,6},{6,2},{1... | collective-permute-start | bytes 1081352 | tf_op jit(solution)/shard_map/ppermute | solution.py:79
  219.1 18.6 %collective-permute-start.55 = (bf16[144,512]{1,0:T(8,128)(2,1)S(1)}, bf16[144,512]{1,0:T(8,128)(2,1)S(1)}, u32[]{:S(2)}, u32[]{:S(2)}) collective-permute-start(bf16[144,512]{1,0:T(8,128)(2,1)S(1)} %shard_map.199.refs_0_), channel_id=1, source_target_pairs={{0,3},{1,2},{2,1},{3,0},{4,7},{5,6},{6,5},{7,4},{8,11},{9,10},{10,... | collective-permute-start | bytes 442376 | tf_op jit(solution)/shard_map/ppermute | solution.py:75
  233.8 7.8 %collective-permute-start.52 = (bf16[144,512]{1,0:T(8,128)(2,1)S(1)}, bf16[144,512]{1,0:T(8,128)(2,1)S(1)}, u32[]{:S(2)}, u32[]{:S(2)}) collective-permute-start(bf16[144,512]{1,0:T(8,128)(2,1)S(1)} %shard_map.199.refs_0_), channel_id=1, source_target_pairs={{0,1},{1,0},{2,3},{3,2},{4,5},{5,4},{6,7},{7,6},{8,9},{9,8},{10,11... | collective-permute-start | bytes 442376 | tf_op jit(solution)/shard_map/ppermute | solution.py:75
  236.9 20.2 %collective-permute-start.62 = (bf16[512,1024]{1,0:T(8,128)(2,1)S(1)}, bf16[512,1024]{1,0:T(8,128)(2,1)S(1)}, u32[]{:S(2)}, u32[]{:S(2)}) collective-permute-start(bf16[512,1024]{1,0:T(8,128)(2,1)S(1)} %shard_map.206), channel_id=1, source_target_pairs={{4,8},{8,4},{5,9},{9,5},{6,10},{10,6},{7,11},{11,7},{20,24},{24,20... | collective-permute-start | bytes 3145736 | tf_op jit(solution)/shard_map/ppermute | solution.py:87
  237.9 15.6 %collective-permute-start.58 = (bf16[256,1408]{1,0:T(8,128)(2,1)S(1)}, bf16[256,1408]{1,0:T(8,128)(2,1)S(1)}, u32[]{:S(2)}, u32[]{:S(2)}) collective-permute-start(bf16[256,1408]{1,0:T(8,128)(2,1)S(1)} %shard_map.203), channel_id=1, source_target_pairs={{0,4},{4,0},{8,12},{12,8},{1,5},{5,1},{9,13},{13,9},{2,6},{6,2},{1... | collective-permute-start | bytes 2162696 | tf_op jit(solution)/shard_map/ppermute | solution.py:79
  247.1 17.9 %collective-permute-start.65 = (bf16[1056,256]{1,0:T(8,128)(2,1)S(1)}, bf16[1056,256]{1,0:T(8,128)(2,1)S(1)}, u32[]{:S(2)}, u32[]{:S(2)}) collective-permute-start(bf16[1056,256]{1,0:T(8,128)(2,1)S(1)} %get-tuple-element.237.a_ref), channel_id=1, source_target_pairs={{0,4},{12,8},{1,5},{13,9},{2,6},{14,10},{3,7},{15,11},{16,20},{28,... | collective-permute-start | bytes 1622024 | tf_op jit(solution)/shard_map/ppermute | solution.py:83
  257.3 17.5 %collective-permute-start.67 = (bf16[256,1024]{1,0:T(8,128)(2,1)S(1)}, bf16[256,1024]{1,0:T(8,128)(2,1)S(1)}, u32[]{:S(2)}, u32[]{:S(2)}) collective-permute-start(bf16[256,1024]{1,0:T(8,128)(2,1)S(1)} %shard_map.212), channel_id=1, source_target_pairs={{0,4},{4,0},{8,12},{12,8},{1,5},{5,1},{9,13},{13,9},{2,6},{6,2},{1... | collective-permute-start | bytes 1572872 | tf_op jit(solution)/shard_map/ppermute | solution.py:79
  265.2 9.6 %collective-permute-start.66 = (bf16[1056,256]{1,0:T(8,128)(2,1)S(1)}, bf16[1056,256]{1,0:T(8,128)(2,1)S(1)}, u32[]{:S(2)}, u32[]{:S(2)}) collective-permute-start(bf16[1056,256]{1,0:T(8,128)(2,1)S(1)} %shard_map.210), channel_id=1, source_target_pairs={{4,8},{8,4},{5,9},{9,5},{6,10},{10,6},{7,11},{11,7},{20,24},{24,20... | collective-permute-start | bytes 1622024 | tf_op jit(solution)/shard_map/ppermute | solution.py:87
  267.0 7.8 %collective-permute-start.68 = (bf16[64,1408]{1,0:T(8,128)(2,1)S(1)}, bf16[64,1408]{1,0:T(8,128)(2,1)S(1)}, u32[]{:S(2)}, u32[]{:S(2)}) collective-permute-start(bf16[64,1408]{1,0:T(8,128)(2,1)S(1)} %get-tuple-element.247), channel_id=1, source_target_pairs={{0,1},{1,0},{2,3},{3,2},{4,5},{5,4},{6,7},{7,6},{8,9},{9,8},{10,11... | collective-permute-start | bytes 540680 | tf_op jit(solution)/shard_map/ppermute | solution.py:75
  280.0 8.5 %collective-permute-start.72 = (bf16[64,768]{1,0:T(8,128)(2,1)S(1)}, bf16[64,768]{1,0:T(8,128)(2,1)S(1)}, u32[]{:S(2)}, u32[]{:S(2)}) collective-permute-start(bf16[64,768]{1,0:T(8,128)(2,1)S(1)} %get-tuple-element.256), channel_id=1, source_target_pairs={{0,1},{1,0},{2,3},{3,2},{4,5},{5,4},{6,7},{7,6},{8,9},{9,8},{10,11... | collective-permute-start | bytes 294920 | tf_op jit(solution)/shard_map/ppermute | solution.py:75
  280.9 7.7 %collective-permute-start.73 = (bf16[64,768]{1,0:T(8,128)(2,1)S(1)}, bf16[64,768]{1,0:T(8,128)(2,1)S(1)}, u32[]{:S(2)}, u32[]{:S(2)}) collective-permute-start(bf16[64,768]{1,0:T(8,128)(2,1)S(1)} %get-tuple-element.257), channel_id=1, source_target_pairs={{0,2},{1,3},{2,0},{3,1},{4,6},{5,7},{6,4},{7,5},{8,10},{9,11},{10,... | collective-permute-start | bytes 294920 | tf_op jit(solution)/shard_map/ppermute | solution.py:75
  283.6 9.4 %collective-permute-start.71 = (bf16[528,256]{1,0:T(8,128)(2,1)S(1)}, bf16[528,256]{1,0:T(8,128)(2,1)S(1)}, u32[]{:S(2)}, u32[]{:S(2)}) collective-permute-start(bf16[528,256]{1,0:T(8,128)(2,1)S(1)} %shard_map.214), channel_id=1, source_target_pairs={{0,4},{4,0},{8,12},{12,8},{1,5},{5,1},{9,13},{13,9},{2,6},{6,2},{1... | collective-permute-start | bytes 811016 | tf_op jit(solution)/shard_map/ppermute | solution.py:79
  (47 other events, 275.3 us)
